TPU v7x, 32 devices: a whole 2x2x4 slice. The times are simulated.
32 devices in a mesh: samp: 4 (over y, x), gx: 2 (over core), gy: 4 (over z).
Axes of the slice: x: 2, y: 2, z: 4, core: 2. Of those that a mesh axis runs over, the one named last changes fastest.
Arguments:
- load: float32 [4, 2, 256, 2048], P('samp', None, 'gx', 'gy'), parts along dimension 0, may hold values from -6 to 6
- material: int32 [4, 32, 256], P('samp', 'gx', 'gy'), parts along dimension 0, may hold values from 0 to 7
- lame_table: float32 [2, 8], replicated, may hold values from 0.3 to 6
Outputs:
- solution: float32 [4, 2, 256, 2048], P('samp', None, 'gx', 'gy'), parts along dimension 0
- residual: float32 [4, 2, 256, 2048], P('samp', None, 'gx', 'gy'), parts along dimension 0
There are 4 independent parts, one for each index of `samp`. A program takes and returns all parts, laid end to end along the dimension named above; an argument that names none is the same for every part. Nothing has to cross between parts.
All inputs are finite; a program needn't handle non-finite values.
Results may differ from a plain program's by a relative error of at most 0.0003.
Values sent between devices are 32-bit elements; how exact they have to be, the bound alone decides.
No kernel may reach another device: no remote copies, remote signals or barrier semaphores. Data moves between devices by JAX's collectives and lax.ppermute only.
A program may use at most 64 MiB of HBM per device.

v0:
```python
import jax
import jax.numpy as jnp
from jax import lax
from jax.sharding import PartitionSpec as P

TILE = 8
CLASSES = 8
ITERS = 4


def shifted(block, axis, distance):
    devices = range(lax.axis_size(axis))
    route = [(i - distance, i) for i in devices if i - distance in devices]
    return lax.ppermute(block, axis, route)


def padded_2(array, sides, width):
    for axis, dim in sides:
        devices, length = (lax.axis_size(axis), array.shape[dim])
        up = [(i, (i + 1) % devices) for i in range(devices - 1)]
        down = [(j, i) for i, j in up]
        last = lax.slice_in_dim(array, length - width, length, axis=dim)
        leading = lax.slice_in_dim(array, 0, width, axis=dim)
        before = lax.ppermute(last, axis, up)
        after = lax.ppermute(leading, axis, down)
        array = jnp.concatenate([before, array, after], axis=dim)
    return array


def cell_moduli(material, lame_table):
    classes = jnp.arange(CLASSES, dtype=jnp.int32)
    match = (material[..., None] == classes).astype(jnp.float32)
    lam = jnp.sum(match * lame_table[0], axis=-1)
    mu = jnp.sum(match * lame_table[1], axis=-1)

    def expand(tiles):
        count, rows, cols = tiles.shape
        wide = jnp.broadcast_to(tiles[:, :, None, :, None], (count, rows, TILE, cols, TILE))
        return wide.reshape(count, rows * TILE, cols * TILE)

    return (expand(lam), expand(mu))


def cell_terms(nodes, lam, mu):
    low_low = nodes[..., :-1, :-1]
    high_low = nodes[..., 1:, :-1]
    low_high = nodes[..., :-1, 1:]
    high_high = nodes[..., 1:, 1:]
    along_x = 0.5 * (high_low + high_high - (low_low + low_high))
    along_y = 0.5 * (low_high + high_high - (low_low + high_low))
    strain_xx = along_x[:, 0]
    strain_yy = along_y[:, 1]
    shear = along_y[:, 0] + along_x[:, 1]
    stiff = lam + 2.0 * mu
    stress_xx = stiff * strain_xx + lam * strain_yy
    stress_yy = lam * strain_xx + stiff * strain_yy
    stress_xy = mu * shear
    plus = 0.5 * jnp.stack([stress_xx + stress_xy, stress_xy + stress_yy], axis=1)
    minus = 0.5 * jnp.stack([stress_xx - stress_xy, stress_xy - stress_yy], axis=1)
    return (plus, minus)


def on_device(load, material, lame_table):
    rows = load.shape[2]
    cols = load.shape[3]
    lam, mu = cell_moduli(material, lame_table)
    moduli = jnp.stack([lam, mu], axis=1)
    row_before = shifted(moduli[:, :, rows - 1 :, :], "gx", 1)
    widened = jnp.concatenate([row_before, moduli], axis=2)
    col_before = shifted(widened[:, :, :, cols - 1 :], "gy", 1)
    widened = jnp.concatenate([col_before, widened], axis=3)
    lam_rim = widened[:, 0]
    mu_rim = widened[:, 1]

    def operate(field):
        padded = padded_2(field, (("gx", 2), ("gy", 3)), 1)
        plus, minus = cell_terms(padded, lam_rim, mu_rim)
        forces = plus[..., :-1, :-1] - plus[..., 1:, 1:] + minus[..., :-1, 1:] - minus[..., 1:, :-1]
        return 0.05 * field + forces

    solution = jnp.zeros_like(load)
    residual = load
    w_vec = operate(residual)
    z_vec = jnp.zeros_like(load)
    q_vec = jnp.zeros_like(load)
    p_vec = jnp.zeros_like(load)
    gamma_prev = jnp.ones((load.shape[0],), jnp.float32)
    alpha_prev = jnp.ones((load.shape[0],), jnp.float32)
    for step in range(ITERS):
        local_gamma = jnp.sum(residual * residual, axis=(1, 2, 3))
        local_delta = jnp.sum(w_vec * residual, axis=(1, 2, 3))
        gamma, delta = lax.psum((local_gamma, local_delta), ("gx", "gy"))
        if step + 1 < ITERS:
            n_vec = operate(w_vec)
        if step == 0:
            beta = jnp.zeros_like(gamma)
            alpha = gamma / delta
        else:
            beta = gamma / gamma_prev
            alpha = gamma / (delta - beta * gamma / alpha_prev)
        beta_b = beta[:, None, None, None]
        alpha_b = alpha[:, None, None, None]
        if step + 1 < ITERS:
            z_vec = n_vec + beta_b * z_vec
        q_vec = w_vec + beta_b * q_vec
        p_vec = residual + beta_b * p_vec
        solution = solution + alpha_b * p_vec
        residual = residual - alpha_b * q_vec
        if step + 1 < ITERS:
            w_vec = w_vec - alpha_b * z_vec
        gamma_prev = gamma
        alpha_prev = alpha
    return (solution, residual)


def solution(mesh):
    return jax.shard_map(
        on_device,
        mesh=mesh,
        in_specs=(P("samp", None, "gx", "gy"), P("samp", "gx", "gy"), P()),
        out_specs=(P("samp", None, "gx", "gy"), P("samp", None, "gx", "gy")),
        check_vma=False,
    )
```

profile of v0, /device:TPU:0, one launch (start us, length us, event | category | flops | bytes accessed | tf_op | source)
XLA Modules:
  0.0 158.6 jit_solution(6771983282719764883)
XLA Ops:
  0.6 0.8 slice_bitcast_fusion.1
  1.4 0.8 select_reduce_fusion
  2.2 2.5 %broadcast_in_dim.10 = f32[16,8,64,8]{3,2,1,0:T(8,128)} broadcast(f32[16,64]{1,0:T(8,128)S(1)} %get-tuple-element.10), dimensions={0,2} | broadcast | bytes 266240 | tf_op jit(solution)/shard_map/broadcast_in_dim | solution.py:38
  4.7 4.0 %broadcast_in_dim.11 = f32[1,1,128,512]{3,2,1,0:T(8,128)S(1)} reshape(f32[16,8,64,8]{3,2,1,0:T(8,128)} %broadcast_in_dim.10) | data formatting | bytes 524288 | tf_op jit(solution)/shard_map/broadcast_in_dim | solution.py:38
  8.7 2.5 %broadcast_in_dim.8 = f32[16,8,64,8]{3,2,1,0:T(8,128)} broadcast(f32[16,64]{1,0:T(8,128)S(1)} %get-tuple-element.11), dimensions={0,2} | broadcast | bytes 266240 | tf_op jit(solution)/shard_map/broadcast_in_dim | solution.py:38
  11.3 4.0 %broadcast_in_dim.9 = f32[1,1,128,512]{3,2,1,0:T(8,128)S(1)} reshape(f32[16,8,64,8]{3,2,1,0:T(8,128)} %broadcast_in_dim.8) | data formatting | bytes 524288 | tf_op jit(solution)/shard_map/broadcast_in_dim | solution.py:38
  15.3 2.4 %collective-permute-start = (f32[1,2,1,512]{3,2,1,0:T(1,128)S(1)}, f32[1,2,1,512]{3,2,1,0:T(1,128)S(1)}, u32[]{:S(2)}, u32[]{:S(2)}) collective-permute-start(f32[1,2,1,512]{3,2,1,0:T(1,128)S(1)} %slice.296), channel_id=1, source_target_pairs={{0,4},{1,5},{2,6},{3,7},{8,12},{9,13},{10,14},{11,15},{16,20},{17,... | collective-permute-start | bytes 12296 | tf_op jit(solution)/shard_map/ppermute | solution.py:14
  17.8 1.3 collective-permute-start.2
  19.1 1.3 collective-permute-start.3
  20.5 4.3 %collective-permute-start.1 = (f32[1,2,129,1]{3,2,1,0:T(8,128)S(1)}, f32[1,2,129,1]{3,2,1,0:T(8,128)S(1)}, u32[]{:S(2)}, u32[]{:S(2)}) collective-permute-start(f32[1,2,129,1]{3,2,1,0:T(8,128)S(1)} %pad_maximum_fusion.16), channel_id=1, source_target_pairs={{0,1},{1,2},{2,3},{4,5},{5,6},{6,7},{8,9},{9,10},{10,11},{12,13},{... | collective-permute-start | bytes 3104 | tf_op jit(solution)/shard_map/ppermute | solution.py:14
  24.9 3.5 %collective-permute-start.4 = (f32[1,2,130,1]{3,2,1,0:T(8,128)S(1)}, f32[1,2,130,1]{3,2,1,0:T(8,128)S(1)}, u32[]{:S(2)}, u32[]{:S(2)}) collective-permute-start(f32[1,2,130,1]{3,2,1,0:T(8,128)S(1)} %get-tuple-element.74), channel_id=1, source_target_pairs={{0,1},{1,2},{2,3},{4,5},{5,6},{6,7},{8,9},{9,10},{10,11},{12,13},{... | collective-permute-start | bytes 3128 | tf_op jit(solution)/shard_map/ppermute | solution.py:24
  28.4 1.3 collective-permute-start.5
  30.0 2.3 %collective-permute-done.4 = f32[1,2,130,1]{3,2,1,0:T(8,128)S(1)} collective-permute-done((f32[1,2,130,1]{3,2,1,0:T(8,128)S(1)}, f32[1,2,130,1]{3,2,1,0:T(8,128)S(1)}, u32[]{:S(2)}, u32[]{:S(2)}) %collective-permute-start.4) | collective-permute-done | bytes 1072 | tf_op jit(solution)/shard_map/ppermute | solution.py:24
  32.3 4.1 %collective-permute-done.5 = f32[1,2,130,1]{3,2,1,0:T(8,128)S(1)} collective-permute-done((f32[1,2,130,1]{3,2,1,0:T(8,128)S(1)}, f32[1,2,130,1]{3,2,1,0:T(8,128)S(1)}, u32[]{:S(2)}, u32[]{:S(2)}) %collective-permute-start.5) | collective-permute-done | bytes 1072 | tf_op jit(solution)/shard_map/ppermute | solution.py:25
  36.5 0.3 maximum_maximum_fusion.1
  36.8 0.3 subtract_multiply_fusion.7
  37.5 1.0 multiply_reduce_fusion.6
  38.6 1.6 %collective-permute-start.6 = (f32[1,2,1,512]{3,2,1,0:T(1,128)S(1)}, f32[1,2,1,512]{3,2,1,0:T(1,128)S(1)}, u32[]{:S(2)}, u32[]{:S(2)}) collective-permute-start(f32[1,2,1,512]{3,2,1,0:T(1,128)S(1)} %get-tuple-element.80), channel_id=1, source_target_pairs={{0,4},{1,5},{2,6},{3,7},{8,12},{9,13},{10,14},{11,15},{16,20},{17,... | collective-permute-start | bytes 12296 | tf_op jit(solution)/shard_map/ppermute | solution.py:24
  40.2 1.3 collective-permute-start.7
  41.5 1.8 %collective-permute-done.7 = f32[1,2,1,512]{3,2,1,0:T(1,128)S(1)} collective-permute-done((f32[1,2,1,512]{3,2,1,0:T(1,128)S(1)}, f32[1,2,1,512]{3,2,1,0:T(1,128)S(1)}, u32[]{:S(2)}, u32[]{:S(2)}) %collective-permute-start.7) | collective-permute-done | bytes 4128 | tf_op jit(solution)/shard_map/ppermute | solution.py:25
  43.4 3.5 %collective-permute-start.8 = (f32[1,2,130,1]{3,2,1,0:T(8,128)S(1)}, f32[1,2,130,1]{3,2,1,0:T(8,128)S(1)}, u32[]{:S(2)}, u32[]{:S(2)}) collective-permute-start(f32[1,2,130,1]{3,2,1,0:T(8,128)S(1)} %get-tuple-element.70), channel_id=1, source_target_pairs={{0,1},{1,2},{2,3},{4,5},{5,6},{6,7},{8,9},{9,10},{10,11},{12,13},{... | collective-permute-start | bytes 3128 | tf_op jit(solution)/shard_map/ppermute | solution.py:24
  46.9 1.3 collective-permute-start.9
  48.2 17.0 %all-reduce.3 = (f32[1]{0:T(128)}, f32[1]{0:T(128)}) all-reduce(f32[1]{0:T(128)} %bitcast, f32[1]{0:T(128)} %bitcast.4), channel_id=1, replica_groups=mesh['samp'=4,'gx'=2,'gy'=4] {'gx','gy'}, use_global_device_ids=true, to_apply=%region_1.0 | all-reduce | flops 2 | bytes 16 | tf_op jit(solution)/shard_map/psum | solution.py:92
  66.5 0.3 maximum_maximum_fusion.2
  66.8 0.3 subtract_multiply_fusion.5
  67.6 2.1 %multiply_reduce_fusion.4 = (f32[]{:T(128)}, f32[]{:T(128)}, f32[1,2,128,512]{3,2,1,0:T(8,128)S(1)}, f32[1,2,128,512]{3,2,1,0:T(8,128)}, f32[1,2,128,512]{3,2,1,0:T(8,128)}) fusion(f32[1,2,128,512]{3,2,1,0:T(8,128)S(1)} %get-tuple-element.43, f32[]{:T(128)} %bitcast.5, f32[1,2,129,513]{3,2,1,0:T(8,128)S(1)} %maximum_multiply_fusion.3, ...), kind=kLoop, calls=%fused_computation.56 | loop fusion | flops 1703934 | bytes 4718604 | tf_op jit(solution)/shard_map/reduce_sum | solution.py:91
  69.7 1.6 %collective-permute-start.10 = (f32[1,2,1,512]{3,2,1,0:T(1,128)S(1)}, f32[1,2,1,512]{3,2,1,0:T(1,128)S(1)}, u32[]{:S(2)}, u32[]{:S(2)}) collective-permute-start(f32[1,2,1,512]{3,2,1,0:T(1,128)S(1)} %get-tuple-element.78), channel_id=1, source_target_pairs={{0,4},{1,5},{2,6},{3,7},{8,12},{9,13},{10,14},{11,15},{16,20},{17,... | collective-permute-start | bytes 12296 | tf_op jit(solution)/shard_map/ppermute | solution.py:24
  71.4 1.3 collective-permute-start.11
  72.7 1.8 %collective-permute-done.11 = f32[1,2,1,512]{3,2,1,0:T(1,128)S(1)} collective-permute-done((f32[1,2,1,512]{3,2,1,0:T(1,128)S(1)}, f32[1,2,1,512]{3,2,1,0:T(1,128)S(1)}, u32[]{:S(2)}, u32[]{:S(2)}) %collective-permute-start.11) | collective-permute-done | bytes 4128 | tf_op jit(solution)/shard_map/ppermute | solution.py:25
  74.6 1.7 %collective-permute-start.12 = (f32[1,2,130,1]{3,2,1,0:T(8,128)S(1)}, f32[1,2,130,1]{3,2,1,0:T(8,128)S(1)}, u32[]{:S(2)}, u32[]{:S(2)}) collective-permute-start(f32[1,2,130,1]{3,2,1,0:T(8,128)S(1)} %get-tuple-element.66), channel_id=1, source_target_pairs={{0,1},{1,2},{2,3},{4,5},{5,6},{6,7},{8,9},{9,10},{10,11},{12,13},{... | collective-permute-start | bytes 3128 | tf_op jit(solution)/shard_map/ppermute | solution.py:24
  76.3 1.3 collective-permute-start.13
  77.6 17.1 %all-reduce.2 = (f32[1]{0:T(128)}, f32[1]{0:T(128)}) all-reduce(f32[1]{0:T(128)} %bitcast.6, f32[1]{0:T(128)} %bitcast.7), channel_id=1, replica_groups=mesh['samp'=4,'gx'=2,'gy'=4] {'gx','gy'}, use_global_device_ids=true, to_apply=%region_7.0 | all-reduce | flops 2 | bytes 16 | tf_op jit(solution)/shard_map/psum | solution.py:92
  99.4 0.3 maximum_maximum_fusion.3
  99.7 0.3 subtract_multiply_fusion.3
  100.5 0.7 copy-done.1
  101.3 2.2 %multiply_reduce_fusion.2 = (f32[]{:T(128)}, f32[]{:T(128)}, f32[1,2,128,512]{3,2,1,0:T(8,128)S(1)}, f32[1,2,128,512]{3,2,1,0:T(8,128)}, f32[1,2,128,512]{3,2,1,0:T(8,128)}) fusion(f32[1,2,128,512]{3,2,1,0:T(8,128)S(1)} %get-tuple-element.35, f32[]{:T(128)} %bitcast.8, f32[1,2,128,512]{3,2,1,0:T(8,128)S(1)} %copy-done.5, f32[]{:T(128)} %bitcast.9, ...), kind=kLoop, calls=%fused_computation.51 | loop fusion | flops 2228222 | bytes 5767184 | tf_op jit(solution)/shard_map/reduce_sum | solution.py:91
  103.5 2.3 %collective-permute-start.14 = (f32[1,2,1,512]{3,2,1,0:T(1,128)S(1)}, f32[1,2,1,512]{3,2,1,0:T(1,128)S(1)}, u32[]{:S(2)}, u32[]{:S(2)}) collective-permute-start(f32[1,2,1,512]{3,2,1,0:T(1,128)S(1)} %get-tuple-element.76), channel_id=1, source_target_pairs={{0,4},{1,5},{2,6},{3,7},{8,12},{9,13},{10,14},{11,15},{16,20},{17,... | collective-permute-start | bytes 12296 | tf_op jit(solution)/shard_map/ppermute | solution.py:24
  105.8 1.3 collective-permute-start.15
  107.1 1.8 %collective-permute-done.15 = f32[1,2,1,512]{3,2,1,0:T(1,128)S(1)} collective-permute-done((f32[1,2,1,512]{3,2,1,0:T(1,128)S(1)}, f32[1,2,1,512]{3,2,1,0:T(1,128)S(1)}, u32[]{:S(2)}, u32[]{:S(2)}) %collective-permute-start.15) | collective-permute-done | bytes 4128 | tf_op jit(solution)/shard_map/ppermute | solution.py:25
  108.9 0.8 pad_maximum_fusion.6
  109.7 1.3 collective-permute-start.16
  111.0 1.3 collective-permute-start.17
  112.3 16.9 %all-reduce.1 = (f32[1]{0:T(128)}, f32[1]{0:T(128)}) all-reduce(f32[1]{0:T(128)} %bitcast.10, f32[1]{0:T(128)} %bitcast.11), channel_id=1, replica_groups=mesh['samp'=4,'gx'=2,'gy'=4] {'gx','gy'}, use_global_device_ids=true, to_apply=%region_11.0 | all-reduce | flops 2 | bytes 16 | tf_op jit(solution)/shard_map/psum | solution.py:92
  133.2 0.3 maximum_maximum_fusion.4
  134.3 0.7 copy-done.3
  135.2 2.3 %multiply_reduce_fusion = (f32[]{:T(128)}, f32[]{:T(128)}, f32[1,2,128,512]{3,2,1,0:T(8,128)}, f32[1,2,128,512]{3,2,1,0:T(8,128)}) fusion(f32[1,2,128,512]{3,2,1,0:T(8,128)S(1)} %copy-done.3, f32[]{:T(128)} %bitcast.12, f32[1,2,128,512]{3,2,1,0:T(8,128)S(1)} %get-tuple-element.22, f32[1,2,128,512]{3,2,1,0:T(8,128)S(1)} %get-tuple-element.35, ...), kind=kLoop, calls=%fused_computation.47 | loop fusion | flops 2490366 | bytes 5767188 | tf_op jit(solution)/shard_map/reduce_sum | solution.py:91
  137.4 14.6 %all-reduce = (f32[1]{0:T(128)}, f32[1]{0:T(128)}) all-reduce(f32[1]{0:T(128)} %bitcast.14, f32[1]{0:T(128)} %bitcast.15), channel_id=1, replica_groups=mesh['samp'=4,'gx'=2,'gy'=4] {'gx','gy'}, use_global_device_ids=true, to_apply=%region_15.0 | all-reduce | flops 2 | bytes 16 | tf_op jit(solution)/shard_map/psum | solution.py:92
  155.9 2.7 %multiply_subtract_fusion = (f32[1,2,128,512]{3,2,1,0:T(8,128)}, f32[1,2,128,512]{3,2,1,0:T(8,128)}) fusion(f32[1,2,128,512]{3,2,1,0:T(8,128)} %get-tuple-element.21, f32[1,2,128,512]{3,2,1,0:T(8,128)} %get-tuple-element.20, f32[]{:T(128)} %bitcast.17, f32[]{:T(128)} %bitcast.16, f32[1,2,128,512]{3,2,1,0:T(8,128)} %get-tuple-element.24, f32[]{:T(128)} %bitcast.12, ...), kind=kLoop, calls=%fused_computation.45 | loop fusion | flops 2490368 | bytes 3670044 | tf_op jit(solution)/shard_map/sub | solution.py:108
  (55 shorter events, 3.5 us)
Async XLA Ops:
  8.7 9.0 %copy-start = (f32[1,2,128,512]{3,2,1,0:T(8,128)S(1)}, f32[1,2,128,512]{3,2,1,0:T(8,128)}, u32[]{:S(2)}) copy-start(f32[1,2,128,512]{3,2,1,0:T(8,128)} %param.3) | copy-start | bytes 1572868
  15.3 5.0 %collective-permute-start = (f32[1,2,1,512]{3,2,1,0:T(1,128)S(1)}, f32[1,2,1,512]{3,2,1,0:T(1,128)S(1)}, u32[]{:S(2)}, u32[]{:S(2)}) collective-permute-start(f32[1,2,1,512]{3,2,1,0:T(1,128)S(1)} %slice.296), channel_id=1, source_target_pairs={{0,4},{1,5},{2,6},{3,7},{8,12},{9,13},{10,14},{11,15},{16,20},{17,... | collective-permute-start | bytes 12296 | tf_op jit(solution)/shard_map/ppermute | solution.py:14
  17.8 7.0 %collective-permute-start.2 = (f32[1,2,1,512]{3,2,1,0:T(1,128)S(1)}, f32[1,2,1,512]{3,2,1,0:T(1,128)S(1)}, u32[]{:S(2)}, u32[]{:S(2)}) collective-permute-start(f32[1,2,1,512]{3,2,1,0:T(1,128)S(1)} %get-tuple-element.82), channel_id=1, source_target_pairs={{0,4},{1,5},{2,6},{3,7},{8,12},{9,13},{10,14},{11,15},{16,20},{17,... | collective-permute-start | bytes 12296 | tf_op jit(solution)/shard_map/ppermute | solution.py:24
  19.1 5.7 %collective-permute-start.3 = (f32[1,2,1,512]{3,2,1,0:T(1,128)S(1)}, f32[1,2,1,512]{3,2,1,0:T(1,128)S(1)}, u32[]{:S(2)}, u32[]{:S(2)}) collective-permute-start(f32[1,2,1,512]{3,2,1,0:T(1,128)S(1)} %get-tuple-element.83), channel_id=1, source_target_pairs={{4,0},{5,1},{6,2},{7,3},{12,8},{13,9},{14,10},{15,11},{20,16},{21,... | collective-permute-start | bytes 12296 | tf_op jit(solution)/shard_map/ppermute | solution.py:25
  20.5 9.3 %collective-permute-start.1 = (f32[1,2,129,1]{3,2,1,0:T(8,128)S(1)}, f32[1,2,129,1]{3,2,1,0:T(8,128)S(1)}, u32[]{:S(2)}, u32[]{:S(2)}) collective-permute-start(f32[1,2,129,1]{3,2,1,0:T(8,128)S(1)} %pad_maximum_fusion.16), channel_id=1, source_target_pairs={{0,1},{1,2},{2,3},{4,5},{5,6},{6,7},{8,9},{9,10},{10,11},{12,13},{... | collective-permute-start | bytes 3104 | tf_op jit(solution)/shard_map/ppermute | solution.py:14
  24.9 7.4 %collective-permute-start.4 = (f32[1,2,130,1]{3,2,1,0:T(8,128)S(1)}, f32[1,2,130,1]{3,2,1,0:T(8,128)S(1)}, u32[]{:S(2)}, u32[]{:S(2)}) collective-permute-start(f32[1,2,130,1]{3,2,1,0:T(8,128)S(1)} %get-tuple-element.74), channel_id=1, source_target_pairs={{0,1},{1,2},{2,3},{4,5},{5,6},{6,7},{8,9},{9,10},{10,11},{12,13},{... | collective-permute-start | bytes 3128 | tf_op jit(solution)/shard_map/ppermute | solution.py:24
  28.4 8.0 %collective-permute-start.5 = (f32[1,2,130,1]{3,2,1,0:T(8,128)S(1)}, f32[1,2,130,1]{3,2,1,0:T(8,128)S(1)}, u32[]{:S(2)}, u32[]{:S(2)}) collective-permute-start(f32[1,2,130,1]{3,2,1,0:T(8,128)S(1)} %get-tuple-element.75), channel_id=1, source_target_pairs={{1,0},{2,1},{3,2},{5,4},{6,5},{7,6},{9,8},{10,9},{11,10},{13,12},{... | collective-permute-start | bytes 3128 | tf_op jit(solution)/shard_map/ppermute | solution.py:25
  38.6 2.9 %collective-permute-start.6 = (f32[1,2,1,512]{3,2,1,0:T(1,128)S(1)}, f32[1,2,1,512]{3,2,1,0:T(1,128)S(1)}, u32[]{:S(2)}, u32[]{:S(2)}) collective-permute-start(f32[1,2,1,512]{3,2,1,0:T(1,128)S(1)} %get-tuple-element.80), channel_id=1, source_target_pairs={{0,4},{1,5},{2,6},{3,7},{8,12},{9,13},{10,14},{11,15},{16,20},{17,... | collective-permute-start | bytes 12296 | tf_op jit(solution)/shard_map/ppermute | solution.py:24
  40.2 3.1 %collective-permute-start.7 = (f32[1,2,1,512]{3,2,1,0:T(1,128)S(1)}, f32[1,2,1,512]{3,2,1,0:T(1,128)S(1)}, u32[]{:S(2)}, u32[]{:S(2)}) collective-permute-start(f32[1,2,1,512]{3,2,1,0:T(1,128)S(1)} %get-tuple-element.81), channel_id=1, source_target_pairs={{4,0},{5,1},{6,2},{7,3},{12,8},{13,9},{14,10},{15,11},{20,16},{21,... | collective-permute-start | bytes 12296 | tf_op jit(solution)/shard_map/ppermute | solution.py:25
  43.4 23.1 %collective-permute-start.8 = (f32[1,2,130,1]{3,2,1,0:T(8,128)S(1)}, f32[1,2,130,1]{3,2,1,0:T(8,128)S(1)}, u32[]{:S(2)}, u32[]{:S(2)}) collective-permute-start(f32[1,2,130,1]{3,2,1,0:T(8,128)S(1)} %get-tuple-element.70), channel_id=1, source_target_pairs={{0,1},{1,2},{2,3},{4,5},{5,6},{6,7},{8,9},{9,10},{10,11},{12,13},{... | collective-permute-start | bytes 3128 | tf_op jit(solution)/shard_map/ppermute | solution.py:24
  46.9 19.6 %collective-permute-start.9 = (f32[1,2,130,1]{3,2,1,0:T(8,128)S(1)}, f32[1,2,130,1]{3,2,1,0:T(8,128)S(1)}, u32[]{:S(2)}, u32[]{:S(2)}) collective-permute-start(f32[1,2,130,1]{3,2,1,0:T(8,128)S(1)} %get-tuple-element.71), channel_id=1, source_target_pairs={{1,0},{2,1},{3,2},{5,4},{6,5},{7,6},{9,8},{10,9},{11,10},{13,12},{... | collective-permute-start | bytes 3128 | tf_op jit(solution)/shard_map/ppermute | solution.py:25
  69.7 2.9 %collective-permute-start.10 = (f32[1,2,1,512]{3,2,1,0:T(1,128)S(1)}, f32[1,2,1,512]{3,2,1,0:T(1,128)S(1)}, u32[]{:S(2)}, u32[]{:S(2)}) collective-permute-start(f32[1,2,1,512]{3,2,1,0:T(1,128)S(1)} %get-tuple-element.78), channel_id=1, source_target_pairs={{0,4},{1,5},{2,6},{3,7},{8,12},{9,13},{10,14},{11,15},{16,20},{17,... | collective-permute-start | bytes 12296 | tf_op jit(solution)/shard_map/ppermute | solution.py:24
  71.4 3.1 %collective-permute-start.11 = (f32[1,2,1,512]{3,2,1,0:T(1,128)S(1)}, f32[1,2,1,512]{3,2,1,0:T(1,128)S(1)}, u32[]{:S(2)}, u32[]{:S(2)}) collective-permute-start(f32[1,2,1,512]{3,2,1,0:T(1,128)S(1)} %get-tuple-element.79), channel_id=1, source_target_pairs={{4,0},{5,1},{6,2},{7,3},{12,8},{13,9},{14,10},{15,11},{20,16},{21,... | collective-permute-start | bytes 12296 | tf_op jit(solution)/shard_map/ppermute | solution.py:25
  74.6 24.8 %collective-permute-start.12 = (f32[1,2,130,1]{3,2,1,0:T(8,128)S(1)}, f32[1,2,130,1]{3,2,1,0:T(8,128)S(1)}, u32[]{:S(2)}, u32[]{:S(2)}) collective-permute-start(f32[1,2,130,1]{3,2,1,0:T(8,128)S(1)} %get-tuple-element.66), channel_id=1, source_target_pairs={{0,1},{1,2},{2,3},{4,5},{5,6},{6,7},{8,9},{9,10},{10,11},{12,13},{... | collective-permute-start | bytes 3128 | tf_op jit(solution)/shard_map/ppermute | solution.py:24
  76.3 23.1 %collective-permute-start.13 = (f32[1,2,130,1]{3,2,1,0:T(8,128)S(1)}, f32[1,2,130,1]{3,2,1,0:T(8,128)S(1)}, u32[]{:S(2)}, u32[]{:S(2)}) collective-permute-start(f32[1,2,130,1]{3,2,1,0:T(8,128)S(1)} %get-tuple-element.67), channel_id=1, source_target_pairs={{1,0},{2,1},{3,2},{5,4},{6,5},{7,6},{9,8},{10,9},{11,10},{13,12},{... | collective-permute-start | bytes 3128 | tf_op jit(solution)/shard_map/ppermute | solution.py:25
  100.1 1.0 copy-start.1
  100.1 1.2 copy-start.5
  103.5 3.6 %collective-permute-start.14 = (f32[1,2,1,512]{3,2,1,0:T(1,128)S(1)}, f32[1,2,1,512]{3,2,1,0:T(1,128)S(1)}, u32[]{:S(2)}, u32[]{:S(2)}) collective-permute-start(f32[1,2,1,512]{3,2,1,0:T(1,128)S(1)} %get-tuple-element.76), channel_id=1, source_target_pairs={{0,4},{1,5},{2,6},{3,7},{8,12},{9,13},{10,14},{11,15},{16,20},{17,... | collective-permute-start | bytes 12296 | tf_op jit(solution)/shard_map/ppermute | solution.py:24
  105.8 3.1 %collective-permute-start.15 = (f32[1,2,1,512]{3,2,1,0:T(1,128)S(1)}, f32[1,2,1,512]{3,2,1,0:T(1,128)S(1)}, u32[]{:S(2)}, u32[]{:S(2)}) collective-permute-start(f32[1,2,1,512]{3,2,1,0:T(1,128)S(1)} %get-tuple-element.77), channel_id=1, source_target_pairs={{4,0},{5,1},{6,2},{7,3},{12,8},{13,9},{14,10},{15,11},{20,16},{21,... | collective-permute-start | bytes 12296 | tf_op jit(solution)/shard_map/ppermute | solution.py:25
  109.7 23.5 %collective-permute-start.16 = (f32[1,2,130,1]{3,2,1,0:T(8,128)}, f32[1,2,130,1]{3,2,1,0:T(8,128)S(1)}, u32[]{:S(2)}, u32[]{:S(2)}) collective-permute-start(f32[1,2,130,1]{3,2,1,0:T(8,128)} %get-tuple-element.62), channel_id=1, source_target_pairs={{0,1},{1,2},{2,3},{4,5},{5,6},{6,7},{8,9},{9,10},{10,11},{12,13},{... | collective-permute-start | bytes 3128 | tf_op jit(solution)/shard_map/ppermute | solution.py:24
  111.0 22.2 %collective-permute-start.17 = (f32[1,2,130,1]{3,2,1,0:T(8,128)}, f32[1,2,130,1]{3,2,1,0:T(8,128)S(1)}, u32[]{:S(2)}, u32[]{:S(2)}) collective-permute-start(f32[1,2,130,1]{3,2,1,0:T(8,128)} %get-tuple-element.63), channel_id=1, source_target_pairs={{1,0},{2,1},{3,2},{5,4},{6,5},{7,6},{9,8},{10,9},{11,10},{13,12},{... | collective-permute-start | bytes 3128 | tf_op jit(solution)/shard_map/ppermute | solution.py:25
  134.0 1.0 copy-start.3
  134.0 1.2 copy-start.4
  134.2 21.7 %copy-start.2 = (f32[1,2,128,512]{3,2,1,0:T(8,128)S(1)}, f32[1,2,128,512]{3,2,1,0:T(8,128)}, u32[]{:S(2)}) copy-start(f32[1,2,128,512]{3,2,1,0:T(8,128)} %get-tuple-element.37) | copy-start | bytes 1572868
where the time goes:
time: 159 us
  blocking collectives  65.7 us (41%)
  starting transfers between devices  33.8 us (21%)
  other arithmetic  16.9 us (11%)
  local copies, waits for them, and re-layouts  15.6 us (10%)
  between operations  14.9 us (9%)
  waiting for transfers between devices  11.7 us (7%)
    psum x4, blocking collectives, on_device(): gamma, delta = lax.psum((local_gamma, local_delta), ('gx', 'gy'))  65.7 us
    ppermute x8, starting transfers between devices, padded_2(): before = lax.ppermute(last, axis, up)  16.8 us
    broadcast_in_dim x4, local copies, waits for them, and re-layouts, expand(): jnp.broadcast_to(tiles[:, :, None, :, None], (count, rows, TILE, cols, TI...  13 us
    ppermute x8, starting transfers between devices, padded_2(): after = lax.ppermute(leading, axis, down)  10.3 us
    ppermute x8, waiting for transfers between devices, padded_2(): after = lax.ppermute(leading, axis, down)  9.38 us
    reduce_sum x4, other arithmetic, on_device(): local_delta = jnp.sum(w_vec * residual, axis=(1, 2, 3))  7.56 us
    ppermute x2, starting transfers between devices, shifted(): return lax.ppermute(block, axis, route)  6.7 us
  transfers between devices with their start and end apart: 18, of which 5 were waited for; matrix products, arithmetic and copies ran while one was open for 0% of the time, Pallas kernels for 0%

commit v1 on v0

v1 whole, which is shorter than its diff:
```python
import functools

import jax
import jax.numpy as jnp
from jax import lax
from jax.experimental import pallas as pl
from jax.experimental.pallas import tpu as pltpu
from jax.sharding import PartitionSpec as P

TILE = 8
CLASSES = 8
ITERS = 4
HALO = ITERS
LANES = 128
STRIP = 2 * TILE
F32 = jnp.float32


def iota(shape, dim):
    return lax.broadcasted_iota(jnp.int32, shape, dim)


def fast_two_sum(a, b):
    s = a + b
    return s, b - (s - a)


def two_sum(a, b):
    s = a + b
    t = s - a
    return s, (a - (s - t)) + (b - t)


def split(a):
    t = 4097.0 * a
    high = t - (t - a)
    return high, a - high


def two_prod(a, b):
    p = a * b
    ah, al = split(a)
    bh, bl = split(b)
    return p, ((ah * bh - p) + ah * bl + al * bh) + al * bl


def ds_add(x, y):
    s, e = two_sum(x[0], y[0])
    return fast_two_sum(s, e + (x[1] + y[1]))


def ds_mul(x, y):
    p, e = two_prod(x[0], y[0])
    return fast_two_sum(p, e + (x[0] * y[1] + x[1] * y[0]))


def ds_neg(x):
    return -x[0], -x[1]


def ds_div(x, y):
    inverse = 1.0 / y[0]
    first = x[0] * inverse
    p, e = two_prod(first, y[0])
    rest = ((x[0] - p) - e) + (x[1] - first * y[1])
    return fast_two_sum(first, rest * inverse)


def stress(c, n, lam, mu, right):
    rows = c[0][0].shape
    last = iota(rows, 0) == TILE - 1
    along_x, along_y = [], []
    for comp in range(2):
        tile, up = c[comp]
        down = jnp.where(last, n[comp][1], up)
        diff = down - tile
        total = down + tile
        along_x.append(diff + right(diff))
        along_y.append(right(total) - total)
    exx, eyy = along_x[0], along_y[1]
    trace = lam * (exx + eyy)
    two_mu = mu + mu
    return trace + two_mu * exx, trace + two_mu * eyy, mu * (along_y[0] + along_x[1])


def moved(s):
    return tuple(pltpu.roll(x, 1, 0) for x in s)


def forces(s, here, before, left):
    first = iota(s[0].shape, 0) == 0
    xx, yy, xy = s
    pxx, pyy, pxy = (jnp.where(first, b, h) for b, h in zip(before, here))
    dxx = pxx - xx
    sxy = pxy + xy
    dxy = pxy - xy
    syy = pyy + yy
    return left(dxx + sxy) + (dxx - sxy), left(dxy + syy) + (dxy - syy)


def apply(v, k, tiles, moduli, edge_moduli, edge_mask, right, left):
    def load(t):
        pair = [v[k, c, TILE * t : TILE * (t + 1), :] for c in range(2)]
        return [(x, pltpu.roll(x, TILE - 1, 0)) for x in pair]

    first = load(0)
    edge = load(tiles)
    edge_stress = stress(edge, first, *edge_moduli, right)
    edge_moved = moved(edge_stress)
    before = edge_moved
    here = first
    own = jnp.zeros(first[0][0].shape, F32)
    cross = own
    for t in range(tiles):
        after = load(t + 1)
        s = stress(here, after, *moduli(t), right)
        m = moved(s)
        push = forces(s, m, before, left)
        for c in range(2):
            old = here[c][0]
            new = 0.05 * old + push[c]
            v[k + 1, c, TILE * t : TILE * (t + 1), :] = new
            own = own + old * old
            cross = cross + old * new
        before = m
        here = after
    if k + 1 < ITERS:
        push = forces(edge_stress, edge_moved, before, left)
        for c in range(2):
            new = (0.05 * edge[c][0] + push[c]) * edge_mask
            v[k + 1, c, TILE * tiles : TILE * (tiles + 1), :] = new
    return own, cross


def moment_rows(parts, keep):
    row = iota((2 * ITERS, LANES), 0)
    result = jnp.zeros((2 * ITERS, LANES), F32)
    for index, part in enumerate(parts):
        part = jnp.where(keep, part, 0.0)
        folded = part[:, :LANES]
        for start in range(LANES, part.shape[1], LANES):
            folded = folded + part[:, start : start + LANES]
        total = jnp.sum(folded, axis=0, keepdims=True)
        result = jnp.where(row == index, total, result)
    return result


def prepare(table, top, bottom, material, moduli, *packets, gx):
    rows, cols = material.shape[1:]
    width = top.shape[3]
    spread = iota((cols, width), 1) // TILE == iota((cols, width), 0)
    kinds = jnp.dot(
        material[0].astype(F32).astype(jnp.bfloat16),
        spread.astype(F32).astype(jnp.bfloat16),
        preferred_element_type=F32,
    )
    for which in range(2):
        values = jnp.zeros((rows, width), F32)
        for k in range(CLASSES):
            values = jnp.where(kinds == float(k), 0.25 * table[which, k], values)
        moduli[which] = values
    place = lax.axis_index("gx")

    def fill(packet, down):
        for c in range(2):
            packet[c] = jnp.where(down, bottom[0, c], top[0, c])
            row = jnp.where(down, moduli[c, rows - 1 : rows, :], moduli[c, 0:1, :])
            packet[2, c : c + 1, :] = row
        packet[2, 2:, :] = jnp.zeros((TILE - 2, width), F32)

    if gx == 2:
        fill(packets[0], place == 0)
    else:
        fill(packets[0], True)
        fill(packets[1], False)


def block(load, moduli, above, below, v, packet, *, gx):
    rows, width = load.shape[2:]
    tiles = rows // TILE
    place = lax.axis_index("gx")
    has_above = place > 0
    has_below = place < gx - 1
    sub = iota((TILE, width), 0)
    low = sub < HALO

    def beside(a, b):
        return jnp.where(low, jnp.where(has_below, b, 0.0), jnp.where(has_above, a, 0.0))

    for c in range(2):
        v[0, c, :rows, :] = load[0, c]
        v[0, c, rows : rows + TILE, :] = beside(above[c], below[c])
    edge = [beside(above[2, c : c + 1, :], below[2, c : c + 1, :]) for c in range(2)]
    mask = jnp.where(low, jnp.where(has_below, 1.0, 0.0), 1.0)

    def row_of(t):
        return tuple(jnp.broadcast_to(moduli[c, t : t + 1, :], (TILE, width)) for c in range(2))

    right = lambda x: pltpu.roll(x, width - 1, 1)
    left = lambda x: pltpu.roll(x, 1, 1)
    parts = []
    for k in range(ITERS):
        parts += apply(v, k, tiles, row_of, edge, mask, right, left)
    lane = iota((TILE, width), 1)
    keep = (lane >= HALO) & (lane < width - HALO)
    packet_rows = packet.shape[0]
    packet[packet_rows - TILE :, :] = moment_rows(parts, keep)

    lane = iota((TILE, LANES), 1)
    short = iota((TILE, LANES), 0)
    tile_rows = moduli.shape[1]
    for group in range(packet_rows // TILE - 1):
        result = jnp.zeros((TILE, LANES), F32)
        for part in range(4):
            slot = 4 * group + part
            for c in range(2):
                offset = 32 * part + 16 * c
                if slot <= tiles:
                    ends = [v[0, c, TILE * slot : TILE * (slot + 1), s] for s in (slice(0, LANES), slice(width - LANES, width))]
                elif TILE * (slot - tiles - 1) < tile_rows:
                    first = TILE * (slot - tiles - 1)
                    ends = [moduli[c, first : first + TILE, s] for s in (slice(0, LANES), slice(width - LANES, width))]
                elif TILE * (slot - tiles - 1) == tile_rows:
                    ends = []
                    for s in (slice(0, LANES), slice(width - LANES, width)):
                        x = edge[c][:, s]
                        ends.append(jnp.where(short == 0, x[0:1, :], x[TILE - 1 :, :]))
                else:
                    continue
                first, final = ends
                first = pltpu.roll(first, offset, 1) if offset else first
                final = pltpu.roll(final, (offset + STRIP) % LANES, 1)
                result = jnp.where((lane >= offset) & (lane < offset + TILE), first, result)
                result = jnp.where((lane >= offset + TILE) & (lane < offset + STRIP), final, result)
        packet[TILE * group : TILE * (group + 1), :] = result


def interfaces(*refs, gx, gy, tiles, sources):
    packets = refs[:gy]
    v, moments, lam_rows = refs[gy:]
    mine = lax.axis_index("gy")
    place = lax.axis_index("gx")
    has_below = place < gx - 1
    groups = packets[0].shape[0] // TILE - 1

    def sort(rows):
        arrived = [p[rows, :] for p in packets]
        result = []
        for q in range(gy):
            chosen = arrived[0]
            for k in range(1, gy):
                chosen = jnp.where(sources(mine, k) == q, arrived[k], chosen)
            result.append(chosen)
        return result

    lane = iota((TILE, LANES), 1)
    sub = iota((TILE, LANES), 0)
    for group in range(groups):
        pieces = sort(slice(TILE * group, TILE * (group + 1)))
        for part in range(4):
            slot = 4 * group + part
            for c in range(2):
                result = jnp.zeros((TILE, LANES), F32)
                for q in range(gy):
                    shift = (STRIP * q - 32 * part - 16 * c) % LANES
                    piece = pltpu.roll(pieces[q], shift, 1) if shift else pieces[q]
                    result = jnp.where((lane >= STRIP * q) & (lane < STRIP * (q + 1)), piece, result)
                if slot <= tiles:
                    v[0, c, TILE * slot : TILE * (slot + 1), :] = result
                else:
                    first = TILE * (slot - tiles - 1)
                    if first + TILE <= lam_rows.shape[1]:
                        lam_rows[c, first : first + TILE, :] = result
    low = sub < HALO
    edge = [jnp.where(low, lam_rows[c, tiles : tiles + 1, :], lam_rows[c, tiles + 1 : tiles + 2, :]) for c in range(2)]
    mask = jnp.where(low, jnp.where(has_below, 1.0, 0.0), 1.0)

    def row_of(t):
        return tuple(jnp.broadcast_to(lam_rows[c, t : t + 1, :], (TILE, LANES)) for c in range(2))

    at_end = lane == STRIP * gy - 1
    at_start = lane == 0
    right = lambda x: jnp.where(at_end, 0.0, pltpu.roll(x, LANES - 1, 1))
    left = lambda x: jnp.where(at_start, 0.0, pltpu.roll(x, 1, 1))
    parts = []
    for k in range(ITERS):
        parts += apply(v, k, tiles, row_of, edge, mask, right, left)
    column = lane % STRIP
    keep = ((column < HALO) | (column >= STRIP - HALO)) & (lane < STRIP * gy)
    high = moment_rows(parts, keep)
    rest = jnp.zeros_like(high)
    for piece in sort(slice(TILE * groups, TILE * (groups + 1))):
        high, e = two_sum(high, piece)
        rest = rest + e
    moments[0] = high
    moments[1] = rest


def coefficients(moments):
    shape = moments[0].shape
    take = lambda x, l: jnp.broadcast_to(x[l : l + 1, :], shape)
    s = [(take(moments[0], l), take(moments[1], l)) for l in range(2 * ITERS)]
    q = list(s)
    zero = (jnp.zeros(shape, F32), jnp.zeros(shape, F32))
    one = (jnp.ones(shape, F32), zero[0])
    solution = []
    residual = [one]
    direction = []
    for k in range(ITERS):
        if k:
            beta = ds_neg(ds_div(ds_mul(alpha, s[k]), previous))
            q = [None] * k + [ds_add(s[l], ds_mul(beta, q[l])) if l < len(s) else None for l in range(k, len(q))]
            q = q[: len(s)]
            grown = [ds_mul(beta, x) for x in direction] + [None]
            direction = [ds_add(r, g) if g is not None else r for r, g in zip(residual, grown)]
        else:
            direction = [one]
        alpha = ds_div(s[k], q[k + 1])
        previous = s[k]
        if k + 1 < ITERS:
            s = [None] * (k + 1) + [ds_add(s[l], ds_neg(ds_mul(alpha, q[l + 1]))) for l in range(k + 1, len(s) - 1)]
        step = [ds_mul(alpha, x) for x in direction]
        solution = [ds_add(a, b) for a, b in zip(solution, step)] + [step[-1]]
        residual = [residual[0]] + [ds_add(r, ds_neg(b)) for r, b in zip(residual[1:], step)] + [ds_neg(step[-1])]
    return [x[0] for x in solution], [x[0] for x in residual]


def combine(*refs, gx):
    gathered = refs[:gx]
    v, strips, solution, residual = refs[gx:]
    rows, width = solution.shape[2:]
    total = (gathered[0][0], gathered[0][1])
    for other in gathered[1:]:
        total = ds_add(total, (other[0], other[1]))
    distance = LANES // 2
    while distance:
        total = ds_add(total, tuple(pltpu.roll(x, distance, 1) for x in total))
        distance //= 2
    weights = coefficients(total)
    mine = lax.axis_index("gy")
    lane = iota((TILE, LANES), 1)
    to_left = lax.rem(LANES - STRIP * mine, LANES)
    to_right = lax.rem(2 * LANES - STRIP - STRIP * mine, LANES)
    for t in range(rows // TILE):
        at = slice(TILE * t, TILE * (t + 1))
        for c in range(2):
            for out, w in zip((solution, residual), weights):
                edge = sum(w[k] * strips[k, c, at, :] for k in range(len(w)))
                for start in range(0, width, LANES):
                    value = sum(w[k] * v[k, c, at, start : start + LANES] for k in range(len(w)))
                    if start == 0:
                        value = jnp.where(lane < HALO, pltpu.roll(edge, to_left, 1), value)
                    if start + LANES == width:
                        value = jnp.where(lane >= LANES - HALO, pltpu.roll(edge, to_right, 1), value)
                    out[0, c, at, start : start + LANES] = value


def routes(n):
    if n & (n - 1) == 0:
        return [[(i, i ^ k) for i in range(n)] for k in range(1, n)]
    return [[(i, (i + k) % n) for i in range(n)] for k in range(1, n)]


def source_of(n):
    if n & (n - 1) == 0:
        return lambda mine, k: mine ^ k
    return lambda mine, k: lax.rem(mine - k + n, n)


def on_device(load, material, lame_table):
    gx, gy = lax.axis_size("gx"), lax.axis_size("gy")
    rows, width = load.shape[2:]
    tiles = rows // TILE
    tile_rows = material.shape[1]
    vmem = pl.BlockSpec(memory_space=pltpu.VMEM)
    shape = lambda *dims: jax.ShapeDtypeStruct(dims, F32)

    packets = 1 if gx == 2 else 2
    moduli, *sent = pl.pallas_call(
        functools.partial(prepare, gx=gx),
        grid=(1,),
        in_specs=[
            pl.BlockSpec(memory_space=pltpu.SMEM),
            pl.BlockSpec((1, 2, TILE, width), lambda i: (0, 0, 0, 0)),
            pl.BlockSpec((1, 2, TILE, width), lambda i: (0, 0, tiles - 1, 0)),
            pl.BlockSpec(material.shape, lambda i: (0, 0, 0)),
        ],
        out_specs=[pl.BlockSpec((2, tile_rows, width), lambda i: (0, 0, 0))]
        + [pl.BlockSpec((3, TILE, width), lambda i: (0, 0, 0))] * packets,
        out_shape=[shape(2, tile_rows, width)] + [shape(3, TILE, width)] * packets,
        name="prepare",
    )(lame_table, load, load, material)

    if gx == 2:
        above = below = lax.ppermute(sent[0], "gx", [(0, 1), (1, 0)])
    else:
        above = lax.ppermute(sent[0], "gx", [(i, i + 1) for i in range(gx - 1)])
        below = lax.ppermute(sent[1], "gx", [(i + 1, i) for i in range(gx - 1)])

    slots = tiles + 1 + -(-(tile_rows + 2) // TILE)
    packet_rows = TILE * (-(-slots // 4) + 1)
    v, packet = pl.pallas_call(
        functools.partial(block, gx=gx),
        in_specs=[vmem] * 4,
        out_specs=[vmem] * 2,
        out_shape=[shape(ITERS + 1, 2, rows + TILE, width), shape(packet_rows, LANES)],
        name="block",
    )(load, moduli, above, below)

    arrived = [packet] + [lax.ppermute(packet, "gy", route) for route in routes(gy)]
    strips, moments = pl.pallas_call(
        functools.partial(interfaces, gx=gx, gy=gy, tiles=tiles, sources=source_of(gy)),
        in_specs=[vmem] * gy,
        out_specs=[vmem] * 2,
        out_shape=[shape(ITERS + 1, 2, rows + TILE, LANES), shape(2, 2 * ITERS, LANES)],
        scratch_shapes=[pltpu.VMEM((2, tile_rows + TILE, LANES), F32)],
        name="interfaces",
    )(*arrived)

    gathered = [moments] + [lax.ppermute(moments, "gx", route) for route in routes(gx)]
    return pl.pallas_call(
        functools.partial(combine, gx=gx),
        in_specs=[vmem] * (gx + 2),
        out_specs=[vmem] * 2,
        out_shape=[shape(*load.shape)] * 2,
        name="combine",
    )(*gathered, v, strips)


def solution(mesh):
    return jax.shard_map(
        on_device,
        mesh=mesh,
        in_specs=(P("samp", None, "gx", "gy"), P("samp", "gx", "gy"), P()),
        out_specs=(P("samp", None, "gx", "gy"), P("samp", None, "gx", "gy")),
        check_vma=False,
    )
```

time: 159 us -> 34 us (0.21)
  blocking collectives: 65.7 us -> 0 us
  starting transfers between devices: 33.8 us -> 6 us
  Pallas kernels: 0 us -> 17.8 us
  other arithmetic: 16.9 us -> 0 us
  between operations: 14.9 us -> 0.64 us
  local copies, waits for them, and re-layouts: 15.6 us -> 2.42 us
  waiting for transfers between devices: 11.7 us -> 6.84 us
    psum x4 -> x0, blocking collectives: 65.7 us -> none  [on_device(): gamma, delta = lax.psum((local_gamma, local_delta), ('gx', 'gy'))]
    ppermute x18 -> x5, starting transfers between devices: 33.8 us -> 6 us  [the longest x3 5.5 us: on_device(): lax.ppermute(packet, 'gy', route)]
    pallas_call x0 -> x4, Pallas kernels: none -> 17.8 us  [the longest x1 9.2 us: on_device(): pl.pallas_call(functools.partial(block, gx=gx), in_specs=[vmem] * 4, out_...]
    broadcast_in_dim x4 -> x0, local copies, waits for them, and re-layouts: 13 us -> none  [expand(): jnp.broadcast_to(tiles[:, :, None, :, None], (count, rows, TILE, cols, TI...]
    reduce_sum x5 -> x0, other arithmetic: 8.37 us -> none  [the longest x4 7.56 us: on_device(): local_delta = jnp.sum(w_vec * residual, axis=(1, 2, 3))]
    ppermute x18 -> x5, waiting for transfers between devices: 11.7 us -> 6.84 us  [the longest x3 4.37 us: on_device(): lax.ppermute(packet, 'gy', route)]
    sub x5 -> x0, other arithmetic: 2.85 us -> none  [the longest x1 2.66 us: on_device(): residual = residual - alpha_b * q_vec]
    mul x11 -> x0, other arithmetic: 1.6 us -> none  [the longest x4 1.1 us: cell_terms(): along_x = 0.5 * (high_low + high_high - (low_low + low_high))]
  transfers between devices with their start and end apart: 18 -> 5, of which waited for: 5 -> 4; matrix products, arithmetic and copies ran while one was open for 0% -> 0% of each run, Pallas kernels for 0% -> 0%
where the time goes in v1:
time: 34 us; the launch traced here: 33.7 us
  Pallas kernels  17.8 us (52%)
  waiting for transfers between devices  6.84 us (20%)
  starting transfers between devices  6 us (18%)
  local copies, waits for them, and re-layouts  2.42 us (7%)
  between operations  0.64 us (2%)
    pallas_call x1, Pallas kernels, on_device(): pl.pallas_call(functools.partial(block, gx=gx), in_specs=[vmem] * 4, out_...  9.2 us
    ppermute x3, starting transfers between devices, on_device(): lax.ppermute(packet, 'gy', route)  5.5 us
    ppermute x3, waiting for transfers between devices, on_device(): lax.ppermute(packet, 'gy', route)  4.37 us
    pallas_call x1, Pallas kernels, on_device(): pl.pallas_call(functools.partial(combine, gx=gx), in_specs=[vmem] * (gx +...  4.05 us
    pallas_call x1, Pallas kernels, on_device(): pl.pallas_call(functools.partial(interfaces, gx=gx, gy=gy, tiles=tiles, s...  2.92 us
    unnamed x10, local copies, waits for them, and re-layouts  2.42 us
    pallas_call x1, Pallas kernels, on_device(): pl.pallas_call(functools.partial(prepare, gx=gx), grid=(1,), in_specs=[pl...  1.62 us
    ppermute x1, waiting for transfers between devices, on_device(): lax.ppermute(moments, 'gx', route)  1.38 us
  transfers between devices with their start and end apart: 5, of which 4 were waited for; matrix products, arithmetic and copies ran while one was open for 0% of the time, Pallas kernels for 0%

profile of v1, /device:TPU:0, one launch (start us, length us, event | category | flops | bytes accessed | tf_op | source)
XLA Modules:
  0.0 33.7 jit_solution(1367489787724282679)
XLA Ops:
  0.6 1.6 %prepare.1 = (f32[2,16,512]{2,1,0:T(8,128)}, f32[3,8,512]{2,1,0:T(8,128)}) custom-call(f32[2,8]{1,0:T(2,128)} %table.1, f32[1,2,128,512]{3,2,1,0:T(8,128)} %load.1, f32[1,2,128,512]{3,2,1,0:T(8,128)} %load.1, s32[1,16,64]{2,1,0:T(8,128)} %material.1), custom_call_target="tpu_custom_call" | custom-call | tf_op jit(solution)/shard_map/prepare/pallas_call | solution.py:379
  2.3 0.5 %collective-permute-start = (f32[3,8,512]{2,1,0:T(8,128)}, f32[3,8,512]{2,1,0:T(8,128)S(1)}, u32[]{:S(2)}, u32[]{:S(2)}) collective-permute-start(f32[3,8,512]{2,1,0:T(8,128)} %get-tuple-element.9), channel_id=1, source_target_pairs={{0,4},{4,0},{1,5},{5,1},{2,6},{6,2},{3,7},{7,3},{8,12},{12,8},{9,1... | collective-permute-start | bytes 147464 | tf_op jit(solution)/shard_map/ppermute | solution.py:395
  2.7 1.1 %collective-permute-done.above.below = f32[3,8,512]{2,1,0:T(8,128)S(1)} collective-permute-done((f32[3,8,512]{2,1,0:T(8,128)}, f32[3,8,512]{2,1,0:T(8,128)S(1)}, u32[]{:S(2)}, u32[]{:S(2)}) %collective-permute-start) | collective-permute-done | bytes 49184 | tf_op jit(solution)/shard_map/ppermute | solution.py:395
  3.8 0.0 copy-start
  3.8 0.6 %copy-done = f32[3,8,512]{2,1,0:T(8,128)} copy-done((f32[3,8,512]{2,1,0:T(8,128)}, f32[3,8,512]{2,1,0:T(8,128)S(1)}, u32[]{:S(2)}) %copy-start) | copy-done | bytes 49176
  4.5 9.2 %block.1 = (f32[5,2,136,512]{3,2,1,0:T(8,128)}, f32[48,128]{1,0:T(8,128)}) custom-call(f32[1,2,128,512]{3,2,1,0:T(8,128)} %load.1, f32[2,16,512]{2,1,0:T(8,128)} %get-tuple-element.8.moduli, f32[3,8,512]{2,1,0:T(8,128)} %copy-done, f32[3,8,512]{2,1,0:T(8,128)} %copy-done), custom_call_target="tpu_custom_call" | custom-call | tf_op jit(solution)/shard_map/block/pallas_call | solution.py:402
  13.7 4.9 %collective-permute-start.3 = (f32[48,128]{1,0:T(8,128)}, f32[48,128]{1,0:T(8,128)S(1)}, u32[]{:S(2)}, u32[]{:S(2)}) collective-permute-start(f32[48,128]{1,0:T(8,128)} %get-tuple-element.10.refs_0_), channel_id=1, source_target_pairs={{0,3},{1,2},{2,1},{3,0},{4,7},{5,6},{6,5},{7,4},{8,11},{9,10},{10,... | collective-permute-start | bytes 73736 | tf_op jit(solution)/shard_map/ppermute | solution.py:410
  18.6 0.0 collective-permute-start.2
  18.6 0.6 %collective-permute-start.1 = (f32[48,128]{1,0:T(8,128)}, f32[48,128]{1,0:T(8,128)S(1)}, u32[]{:S(2)}, u32[]{:S(2)}) collective-permute-start(f32[48,128]{1,0:T(8,128)} %get-tuple-element.10.refs_0_), channel_id=1, source_target_pairs={{0,1},{1,0},{2,3},{3,2},{4,5},{5,4},{6,7},{7,6},{8,9},{9,8},{10,11... | collective-permute-start | bytes 73736 | tf_op jit(solution)/shard_map/ppermute | solution.py:410
  19.2 1.4 %collective-permute-done.3.refs_3_ = f32[48,128]{1,0:T(8,128)S(1)} collective-permute-done((f32[48,128]{1,0:T(8,128)}, f32[48,128]{1,0:T(8,128)S(1)}, u32[]{:S(2)}, u32[]{:S(2)}) %collective-permute-start.3) | collective-permute-done | bytes 24608 | tf_op jit(solution)/shard_map/ppermute | solution.py:410
  20.6 0.0 copy-start.1
  20.6 2.9 %collective-permute-done.2.refs_2_ = f32[48,128]{1,0:T(8,128)S(1)} collective-permute-done((f32[48,128]{1,0:T(8,128)}, f32[48,128]{1,0:T(8,128)S(1)}, u32[]{:S(2)}, u32[]{:S(2)}) %collective-permute-start.2) | collective-permute-done | bytes 24608 | tf_op jit(solution)/shard_map/ppermute | solution.py:410
  23.5 0.0 copy-start.2
  23.5 0.0 collective-permute-done.1.refs_1_
  23.5 0.0 copy-done.1
  23.5 0.6 %copy-done.2 = f32[48,128]{1,0:T(8,128)} copy-done((f32[48,128]{1,0:T(8,128)}, f32[48,128]{1,0:T(8,128)S(1)}, u32[]{:S(2)}) %copy-start.2) | copy-done | bytes 24600
  24.1 0.0 copy-start.3
  24.1 0.6 %copy-done.3 = f32[48,128]{1,0:T(8,128)} copy-done((f32[48,128]{1,0:T(8,128)}, f32[48,128]{1,0:T(8,128)S(1)}, u32[]{:S(2)}) %copy-start.3) | copy-done | bytes 24600
  24.7 2.9 %interfaces.1 = (f32[5,2,136,128]{3,2,1,0:T(8,128)}, f32[2,8,128]{2,1,0:T(8,128)}) custom-call(f32[48,128]{1,0:T(8,128)} %get-tuple-element.10.refs_0_, f32[48,128]{1,0:T(8,128)} %copy-done.3, f32[48,128]{1,0:T(8,128)} %copy-done.2, f32[48,128]{1,0:T(8,128)} %copy-done.1), custom_call_target="tpu_custom_call" | custom-call | tf_op jit(solution)/shard_map/interfaces/pallas_call | solution.py:411
  27.7 0.0 collective-permute-start.4
  27.7 1.4 %collective-permute-done.4.refs_1_ = f32[2,8,128]{2,1,0:T(8,128)S(1)} collective-permute-done((f32[2,8,128]{2,1,0:T(8,128)}, f32[2,8,128]{2,1,0:T(8,128)S(1)}, u32[]{:S(2)}, u32[]{:S(2)}) %collective-permute-start.4) | collective-permute-done | bytes 8224 | tf_op jit(solution)/shard_map/ppermute | solution.py:420
  29.1 0.0 copy-start.4
  29.1 0.6 %copy-done.4 = f32[2,8,128]{2,1,0:T(8,128)} copy-done((f32[2,8,128]{2,1,0:T(8,128)}, f32[2,8,128]{2,1,0:T(8,128)S(1)}, u32[]{:S(2)}) %copy-start.4) | copy-done | bytes 8216
  29.6 4.0 %combine.1 = (f32[1,2,128,512]{3,2,1,0:T(8,128)}, f32[1,2,128,512]{3,2,1,0:T(8,128)}) custom-call(f32[2,8,128]{2,1,0:T(8,128)} %get-tuple-element.11.refs_0_, f32[2,8,128]{2,1,0:T(8,128)} %copy-done.4, f32[5,2,136,512]{3,2,1,0:T(8,128)} %get-tuple-element.12.refs_2_, f32[5,2,136,128]{3,2,1,0:T(8,128)} %get-tuple-element.13.refs_3_), custom_call_target="tpu_custom_call" | custom-call | tf_op jit(solution)/shard_map/combine/pallas_call | solution.py:421
Async XLA Ops:
  2.3 1.6 %collective-permute-start = (f32[3,8,512]{2,1,0:T(8,128)}, f32[3,8,512]{2,1,0:T(8,128)S(1)}, u32[]{:S(2)}, u32[]{:S(2)}) collective-permute-start(f32[3,8,512]{2,1,0:T(8,128)} %get-tuple-element.9), channel_id=1, source_target_pairs={{0,4},{4,0},{1,5},{5,1},{2,6},{6,2},{3,7},{7,3},{8,12},{12,8},{9,1... | collective-permute-start | bytes 147464 | tf_op jit(solution)/shard_map/ppermute | solution.py:395
  3.8 0.6 %copy-start = (f32[3,8,512]{2,1,0:T(8,128)}, f32[3,8,512]{2,1,0:T(8,128)S(1)}, u32[]{:S(2)}) copy-start(f32[3,8,512]{2,1,0:T(8,128)S(1)} %collective-permute-done.above.below) | copy-start | bytes 147460
  13.7 6.9 %collective-permute-start.3 = (f32[48,128]{1,0:T(8,128)}, f32[48,128]{1,0:T(8,128)S(1)}, u32[]{:S(2)}, u32[]{:S(2)}) collective-permute-start(f32[48,128]{1,0:T(8,128)} %get-tuple-element.10.refs_0_), channel_id=1, source_target_pairs={{0,3},{1,2},{2,1},{3,0},{4,7},{5,6},{6,5},{7,4},{8,11},{9,10},{10,... | collective-permute-start | bytes 73736 | tf_op jit(solution)/shard_map/ppermute | solution.py:410
  18.6 4.9 %collective-permute-start.2 = (f32[48,128]{1,0:T(8,128)}, f32[48,128]{1,0:T(8,128)S(1)}, u32[]{:S(2)}, u32[]{:S(2)}) collective-permute-start(f32[48,128]{1,0:T(8,128)} %get-tuple-element.10.refs_0_), channel_id=1, source_target_pairs={{0,2},{1,3},{2,0},{3,1},{4,6},{5,7},{6,4},{7,5},{8,10},{9,11},{10,... | collective-permute-start | bytes 73736 | tf_op jit(solution)/shard_map/ppermute | solution.py:410
  18.6 4.9 %collective-permute-start.1 = (f32[48,128]{1,0:T(8,128)}, f32[48,128]{1,0:T(8,128)S(1)}, u32[]{:S(2)}, u32[]{:S(2)}) collective-permute-start(f32[48,128]{1,0:T(8,128)} %get-tuple-element.10.refs_0_), channel_id=1, source_target_pairs={{0,1},{1,0},{2,3},{3,2},{4,5},{5,4},{6,7},{7,6},{8,9},{9,8},{10,11... | collective-permute-start | bytes 73736 | tf_op jit(solution)/shard_map/ppermute | solution.py:410
  20.6 2.9 %copy-start.1 = (f32[48,128]{1,0:T(8,128)}, f32[48,128]{1,0:T(8,128)S(1)}, u32[]{:S(2)}) copy-start(f32[48,128]{1,0:T(8,128)S(1)} %collective-permute-done.3.refs_3_) | copy-start | bytes 73732
  23.5 0.6 %copy-start.2 = (f32[48,128]{1,0:T(8,128)}, f32[48,128]{1,0:T(8,128)S(1)}, u32[]{:S(2)}) copy-start(f32[48,128]{1,0:T(8,128)S(1)} %collective-permute-done.2.refs_2_) | copy-start | bytes 73732
  24.1 0.6 %copy-start.3 = (f32[48,128]{1,0:T(8,128)}, f32[48,128]{1,0:T(8,128)S(1)}, u32[]{:S(2)}) copy-start(f32[48,128]{1,0:T(8,128)S(1)} %collective-permute-done.1.refs_1_) | copy-start | bytes 73732
  27.7 1.4 %collective-permute-start.4 = (f32[2,8,128]{2,1,0:T(8,128)}, f32[2,8,128]{2,1,0:T(8,128)S(1)}, u32[]{:S(2)}, u32[]{:S(2)}) collective-permute-start(f32[2,8,128]{2,1,0:T(8,128)} %get-tuple-element.11.refs_0_), channel_id=1, source_target_pairs={{0,4},{4,0},{1,5},{5,1},{2,6},{6,2},{3,7},{7,3},{8,12},{12,8},{9,1... | collective-permute-start | bytes 24584 | tf_op jit(solution)/shard_map/ppermute | solution.py:420
  29.1 0.6 %copy-start.4 = (f32[2,8,128]{2,1,0:T(8,128)}, f32[2,8,128]{2,1,0:T(8,128)S(1)}, u32[]{:S(2)}) copy-start(f32[2,8,128]{2,1,0:T(8,128)S(1)} %collective-permute-done.4.refs_1_) | copy-start | bytes 24580

commit v2 on v1

--- a/solution.py
+++ b/solution.py
@@ -13,6 +13,7 @@
 HALO = ITERS
 LANES = 128
 STRIP = 2 * TILE
+VMEM_LIMIT = 16 << 20
 F32 = jnp.float32
 
 
@@ -373,7 +374,9 @@
     tiles = rows // TILE
     tile_rows = material.shape[1]
     vmem = pl.BlockSpec(memory_space=pltpu.VMEM)
-    shape = lambda *dims: jax.ShapeDtypeStruct(dims, F32)
+    shape = lambda *dims: pltpu.VMEM(dims, F32)
+    params = pltpu.CompilerParams(vmem_limit_bytes=VMEM_LIMIT)
+    pin = lambda x: pltpu.with_memory_space_constraint(x, pltpu.VMEM)
 
     packets = 1 if gx == 2 else 2
     moduli, *sent = pl.pallas_call(
@@ -388,8 +391,9 @@
         out_specs=[pl.BlockSpec((2, tile_rows, width), lambda i: (0, 0, 0))]
         + [pl.BlockSpec((3, TILE, width), lambda i: (0, 0, 0))] * packets,
         out_shape=[shape(2, tile_rows, width)] + [shape(3, TILE, width)] * packets,
+        compiler_params=params,
         name="prepare",
-    )(lame_table, load, load, material)
+    )(*(pltpu.with_memory_space_constraint(x, pltpu.HBM) for x in (lame_table, load, load, material)))
 
     if gx == 2:
         above = below = lax.ppermute(sent[0], "gx", [(0, 1), (1, 0)])
@@ -404,8 +408,9 @@
         in_specs=[vmem] * 4,
         out_specs=[vmem] * 2,
         out_shape=[shape(ITERS + 1, 2, rows + TILE, width), shape(packet_rows, LANES)],
+        compiler_params=params,
         name="block",
-    )(load, moduli, above, below)
+    )(pin(load), pin(moduli), pin(above), pin(below))
 
     arrived = [packet] + [lax.ppermute(packet, "gy", route) for route in routes(gy)]
     strips, moments = pl.pallas_call(
@@ -414,17 +419,19 @@
         out_specs=[vmem] * 2,
         out_shape=[shape(ITERS + 1, 2, rows + TILE, LANES), shape(2, 2 * ITERS, LANES)],
         scratch_shapes=[pltpu.VMEM((2, tile_rows + TILE, LANES), F32)],
+        compiler_params=params,
         name="interfaces",
-    )(*arrived)
+    )(*map(pin, arrived))
 
     gathered = [moments] + [lax.ppermute(moments, "gx", route) for route in routes(gx)]
     return pl.pallas_call(
         functools.partial(combine, gx=gx),
         in_specs=[vmem] * (gx + 2),
         out_specs=[vmem] * 2,
-        out_shape=[shape(*load.shape)] * 2,
+        out_shape=[jax.ShapeDtypeStruct(load.shape, F32)] * 2,
+        compiler_params=params,
         name="combine",
-    )(*gathered, v, strips)
+    )(*map(pin, gathered), pin(v), pin(strips))
 
 
 def solution(mesh):

time: 34 us -> 25.4 us (0.75)
  Pallas kernels: 17.8 us -> 11 us
  local copies, waits for them, and re-layouts: 2.42 us -> 1.04 us
  waiting for transfers between devices: 6.84 us -> 6.12 us
    pallas_call x1, Pallas kernels: 9.2 us -> 6.66 us  [on_device(): pl.pallas_call(functools.partial(block, gx=gx), in_specs=[vmem] * 4, out_...]
    pallas_call x1, Pallas kernels: 4.05 us -> 2.1 us  [on_device(): pl.pallas_call(functools.partial(combine, gx=gx), in_specs=[vmem] * (gx +...]
    pallas_call x1, Pallas kernels: 2.92 us -> 1.31 us  [on_device(): pl.pallas_call(functools.partial(interfaces, gx=gx, gy=gy, tiles=tiles, s...]
    unnamed x10 -> x2, local copies, waits for them, and re-layouts: 2.42 us -> 1.04 us
    pallas_call x1, Pallas kernels: 1.62 us -> 0.99 us  [on_device(): pl.pallas_call(functools.partial(prepare, gx=gx), grid=(1,), in_specs=[pl...]
where the time goes in v2:
time: 25.4 us; the launch traced here: 25.1 us
  Pallas kernels  11 us (43%)
  starting transfers between devices  6.27 us (25%)
  waiting for transfers between devices  6.12 us (24%)
  local copies, waits for them, and re-layouts  1.04 us (4%)
  between operations  0.65 us (3%)
    pallas_call x1, Pallas kernels, on_device(): pl.pallas_call(functools.partial(block, gx=gx), in_specs=[vmem] * 4, out_...  6.66 us
    ppermute x3, starting transfers between devices, on_device(): lax.ppermute(packet, 'gy', route)  5.64 us
    ppermute x3, waiting for transfers between devices, on_device(): lax.ppermute(packet, 'gy', route)  4.08 us
    pallas_call x1, Pallas kernels, on_device(): pl.pallas_call(functools.partial(combine, gx=gx), in_specs=[vmem] * (gx +...  2.1 us
    pallas_call x1, Pallas kernels, on_device(): pl.pallas_call(functools.partial(interfaces, gx=gx, gy=gy, tiles=tiles, s...  1.31 us
    ppermute x1, waiting for transfers between devices, on_device(): lax.ppermute(moments, 'gx', route)  1.16 us
    unnamed x2, local copies, waits for them, and re-layouts  1.04 us
    pallas_call x1, Pallas kernels, on_device(): pl.pallas_call(functools.partial(prepare, gx=gx), grid=(1,), in_specs=[pl...  0.99 us
  transfers between devices with their start and end apart: 5, of which 4 were waited for; matrix products, arithmetic and copies ran while one was open for 0% of the time, Pallas kernels for 0%

profile of v2, /device:TPU:0, one launch (start us, length us, event | category | flops | bytes accessed | tf_op | source)
XLA Modules:
  0.0 25.1 jit_solution(1502857323040103005)
XLA Ops:
  0.6 1.0 %prepare.1 = (f32[2,16,512]{2,1,0:T(8,128)S(1)}, f32[3,8,512]{2,1,0:T(8,128)S(1)}) custom-call(f32[2,8]{1,0:T(2,128)} %table.1, f32[1,2,128,512]{3,2,1,0:T(8,128)} %load.1, f32[1,2,128,512]{3,2,1,0:T(8,128)} %load.1, s32[1,16,64]{2,1,0:T(8,128)} %material.1), custom_call_target="tpu_custom_call" | custom-call | tf_op jit(solution)/shard_map/prepare/pallas_call | solution.py:382
  1.6 0.6 %collective-permute-start = (f32[3,8,512]{2,1,0:T(8,128)S(1)}, f32[3,8,512]{2,1,0:T(8,128)S(1)}, u32[]{:S(2)}, u32[]{:S(2)}) collective-permute-start(f32[3,8,512]{2,1,0:T(8,128)S(1)} %get-tuple-element.9), channel_id=1, source_target_pairs={{0,4},{4,0},{1,5},{5,1},{2,6},{6,2},{3,7},{7,3},{8,12},{12,8},{9,1... | collective-permute-start | bytes 147464 | tf_op jit(solution)/shard_map/ppermute | solution.py:399
  2.2 0.9 %collective-permute-done.above.below = f32[3,8,512]{2,1,0:T(8,128)S(1)} collective-permute-done((f32[3,8,512]{2,1,0:T(8,128)S(1)}, f32[3,8,512]{2,1,0:T(8,128)S(1)}, u32[]{:S(2)}, u32[]{:S(2)}) %collective-permute-start) | collective-permute-done | bytes 49184 | tf_op jit(solution)/shard_map/ppermute | solution.py:399
  3.1 0.0 copy-start
  3.1 1.0 %copy-done = f32[1,2,128,512]{3,2,1,0:T(8,128)S(1)} copy-done((f32[1,2,128,512]{3,2,1,0:T(8,128)S(1)}, f32[1,2,128,512]{3,2,1,0:T(8,128)}, u32[]{:S(2)}) %copy-start) | copy-done | bytes 524312
  4.1 6.7 %block.1 = (f32[5,2,136,512]{3,2,1,0:T(8,128)S(1)}, f32[48,128]{1,0:T(8,128)S(1)}) custom-call(f32[1,2,128,512]{3,2,1,0:T(8,128)S(1)} %copy-done, f32[2,16,512]{2,1,0:T(8,128)S(1)} %get-tuple-element.8.moduli, f32[3,8,512]{2,1,0:T(8,128)S(1)} %collective-permute-done.above.below, f32[3,8,512]{2,1,0:T(8,128)S(1)} %collective-permute-done.above.below), custom_call_target="tpu_custom_call" | custom-call | tf_op jit(solution)/shard_map/block/pallas_call | solution.py:406
  10.8 5.0 %collective-permute-start.3 = (f32[48,128]{1,0:T(8,128)S(1)}, f32[48,128]{1,0:T(8,128)S(1)}, u32[]{:S(2)}, u32[]{:S(2)}) collective-permute-start(f32[48,128]{1,0:T(8,128)S(1)} %get-tuple-element.10.refs_0_), channel_id=1, source_target_pairs={{0,3},{1,2},{2,1},{3,0},{4,7},{5,6},{6,5},{7,4},{8,11},{9,10},{10,... | collective-permute-start | bytes 73736 | tf_op jit(solution)/shard_map/ppermute | solution.py:415
  15.8 0.0 collective-permute-start.2
  15.8 0.6 %collective-permute-start.1 = (f32[48,128]{1,0:T(8,128)S(1)}, f32[48,128]{1,0:T(8,128)S(1)}, u32[]{:S(2)}, u32[]{:S(2)}) collective-permute-start(f32[48,128]{1,0:T(8,128)S(1)} %get-tuple-element.10.refs_0_), channel_id=1, source_target_pairs={{0,1},{1,0},{2,3},{3,2},{4,5},{5,4},{6,7},{7,6},{8,9},{9,8},{10,11... | collective-permute-start | bytes 73736 | tf_op jit(solution)/shard_map/ppermute | solution.py:415
  16.4 1.2 %collective-permute-done.3.refs_3_ = f32[48,128]{1,0:T(8,128)S(1)} collective-permute-done((f32[48,128]{1,0:T(8,128)S(1)}, f32[48,128]{1,0:T(8,128)S(1)}, u32[]{:S(2)}, u32[]{:S(2)}) %collective-permute-start.3) | collective-permute-done | bytes 24608 | tf_op jit(solution)/shard_map/ppermute | solution.py:415
  17.6 2.9 %collective-permute-done.2.refs_2_ = f32[48,128]{1,0:T(8,128)S(1)} collective-permute-done((f32[48,128]{1,0:T(8,128)S(1)}, f32[48,128]{1,0:T(8,128)S(1)}, u32[]{:S(2)}, u32[]{:S(2)}) %collective-permute-start.2) | collective-permute-done | bytes 24608 | tf_op jit(solution)/shard_map/ppermute | solution.py:415
  20.5 0.0 collective-permute-done.1.refs_1_
  20.5 1.3 %interfaces.1 = (f32[5,2,136,128]{3,2,1,0:T(8,128)S(1)}, f32[2,8,128]{2,1,0:T(8,128)S(1)}) custom-call(f32[48,128]{1,0:T(8,128)S(1)} %get-tuple-element.10.refs_0_, f32[48,128]{1,0:T(8,128)S(1)} %collective-permute-done.1.refs_1_, f32[48,128]{1,0:T(8,128)S(1)} %collective-permute-done.2.refs_2_, f32[48,128]{1,0:T(8,128)S(1)} %collective-permute-done.3.refs_3_), custom_call_target="tpu_custom_call" | custom-call | tf_op jit(solution)/shard_map/interfaces/pallas_call | solution.py:416
  21.8 0.1 collective-permute-start.4
  21.9 1.2 %collective-permute-done.4.refs_1_ = f32[2,8,128]{2,1,0:T(8,128)S(1)} collective-permute-done((f32[2,8,128]{2,1,0:T(8,128)S(1)}, f32[2,8,128]{2,1,0:T(8,128)S(1)}, u32[]{:S(2)}, u32[]{:S(2)}) %collective-permute-start.4) | collective-permute-done | bytes 8224 | tf_op jit(solution)/shard_map/ppermute | solution.py:426
  23.0 2.1 %combine.1 = (f32[1,2,128,512]{3,2,1,0:T(8,128)}, f32[1,2,128,512]{3,2,1,0:T(8,128)}) custom-call(f32[2,8,128]{2,1,0:T(8,128)S(1)} %get-tuple-element.11.refs_0_, f32[2,8,128]{2,1,0:T(8,128)S(1)} %collective-permute-done.4.refs_1_, f32[5,2,136,512]{3,2,1,0:T(8,128)S(1)} %get-tuple-element.12.refs_2_, f32[5,2,136,128]{3,2,1,0:T(8,128)S(1)} %get-tuple-element.13.refs_3_), custom_call_target="tpu_custom_call" | custom-call | tf_op jit(solution)/shard_map/combine/pallas_call | solution.py:427
Async XLA Ops:
  1.6 1.4 %collective-permute-start = (f32[3,8,512]{2,1,0:T(8,128)S(1)}, f32[3,8,512]{2,1,0:T(8,128)S(1)}, u32[]{:S(2)}, u32[]{:S(2)}) collective-permute-start(f32[3,8,512]{2,1,0:T(8,128)S(1)} %get-tuple-element.9), channel_id=1, source_target_pairs={{0,4},{4,0},{1,5},{5,1},{2,6},{6,2},{3,7},{7,3},{8,12},{12,8},{9,1... | collective-permute-start | bytes 147464 | tf_op jit(solution)/shard_map/ppermute | solution.py:399
  3.1 1.0 %copy-start = (f32[1,2,128,512]{3,2,1,0:T(8,128)S(1)}, f32[1,2,128,512]{3,2,1,0:T(8,128)}, u32[]{:S(2)}) copy-start(f32[1,2,128,512]{3,2,1,0:T(8,128)} %load.1) | copy-start | bytes 1572868
  10.8 6.8 %collective-permute-start.3 = (f32[48,128]{1,0:T(8,128)S(1)}, f32[48,128]{1,0:T(8,128)S(1)}, u32[]{:S(2)}, u32[]{:S(2)}) collective-permute-start(f32[48,128]{1,0:T(8,128)S(1)} %get-tuple-element.10.refs_0_), channel_id=1, source_target_pairs={{0,3},{1,2},{2,1},{3,0},{4,7},{5,6},{6,5},{7,4},{8,11},{9,10},{10,... | collective-permute-start | bytes 73736 | tf_op jit(solution)/shard_map/ppermute | solution.py:415
  15.8 4.7 %collective-permute-start.2 = (f32[48,128]{1,0:T(8,128)S(1)}, f32[48,128]{1,0:T(8,128)S(1)}, u32[]{:S(2)}, u32[]{:S(2)}) collective-permute-start(f32[48,128]{1,0:T(8,128)S(1)} %get-tuple-element.10.refs_0_), channel_id=1, source_target_pairs={{0,2},{1,3},{2,0},{3,1},{4,6},{5,7},{6,4},{7,5},{8,10},{9,11},{10,... | collective-permute-start | bytes 73736 | tf_op jit(solution)/shard_map/ppermute | solution.py:415
  15.8 4.7 %collective-permute-start.1 = (f32[48,128]{1,0:T(8,128)S(1)}, f32[48,128]{1,0:T(8,128)S(1)}, u32[]{:S(2)}, u32[]{:S(2)}) collective-permute-start(f32[48,128]{1,0:T(8,128)S(1)} %get-tuple-element.10.refs_0_), channel_id=1, source_target_pairs={{0,1},{1,0},{2,3},{3,2},{4,5},{5,4},{6,7},{7,6},{8,9},{9,8},{10,11... | collective-permute-start | bytes 73736 | tf_op jit(solution)/shard_map/ppermute | solution.py:415
  21.8 1.2 %collective-permute-start.4 = (f32[2,8,128]{2,1,0:T(8,128)S(1)}, f32[2,8,128]{2,1,0:T(8,128)S(1)}, u32[]{:S(2)}, u32[]{:S(2)}) collective-permute-start(f32[2,8,128]{2,1,0:T(8,128)S(1)} %get-tuple-element.11.refs_0_), channel_id=1, source_target_pairs={{0,4},{4,0},{1,5},{5,1},{2,6},{6,2},{3,7},{7,3},{8,12},{12,8},{9,1... | collective-permute-start | bytes 24584 | tf_op jit(solution)/shard_map/ppermute | solution.py:426

commit v3 on v2

v3 whole, which is shorter than its diff:
```python
import functools

import jax
import jax.numpy as jnp
from jax import lax
from jax.experimental import pallas as pl
from jax.experimental.pallas import tpu as pltpu
from jax.sharding import PartitionSpec as P

TILE = 8
CLASSES = 8
ITERS = 4
HALO = ITERS
LANES = 128
STRIP = 2 * TILE
VMEM_LIMIT = 16 << 20
F32 = jnp.float32


def iota(shape, dim):
    return lax.broadcasted_iota(jnp.int32, shape, dim)


def fast_two_sum(a, b):
    s = a + b
    return s, b - (s - a)


def two_sum(a, b):
    s = a + b
    t = s - a
    return s, (a - (s - t)) + (b - t)


def split(a):
    t = 4097.0 * a
    high = t - (t - a)
    return high, a - high


def two_prod(a, b):
    p = a * b
    ah, al = split(a)
    bh, bl = split(b)
    return p, ((ah * bh - p) + ah * bl + al * bh) + al * bl


def ds_add(x, y):
    s, e = two_sum(x[0], y[0])
    return fast_two_sum(s, e + (x[1] + y[1]))


def ds_mul(x, y):
    p, e = two_prod(x[0], y[0])
    return fast_two_sum(p, e + (x[0] * y[1] + x[1] * y[0]))


def ds_neg(x):
    return -x[0], -x[1]


def ds_scale(c, x):
    p, e = two_prod(jnp.full(x[0].shape, c, F32), x[0])
    return fast_two_sum(p, e + c * x[1])


def ds_inverse(x):
    first = 1.0 / x[0]
    p, e = two_prod(first, x[0])
    rest = ((1.0 - p) - e) - first * x[1]
    return fast_two_sum(first, first * rest)


def spread(x, right):
    beside = right(x)
    return x + beside, beside - x


def stress(here, below, bulk, mu):
    (p0, m0), (p1, m1) = here
    (n0, o0), (n1, o1) = below
    exx, eyy = n0 - p0, o1 + m1
    gxy = (o0 + m0) + (n1 - p1)
    mean = bulk * (exx + eyy)
    apart = mu * (exx - eyy)
    return mean + apart, mean - apart, mu * gxy


def forces(before, s, left):
    pxx, pyy, pxy = before
    xx, yy, xy = s
    dxx = pxx - xx
    sxy = pxy + xy
    dxy = pxy - xy
    syy = pyy + yy
    return left(dxx + sxy) + (dxx - sxy), left(dxy + syy) + (dxy - syy)


def apply(k, v, strips, moduli, partial, mask, tiles, right, left):
    groups = tiles // TILE
    sub = iota(strips.shape[2:], 0)
    up = lambda x: pltpu.roll(x, TILE - 1, 0)
    down = lambda x: pltpu.roll(x, 1, 0)
    tile = lambda c, t: v[k, c, TILE * t : TILE * (t + 1), :]
    modulus = lambda g: (moduli[0, g], moduli[1, g])

    top, bottom = ([strips[s, c] for c in range(2)] for s in range(2))
    above = [jnp.where(sub == 0, pltpu.roll(top[c], 5, 0), down(tile(c, tiles - 1))) for c in range(2)]
    below = [jnp.where(sub == TILE - 1, pltpu.roll(bottom[c], 3, 0), up(tile(c, 0))) for c in range(2)]

    for s, old in enumerate((top, bottom)):
        here = [spread(x, right) for x in old]
        after = [(up(p), up(m)) for p, m in here]
        t = stress(here, after, *modulus(groups + 1 + s))
        new = forces(tuple(down(x) for x in t), t, left)
        for c in range(2):
            strips[s, c] = new[c] * mask if s else new[c]

    own = cross = None
    old = [tile(c, 0) for c in range(2)]
    here = [spread(x, right) for x in old]
    before = stress([spread(x, right) for x in above], here, *modulus(groups))
    for t in range(tiles):
        ahead = [tile(c, t + 1) for c in range(2)] if t + 1 < tiles else below
        after = [spread(x, right) for x in ahead]
        s = stress(here, after, *modulus(t // TILE))
        new = forces(before, s, left)
        square = old[0] * old[0] + old[1] * old[1]
        mixed = old[0] * new[0] + old[1] * new[1]
        own = square if own is None else own + square
        cross = mixed if cross is None else cross + mixed
        for c in range(2):
            v[k + 1, c, TILE * t : TILE * (t + 1), :] = new[c]
        before, here, old = s, after, ahead
    partial[2 * k] = own
    partial[2 * k + 1] = cross


def moment_rows(partial, keep):
    row = iota((2 * ITERS, LANES), 0)
    result = jnp.zeros((2 * ITERS, LANES), F32)
    for index in range(2 * ITERS):
        part = jnp.where(keep, partial[index], 0.0)
        folded = part[:, :LANES]
        for start in range(LANES, part.shape[1], LANES):
            folded = folded + part[:, start : start + LANES]
        total = jnp.sum(folded, axis=0, keepdims=True)
        result = jnp.where(row == index, total, result)
    return result


def fill_moduli(moduli, c, groups, first, last, edge):
    sub = iota(edge.shape, 0)
    low = sub < HALO
    above, below = edge[1:2, :], edge[0:1, :]
    moduli[c, groups] = jnp.where(sub == 0, above, pltpu.roll(moduli[c, groups - 1], 1, 0))
    moduli[c, groups + 1] = jnp.where(low, above, first)
    moduli[c, groups + 2] = jnp.where(low, last, below)


def fill_strips(strips, c, halo, first, last):
    low = iota(halo.shape, 0) < HALO
    strips[0, c] = pltpu.roll(jnp.where(low, first, halo), HALO, 0)
    strips[1, c] = pltpu.roll(jnp.where(low, halo, last), HALO, 0)


def prepare(table, load, material, u, moduli, *rest, gx):
    *packets, kinds_buffer, lines, sems = rest
    rows, cols = material.shape[1:]
    height, width = load.shape[2:]
    groups = rows // TILE
    columns = [slice(start, start + LANES) for start in range(0, width, LANES)]
    ends = [slice(0, TILE), slice(height - TILE, height)]
    first = pltpu.make_async_copy(material.at[0], kinds_buffer, sems.at[0, 0])
    first.start()
    copies = []
    for i, at in enumerate(ends + [slice(TILE, height - TILE)]):
        copies.append([])
        for l, lanes in enumerate(columns):
            copy = pltpu.make_async_copy(load.at[0, :, at, lanes], u.at[:, l, at, :], sems.at[i + 1, l])
            copy.start()
            copies[i].append(copy)
    first.wait()
    grid = (cols, width)
    expand = iota(grid, 1) // TILE == iota(grid, 0)
    kinds = jnp.dot(
        kinds_buffer[...].astype(F32).astype(jnp.bfloat16),
        expand.astype(F32).astype(jnp.bfloat16),
        preferred_element_type=F32,
    )
    bulk = jnp.zeros((rows, width), F32)
    shear = bulk
    for k in range(CLASSES):
        mu = 0.25 * table[1, k]
        here = kinds == float(k)
        bulk = jnp.where(here, 0.25 * table[0, k] + mu, bulk)
        shear = jnp.where(here, mu, shear)
    for c, values in enumerate((bulk, shear)):
        for l, lanes in enumerate(columns):
            lines[c, l] = values[:, lanes]
            for g in range(groups):
                moduli[c, g, :, lanes] = lines[c, l, pl.ds(g, TILE, stride=groups), :]
    place = lax.axis_index("gx")
    for copy in copies[0] + copies[1]:
        copy.wait()

    def fill(packet, down):
        for c in range(2):
            for l, lanes in enumerate(columns):
                packet[c, :, lanes] = jnp.where(down, u[c, l, ends[1], :], u[c, l, ends[0], :])
            row = jnp.where(down, moduli[c, groups - 1, TILE - 1 :, :], moduli[c, 0, 0:1, :])
            packet[2, c : c + 1, :] = row
        packet[2, 2:, :] = jnp.zeros((TILE - 2, width), F32)

    if gx == 2:
        fill(packets[0], place == 0)
    else:
        fill(packets[0], True)
        fill(packets[1], False)
    for copy in copies[2]:
        copy.wait()


def block(u, group_moduli, above, below, v, packet, strips, moduli, partial, *, gx):
    rows, width = v.shape[2:]
    tiles = rows // TILE
    columns = [slice(start, start + LANES) for start in range(0, width, LANES)]
    groups = tiles // TILE
    place = lax.axis_index("gx")
    has_above = place > 0
    has_below = place < gx - 1
    sub = iota((TILE, width), 0)
    low = sub < HALO

    halo, edge = [], []
    for c in range(2):
        under = jnp.where(has_below, below[c], 0.0)
        over = jnp.where(has_above, above[c], 0.0)
        halo.append(jnp.where(low, under, over))
        ends = (
            jnp.concatenate([u[c, l, at, :] for l in range(len(columns))], axis=1)
            for at in (slice(0, TILE), slice(rows - TILE, rows))
        )
        fill_strips(strips, c, halo[c], *ends)
        for t in range(tiles):
            for l, lanes in enumerate(columns):
                v[0, c, TILE * t : TILE * (t + 1), lanes] = u[c, l, pl.ds(t, TILE, stride=tiles), :]
        for g in range(groups):
            moduli[c, g] = group_moduli[c, g]
        under = jnp.where(has_below, below[2, c : c + 1, :], 0.0)
        over = jnp.where(has_above, above[2, c : c + 1, :], 0.0)
        edge.append(jnp.where(sub == 0, under, over))
        ends = moduli[c, 0, 0:1, :], moduli[c, groups - 1, TILE - 1 :, :]
        fill_moduli(moduli, c, groups, *ends, edge[c])
    mask = jnp.where(low, 1.0, jnp.where(has_below, 1.0, 0.0))
    right = lambda x: pltpu.roll(x, width - 1, 1)
    left = lambda x: pltpu.roll(x, 1, 1)

    lane = iota((TILE, LANES), 1)
    packet_rows = packet.shape[0]
    for group in range(packet_rows // TILE - 1):
        result = jnp.zeros((TILE, LANES), F32)
        for part in range(4):
            slot = 4 * group + part
            for c in range(2):
                if slot < tiles:
                    pick = lambda s: v[0, c, TILE * slot : TILE * (slot + 1), s]
                elif slot == tiles:
                    pick = lambda s: halo[c][:, s]
                elif slot <= tiles + groups:
                    pick = lambda s: moduli[c, slot - tiles - 1, :, s]
                elif slot == tiles + groups + 1:
                    pick = lambda s: edge[c][:, s]
                else:
                    continue
                offset = 32 * part + STRIP * c
                first = pick(slice(0, LANES))
                first = pltpu.roll(first, offset, 1) if offset else first
                final = pltpu.roll(pick(slice(width - LANES, width)), (offset + STRIP) % LANES, 1)
                result = jnp.where((lane >= offset) & (lane < offset + TILE), first, result)
                result = jnp.where((lane >= offset + TILE) & (lane < offset + STRIP), final, result)
        packet[TILE * group : TILE * (group + 1), :] = result

    @pl.loop(0, ITERS)
    def _(k):
        apply(k, v, strips, moduli, partial, mask, tiles, right, left)

    lane = iota((TILE, width), 1)
    keep = (lane >= HALO) & (lane < width - HALO)
    packet[packet_rows - TILE :, :] = moment_rows(partial, keep)


def interfaces(*refs, gx, gy, sources):
    packets = refs[:gy]
    v, moments, strips, moduli, partial = refs[gy:]
    tiles = v.shape[2] // TILE
    groups = tiles // TILE
    mine = lax.axis_index("gy")
    has_below = lax.axis_index("gx") < gx - 1
    lines = packets[0].shape[0] // TILE - 1

    def sort(rows):
        arrived = [p[rows, :] for p in packets]
        result = []
        for q in range(gy):
            chosen = arrived[0]
            for k in range(1, gy):
                chosen = jnp.where(sources(mine, k) == q, arrived[k], chosen)
            result.append(chosen)
        return result

    lane = iota((TILE, LANES), 1)
    sub = iota((TILE, LANES), 0)
    halo, edge = [None] * 2, [None] * 2
    for line in range(lines):
        pieces = sort(slice(TILE * line, TILE * (line + 1)))
        for part in range(4):
            slot = 4 * line + part
            for c in range(2):
                result = jnp.zeros((TILE, LANES), F32)
                for q in range(gy):
                    shift = (STRIP * q - 32 * part - STRIP * c) % LANES
                    piece = pltpu.roll(pieces[q], shift, 1) if shift else pieces[q]
                    result = jnp.where((lane >= STRIP * q) & (lane < STRIP * (q + 1)), piece, result)
                if slot < tiles:
                    v[0, c, TILE * slot : TILE * (slot + 1), :] = result
                elif slot == tiles:
                    halo[c] = result
                elif slot <= tiles + groups:
                    moduli[c, slot - tiles - 1] = result
                elif slot == tiles + groups + 1:
                    edge[c] = result
    for c in range(2):
        first = last = halo[c]
        for r in range(HALO):
            row = TILE * r
            first = jnp.where(sub == r, v[0, c, row : row + 1, :], first)
            row = TILE * (tiles - r) - 1
            last = jnp.where(sub == TILE - 1 - r, v[0, c, row : row + 1, :], last)
        fill_strips(strips, c, halo[c], first, last)
        ends = moduli[c, 0, 0:1, :], moduli[c, groups - 1, TILE - 1 :, :]
        fill_moduli(moduli, c, groups, *ends, edge[c])
    mask = jnp.where(sub < HALO, 1.0, jnp.where(has_below, 1.0, 0.0))
    at_end = lane == STRIP * gy - 1
    at_start = lane == 0
    right = lambda x: jnp.where(at_end, 0.0, pltpu.roll(x, LANES - 1, 1))
    left = lambda x: jnp.where(at_start, 0.0, pltpu.roll(x, 1, 1))

    @pl.loop(0, ITERS)
    def _(k):
        apply(k, v, strips, moduli, partial, mask, tiles, right, left)

    column = lane % STRIP
    keep = ((column < HALO) | (column >= STRIP - HALO)) & (lane < STRIP * gy)
    high = moment_rows(partial, keep)
    rest = jnp.zeros_like(high)
    for piece in sort(slice(TILE * lines, TILE * (lines + 1))):
        high, e = two_sum(high, piece)
        rest = rest + e
    moments[0] = high
    moments[1] = rest


def coefficients(moments):
    shape = moments[0].shape
    take = lambda x, l: jnp.broadcast_to(x[l : l + 1, :], shape)
    s = {l: (take(moments[0], l), take(moments[1], l)) for l in range(2 * ITERS)}
    q = dict(s)
    zero = jnp.zeros(shape, F32)
    residual = [zero + 1.0]
    solution = []
    for k in range(ITERS):
        if k:
            beta = ds_neg(ds_mul(s[k], inverse))
            q = {l: ds_add(s[l], ds_mul(beta, q[l])) for l in range(k, 2 * ITERS - k)}
            direction = [r + beta[0] * p for r, p in zip(residual, direction + [zero])]
        else:
            direction = residual
        push = {l: ds_add(ds_scale(0.05, q[l]), q[l + 1]) for l in range(k, 2 * ITERS - 1 - k)}
        inverse = ds_inverse(push[k])
        alpha = ds_mul(s[k], inverse)
        s = {l: ds_add(s[l], ds_neg(ds_mul(alpha, push[l]))) for l in range(k + 1, 2 * ITERS - 1 - k)}
        solution = [x + alpha[0] * p for x, p in zip(solution + [zero], direction)]
        change = [0.05 * a + b for a, b in zip(direction + [zero], [zero] + direction)]
        residual = [r - alpha[0] * d for r, d in zip(residual + [zero], change)]
    return solution, residual


def combine(*refs, gx):
    gathered = refs[:gx]
    v, strips, *outs, buffer, sems = refs[gx:]
    rows, width = v.shape[2:]
    tiles = rows // TILE
    columns = [slice(start, start + LANES) for start in range(0, width, LANES)]
    total = (gathered[0][0], gathered[0][1])
    for other in gathered[1:]:
        total = ds_add(total, (other[0], other[1]))
    distance = LANES // 2
    while distance:
        total = ds_add(total, tuple(pltpu.roll(x, distance, 1) for x in total))
        distance //= 2
    weights = coefficients(total)
    mine = lax.axis_index("gy")
    lane = iota((TILE, LANES), 1)
    to_left = lax.rem(LANES - STRIP * mine, LANES)
    to_right = lax.rem(2 * LANES - STRIP - STRIP * mine, LANES)
    copies = []
    for c in range(2):
        for i, w in enumerate(weights):

            @pl.loop(0, tiles, unroll=2)
            def _(t):
                at = pl.ds(pl.multiple_of(TILE * t, TILE), TILE)
                edge = sum(w[k] * strips[k, c, at, :] for k in range(len(w)))
                for l, lanes in enumerate(columns):
                    value = sum(w[k] * v[k, c, at, lanes] for k in range(len(w)))
                    if l == 0:
                        value = jnp.where(lane < HALO, pltpu.roll(edge, to_left, 1), value)
                    if l + 1 == len(columns):
                        value = jnp.where(lane >= LANES - HALO, pltpu.roll(edge, to_right, 1), value)
                    buffer[i, c, l, pl.ds(t, TILE, stride=tiles), :] = value

            for l, lanes in enumerate(columns):
                copy = pltpu.make_async_copy(buffer.at[i, c, l], outs[i].at[0, c, :, lanes], sems.at[i, c, l])
                copy.start()
                copies.append(copy)
    for copy in copies:
        copy.wait()


def routes(n):
    if n & (n - 1) == 0:
        return [[(i, i ^ k) for i in range(n)] for k in range(1, n)]
    return [[(i, (i + k) % n) for i in range(n)] for k in range(1, n)]


def source_of(n):
    if n & (n - 1) == 0:
        return lambda mine, k: mine ^ k
    return lambda mine, k: lax.rem(mine - k + n, n)


def on_device(load, material, lame_table):
    gx, gy = lax.axis_size("gx"), lax.axis_size("gy")
    rows, width = load.shape[2:]
    tiles = rows // TILE
    groups = tiles // TILE
    lines = width // LANES
    tile_rows, tile_cols = material.shape[1:]
    assert rows == TILE * TILE * groups and width % LANES == 0 and STRIP * gy <= LANES
    vmem = pl.BlockSpec(memory_space=pltpu.VMEM)
    hbm = pl.BlockSpec(memory_space=pltpu.HBM)
    shape = lambda *dims: pltpu.VMEM(dims, F32)
    params = pltpu.CompilerParams(vmem_limit_bytes=VMEM_LIMIT)
    pin = lambda x: pltpu.with_memory_space_constraint(x, pltpu.VMEM)
    far = lambda x: pltpu.with_memory_space_constraint(x, pltpu.HBM)
    work = lambda lanes: [
        pltpu.VMEM((2, 2, TILE, lanes), F32),
        pltpu.VMEM((2, groups + 3, TILE, lanes), F32),
        pltpu.VMEM((2 * ITERS, TILE, lanes), F32),
    ]

    packets = 1 if gx == 2 else 2
    u, moduli, *sent = pl.pallas_call(
        functools.partial(prepare, gx=gx),
        in_specs=[pl.BlockSpec(memory_space=pltpu.SMEM), hbm, hbm],
        out_specs=[vmem] * (2 + packets),
        out_shape=[shape(2, lines, rows, LANES), shape(2, groups, TILE, width)] + [shape(3, TILE, width)] * packets,
        scratch_shapes=[
            pltpu.VMEM((tile_rows, tile_cols), jnp.int32),
            pltpu.VMEM((2, lines, tile_rows, LANES), F32),
            pltpu.SemaphoreType.DMA((4, lines)),
        ],
        compiler_params=params,
        name="prepare",
    )(far(lame_table), far(load), far(material))

    if gx == 2:
        above = below = lax.ppermute(sent[0], "gx", [(0, 1), (1, 0)])
    else:
        above = lax.ppermute(sent[0], "gx", [(i, i + 1) for i in range(gx - 1)])
        below = lax.ppermute(sent[1], "gx", [(i + 1, i) for i in range(gx - 1)])

    slots = tiles + groups + 2
    packet_rows = TILE * (-(-slots // 4) + 1)
    v, packet = pl.pallas_call(
        functools.partial(block, gx=gx),
        in_specs=[vmem] * 4,
        out_specs=[vmem] * 2,
        out_shape=[shape(ITERS + 1, 2, rows, width), shape(packet_rows, LANES)],
        scratch_shapes=work(width),
        compiler_params=params,
        name="block",
    )(pin(u), pin(moduli), pin(above), pin(below))

    arrived = [packet] + [lax.ppermute(packet, "gy", route) for route in routes(gy)]
    strips, moments = pl.pallas_call(
        functools.partial(interfaces, gx=gx, gy=gy, sources=source_of(gy)),
        in_specs=[vmem] * gy,
        out_specs=[vmem] * 2,
        out_shape=[shape(ITERS + 1, 2, rows, LANES), shape(2, 2 * ITERS, LANES)],
        scratch_shapes=work(LANES),
        compiler_params=params,
        name="interfaces",
    )(*map(pin, arrived))

    gathered = [moments] + [lax.ppermute(moments, "gx", route) for route in routes(gx)]
    return pl.pallas_call(
        functools.partial(combine, gx=gx),
        in_specs=[vmem] * (gx + 2),
        out_specs=[hbm] * 2,
        out_shape=[jax.ShapeDtypeStruct(load.shape, F32)] * 2,
        scratch_shapes=[pltpu.VMEM((2, 2, lines, rows, LANES), F32), pltpu.SemaphoreType.DMA((2, 2, lines))],
        compiler_params=params,
        name="combine",
    )(*map(pin, gathered), pin(v), pin(strips))


def solution(mesh):
    return jax.shard_map(
        on_device,
        mesh=mesh,
        in_specs=(P("samp", None, "gx", "gy"), P("samp", "gx", "gy"), P()),
        out_specs=(P("samp", None, "gx", "gy"), P("samp", None, "gx", "gy")),
        check_vma=False,
    )
```

time: 25.4 us -> 25.7 us (1.012)
  Pallas kernels: 11 us -> 12.4 us
  local copies, waits for them, and re-layouts: 1.04 us -> 0 us
    pallas_call x1, Pallas kernels: 2.1 us -> 4.29 us  [on_device(): pl.pallas_call(functools.partial(combine, gx=gx), in_specs=[vmem] * (gx +...]
    pallas_call x1, Pallas kernels: 6.66 us -> 4.94 us  [on_device(): pl.pallas_call(functools.partial(block, gx=gx), in_specs=[vmem] * 4, out_...]
    unnamed x2 -> x0, local copies, waits for them, and re-layouts: 1.04 us -> none
    pallas_call x2, Pallas kernels: 2.29 us -> 3.15 us  [the longest x1 2.04 us: on_device(): pl.pallas_call(functools.partial(prepare, gx=gx), in_specs=[pl.BlockSpec(...]
where the time goes in v3:
time: 25.7 us; the launch traced here: 25.4 us
  Pallas kernels  12.4 us (48%)
  starting transfers between devices  6.27 us (24%)
  waiting for transfers between devices  6.12 us (24%)
  between operations  0.66 us (3%)
    ppermute x3, starting transfers between devices, on_device(): lax.ppermute(packet, 'gy', route)  5.64 us
    pallas_call x1, Pallas kernels, on_device(): pl.pallas_call(functools.partial(block, gx=gx), in_specs=[vmem] * 4, out_...  4.94 us
    pallas_call x1, Pallas kernels, on_device(): pl.pallas_call(functools.partial(combine, gx=gx), in_specs=[vmem] * (gx +...  4.29 us
    ppermute x3, waiting for transfers between devices, on_device(): lax.ppermute(packet, 'gy', route)  4.08 us
    pallas_call x1, Pallas kernels, on_device(): pl.pallas_call(functools.partial(prepare, gx=gx), in_specs=[pl.BlockSpec(...  2.04 us
    ppermute x1, waiting for transfers between devices, on_device(): lax.ppermute(moments, 'gx', route)  1.16 us
    pallas_call x1, Pallas kernels, on_device(): pl.pallas_call(functools.partial(interfaces, gx=gx, gy=gy, sources=source...  1.12 us
    ppermute x1, waiting for transfers between devices, on_device(): above = below = lax.ppermute(sent[0], 'gx', [(0, 1), (1, 0)])  0.88 us
  transfers between devices with their start and end apart: 5, of which 4 were waited for; matrix products, arithmetic and copies ran while one was open for 0% of the time, Pallas kernels for 0%

profile of v3, /device:TPU:0, one launch (start us, length us, event | category | flops | bytes accessed | tf_op | source)
XLA Modules:
  0.0 25.4 jit_solution(6010117893119254438)
XLA Ops:
  0.6 2.0 %prepare.1 = (f32[2,4,128,128]{3,2,1,0:T(8,128)S(1)}, f32[2,2,8,512]{3,2,1,0:T(8,128)S(1)}, f32[3,8,512]{2,1,0:T(8,128)S(1)}) custom-call(f32[2,8]{1,0:T(2,128)} %table.1, f32[1,2,128,512]{3,2,1,0:T(8,128)} %load.1, s32[1,16,64]{2,1,0:T(8,128)} %material.1), custom_call_target="tpu_custom_call" | custom-call | tf_op jit(solution)/shard_map/prepare/pallas_call | solution.py:464
  2.7 0.6 %collective-permute-start = (f32[3,8,512]{2,1,0:T(8,128)S(1)}, f32[3,8,512]{2,1,0:T(8,128)S(1)}, u32[]{:S(2)}, u32[]{:S(2)}) collective-permute-start(f32[3,8,512]{2,1,0:T(8,128)S(1)} %get-tuple-element.11), channel_id=1, source_target_pairs={{0,4},{4,0},{1,5},{5,1},{2,6},{6,2},{3,7},{7,3},{8,12},{12,8},{9,1... | collective-permute-start | bytes 147464 | tf_op jit(solution)/shard_map/ppermute | solution.py:479
  3.2 0.9 %collective-permute-done.above.below = f32[3,8,512]{2,1,0:T(8,128)S(1)} collective-permute-done((f32[3,8,512]{2,1,0:T(8,128)S(1)}, f32[3,8,512]{2,1,0:T(8,128)S(1)}, u32[]{:S(2)}, u32[]{:S(2)}) %collective-permute-start) | collective-permute-done | bytes 49184 | tf_op jit(solution)/shard_map/ppermute | solution.py:479
  4.1 4.9 %block.1 = (f32[5,2,128,512]{3,2,1,0:T(8,128)S(1)}, f32[48,128]{1,0:T(8,128)S(1)}) custom-call(f32[2,4,128,128]{3,2,1,0:T(8,128)S(1)} %get-tuple-element.9.u, f32[2,2,8,512]{3,2,1,0:T(8,128)S(1)} %get-tuple-element.10.group_moduli, f32[3,8,512]{2,1,0:T(8,128)S(1)} %collective-permute-done.above.below, f32[3,8,512]{2,1,0:T(8,128)S(1)} %collective-permute-done.above.below), custom_call_target="tpu_custom_call" | custom-call | tf_op jit(solution)/shard_map/block/pallas_call | solution.py:486
  9.1 5.0 %collective-permute-start.3 = (f32[48,128]{1,0:T(8,128)S(1)}, f32[48,128]{1,0:T(8,128)S(1)}, u32[]{:S(2)}, u32[]{:S(2)}) collective-permute-start(f32[48,128]{1,0:T(8,128)S(1)} %get-tuple-element.12.refs_0_), channel_id=1, source_target_pairs={{0,3},{1,2},{2,1},{3,0},{4,7},{5,6},{6,5},{7,4},{8,11},{9,10},{10,... | collective-permute-start | bytes 73736 | tf_op jit(solution)/shard_map/ppermute | solution.py:496
  14.1 0.0 collective-permute-start.2
  14.1 0.6 %collective-permute-start.1 = (f32[48,128]{1,0:T(8,128)S(1)}, f32[48,128]{1,0:T(8,128)S(1)}, u32[]{:S(2)}, u32[]{:S(2)}) collective-permute-start(f32[48,128]{1,0:T(8,128)S(1)} %get-tuple-element.12.refs_0_), channel_id=1, source_target_pairs={{0,1},{1,0},{2,3},{3,2},{4,5},{5,4},{6,7},{7,6},{8,9},{9,8},{10,11... | collective-permute-start | bytes 73736 | tf_op jit(solution)/shard_map/ppermute | solution.py:496
  14.7 1.2 %collective-permute-done.3.refs_3_ = f32[48,128]{1,0:T(8,128)S(1)} collective-permute-done((f32[48,128]{1,0:T(8,128)S(1)}, f32[48,128]{1,0:T(8,128)S(1)}, u32[]{:S(2)}, u32[]{:S(2)}) %collective-permute-start.3) | collective-permute-done | bytes 24608 | tf_op jit(solution)/shard_map/ppermute | solution.py:496
  15.9 2.9 %collective-permute-done.2.refs_2_ = f32[48,128]{1,0:T(8,128)S(1)} collective-permute-done((f32[48,128]{1,0:T(8,128)S(1)}, f32[48,128]{1,0:T(8,128)S(1)}, u32[]{:S(2)}, u32[]{:S(2)}) %collective-permute-start.2) | collective-permute-done | bytes 24608 | tf_op jit(solution)/shard_map/ppermute | solution.py:496
  18.8 0.0 collective-permute-done.1.refs_1_
  18.8 1.1 %interfaces.1 = (f32[5,2,128,128]{3,2,1,0:T(8,128)S(1)}, f32[2,8,128]{2,1,0:T(8,128)S(1)}) custom-call(f32[48,128]{1,0:T(8,128)S(1)} %get-tuple-element.12.refs_0_, f32[48,128]{1,0:T(8,128)S(1)} %collective-permute-done.1.refs_1_, f32[48,128]{1,0:T(8,128)S(1)} %collective-permute-done.2.refs_2_, f32[48,128]{1,0:T(8,128)S(1)} %collective-permute-done.3.refs_3_), custom_call_target="tpu_custom_call" | custom-call | tf_op jit(solution)/shard_map/interfaces/pallas_call | solution.py:497
  19.9 0.1 collective-permute-start.4
  20.0 1.2 %collective-permute-done.4.refs_1_ = f32[2,8,128]{2,1,0:T(8,128)S(1)} collective-permute-done((f32[2,8,128]{2,1,0:T(8,128)S(1)}, f32[2,8,128]{2,1,0:T(8,128)S(1)}, u32[]{:S(2)}, u32[]{:S(2)}) %collective-permute-start.4) | collective-permute-done | bytes 8224 | tf_op jit(solution)/shard_map/ppermute | solution.py:507
  21.2 4.3 %combine.1 = (f32[1,2,128,512]{3,2,1,0:T(8,128)}, f32[1,2,128,512]{3,2,1,0:T(8,128)}) custom-call(f32[2,8,128]{2,1,0:T(8,128)S(1)} %get-tuple-element.13.refs_0_, f32[2,8,128]{2,1,0:T(8,128)S(1)} %collective-permute-done.4.refs_1_, f32[5,2,128,512]{3,2,1,0:T(8,128)S(1)} %get-tuple-element.14.refs_2_, f32[5,2,128,128]{3,2,1,0:T(8,128)S(1)} %get-tuple-element.15.refs_3_), custom_call_target="tpu_custom_call" | custom-call | tf_op jit(solution)/shard_map/combine/pallas_call | solution.py:508
Async XLA Ops:
  2.7 1.4 %collective-permute-start = (f32[3,8,512]{2,1,0:T(8,128)S(1)}, f32[3,8,512]{2,1,0:T(8,128)S(1)}, u32[]{:S(2)}, u32[]{:S(2)}) collective-permute-start(f32[3,8,512]{2,1,0:T(8,128)S(1)} %get-tuple-element.11), channel_id=1, source_target_pairs={{0,4},{4,0},{1,5},{5,1},{2,6},{6,2},{3,7},{7,3},{8,12},{12,8},{9,1... | collective-permute-start | bytes 147464 | tf_op jit(solution)/shard_map/ppermute | solution.py:479
  9.1 6.8 %collective-permute-start.3 = (f32[48,128]{1,0:T(8,128)S(1)}, f32[48,128]{1,0:T(8,128)S(1)}, u32[]{:S(2)}, u32[]{:S(2)}) collective-permute-start(f32[48,128]{1,0:T(8,128)S(1)} %get-tuple-element.12.refs_0_), channel_id=1, source_target_pairs={{0,3},{1,2},{2,1},{3,0},{4,7},{5,6},{6,5},{7,4},{8,11},{9,10},{10,... | collective-permute-start | bytes 73736 | tf_op jit(solution)/shard_map/ppermute | solution.py:496
  14.1 4.7 %collective-permute-start.2 = (f32[48,128]{1,0:T(8,128)S(1)}, f32[48,128]{1,0:T(8,128)S(1)}, u32[]{:S(2)}, u32[]{:S(2)}) collective-permute-start(f32[48,128]{1,0:T(8,128)S(1)} %get-tuple-element.12.refs_0_), channel_id=1, source_target_pairs={{0,2},{1,3},{2,0},{3,1},{4,6},{5,7},{6,4},{7,5},{8,10},{9,11},{10,... | collective-permute-start | bytes 73736 | tf_op jit(solution)/shard_map/ppermute | solution.py:496
  14.1 4.7 %collective-permute-start.1 = (f32[48,128]{1,0:T(8,128)S(1)}, f32[48,128]{1,0:T(8,128)S(1)}, u32[]{:S(2)}, u32[]{:S(2)}) collective-permute-start(f32[48,128]{1,0:T(8,128)S(1)} %get-tuple-element.12.refs_0_), channel_id=1, source_target_pairs={{0,1},{1,0},{2,3},{3,2},{4,5},{5,4},{6,7},{7,6},{8,9},{9,8},{10,11... | collective-permute-start | bytes 73736 | tf_op jit(solution)/shard_map/ppermute | solution.py:496
  19.9 1.2 %collective-permute-start.4 = (f32[2,8,128]{2,1,0:T(8,128)S(1)}, f32[2,8,128]{2,1,0:T(8,128)S(1)}, u32[]{:S(2)}, u32[]{:S(2)}) collective-permute-start(f32[2,8,128]{2,1,0:T(8,128)S(1)} %get-tuple-element.13.refs_0_), channel_id=1, source_target_pairs={{0,4},{4,0},{1,5},{5,1},{2,6},{6,2},{3,7},{7,3},{8,12},{12,8},{9,1... | collective-permute-start | bytes 24584 | tf_op jit(solution)/shard_map/ppermute | solution.py:507

commit v4 on v3

--- a/solution.py
+++ b/solution.py
@@ -71,69 +71,89 @@
     return fast_two_sum(first, first * rest)
 
 
-def spread(x, right):
-    beside = right(x)
-    return x + beside, beside - x
-
-
 def stress(here, below, bulk, mu):
-    (p0, m0), (p1, m1) = here
-    (n0, o0), (n1, o1) = below
-    exx, eyy = n0 - p0, o1 + m1
-    gxy = (o0 + m0) + (n1 - p1)
+    sums, gaps = [], []
+    for (x, right), (y, beside) in zip(here, below):
+        sums.append((x + right, y + beside))
+        gaps.append((right - x, beside - y))
+    exx = sums[0][1] - sums[0][0]
+    eyy = gaps[1][1] + gaps[1][0]
+    gxy = (gaps[0][1] + gaps[0][0]) + (sums[1][1] - sums[1][0])
     mean = bulk * (exx + eyy)
     apart = mu * (exx - eyy)
     return mean + apart, mean - apart, mu * gxy
 
 
-def forces(before, s, left):
+def forces(before, s):
     pxx, pyy, pxy = before
     xx, yy, xy = s
     dxx = pxx - xx
     sxy = pxy + xy
     dxy = pxy - xy
     syy = pyy + yy
-    return left(dxx + sxy) + (dxx - sxy), left(dxy + syy) + (dxy - syy)
-
-
-def apply(k, v, strips, moduli, partial, mask, tiles, right, left):
+    return (dxx + sxy, dxx - sxy), (dxy + syy, dxy - syy)
+
+
+def basis(v, strips, beside, push, moduli, partial, mask, right, left, clear):
+    tiles = v.shape[2]
     groups = tiles // TILE
     sub = iota(strips.shape[2:], 0)
     up = lambda x: pltpu.roll(x, TILE - 1, 0)
     down = lambda x: pltpu.roll(x, 1, 0)
-    tile = lambda c, t: v[k, c, TILE * t : TILE * (t + 1), :]
     modulus = lambda g: (moduli[0, g], moduli[1, g])
 
-    top, bottom = ([strips[s, c] for c in range(2)] for s in range(2))
-    above = [jnp.where(sub == 0, pltpu.roll(top[c], 5, 0), down(tile(c, tiles - 1))) for c in range(2)]
-    below = [jnp.where(sub == TILE - 1, pltpu.roll(bottom[c], 3, 0), up(tile(c, 0))) for c in range(2)]
-
-    for s, old in enumerate((top, bottom)):
-        here = [spread(x, right) for x in old]
-        after = [(up(p), up(m)) for p, m in here]
-        t = stress(here, after, *modulus(groups + 1 + s))
-        new = forces(tuple(down(x) for x in t), t, left)
+    for c in range(2):
+        for t in range(tiles):
+            beside[c, t] = right(v[0, c, t])
+        for s in range(2):
+            beside[c, tiles + s] = right(strips[s, c])
+
+    @pl.loop(0, ITERS)
+    def _(k):
+        last = jnp.maximum(k - 1, 0)
+        tile = lambda c, t: (v[k, c, t], beside[c, t])
+        top, bottom = ([(strips[s, c], beside[c, tiles + s]) for c in range(2)] for s in range(2))
+        for s, here in enumerate((top, bottom)):
+            t = stress(here, [(up(x), up(y)) for x, y in here], *modulus(groups + 1 + s))
+            for c, (x, y) in enumerate(forces(tuple(down(x) for x in t), t)):
+                push[0, c, tiles + s], push[1, c, tiles + s] = (x * mask, y * mask) if s else (x, y)
+        above, below = [], []
         for c in range(2):
-            strips[s, c] = new[c] * mask if s else new[c]
-
-    own = cross = None
-    old = [tile(c, 0) for c in range(2)]
-    here = [spread(x, right) for x in old]
-    before = stress([spread(x, right) for x in above], here, *modulus(groups))
+            join = lambda x, y: jnp.where(sub == 0, pltpu.roll(x, 5, 0), down(y))
+            above.append(tuple(map(join, top[c], tile(c, tiles - 1))))
+            join = lambda x, y: jnp.where(sub == TILE - 1, pltpu.roll(x, 3, 0), up(y))
+            below.append(tuple(map(join, bottom[c], tile(c, 0))))
+
+        own = cross = None
+        here = [tile(c, 0) for c in range(2)]
+        before = stress(above, here, *modulus(groups))
+        for t in range(tiles):
+            after = [tile(c, t + 1) for c in range(2)] if t + 1 < tiles else below
+            s = stress(here, after, *modulus(t // TILE))
+            for c, (x, y) in enumerate(forces(before, s)):
+                push[0, c, t], push[1, c, t] = x, y
+            square = here[0][0] * here[0][0] + here[1][0] * here[1][0]
+            mixed = v[last, 0, t] * here[0][0] + v[last, 1, t] * here[1][0]
+            own = square if own is None else own + square
+            cross = mixed if cross is None else cross + mixed
+            before, here = s, after
+        partial[2 * last + 1] = cross
+        partial[2 * k] = own
+
+        for t in range(tiles + 2):
+            for c in range(2):
+                x, y = push[0, c, t], push[1, c, t]
+                beside[c, t] = clear(x + right(y))
+                if t < tiles:
+                    v[k + 1, c, t] = left(x) + y
+                else:
+                    strips[t - tiles, c] = left(x) + y
+
+    cross = None
     for t in range(tiles):
-        ahead = [tile(c, t + 1) for c in range(2)] if t + 1 < tiles else below
-        after = [spread(x, right) for x in ahead]
-        s = stress(here, after, *modulus(t // TILE))
-        new = forces(before, s, left)
-        square = old[0] * old[0] + old[1] * old[1]
-        mixed = old[0] * new[0] + old[1] * new[1]
-        own = square if own is None else own + square
+        mixed = v[ITERS - 1, 0, t] * v[ITERS, 0, t] + v[ITERS - 1, 1, t] * v[ITERS, 1, t]
         cross = mixed if cross is None else cross + mixed
-        for c in range(2):
-            v[k + 1, c, TILE * t : TILE * (t + 1), :] = new[c]
-        before, here, old = s, after, ahead
-    partial[2 * k] = own
-    partial[2 * k + 1] = cross
+    partial[2 * ITERS - 1] = cross
 
 
 def moment_rows(partial, keep):
@@ -158,29 +178,37 @@
     moduli[c, groups + 2] = jnp.where(low, last, below)
 
 
-def fill_strips(strips, c, halo, first, last):
-    low = iota(halo.shape, 0) < HALO
+def fill_strips(strips, c, halo, v):
+    sub = iota(halo.shape, 0)
+    low = sub < HALO
+    tiles = v.shape[2]
+    first = last = halo
+    for r in range(HALO):
+        first = jnp.where(sub == r, v[0, c, r, 0:1, :], first)
+        last = jnp.where(sub == TILE - 1 - r, v[0, c, tiles - 1 - r, TILE - 1 :, :], last)
     strips[0, c] = pltpu.roll(jnp.where(low, first, halo), HALO, 0)
     strips[1, c] = pltpu.roll(jnp.where(low, halo, last), HALO, 0)
 
 
-def prepare(table, load, material, u, moduli, *rest, gx):
-    *packets, kinds_buffer, lines, sems = rest
+def prepare(table, load, material, v, moduli, *rest, gx):
+    *packets, kinds_buffer, lines, ends, scalars, sems = rest
     rows, cols = material.shape[1:]
     height, width = load.shape[2:]
-    groups = rows // TILE
+    tiles = height // TILE
+    groups = tiles // TILE
     columns = [slice(start, start + LANES) for start in range(0, width, LANES)]
-    ends = [slice(0, TILE), slice(height - TILE, height)]
-    first = pltpu.make_async_copy(material.at[0], kinds_buffer, sems.at[0, 0])
-    first.start()
-    copies = []
-    for i, at in enumerate(ends + [slice(TILE, height - TILE)]):
-        copies.append([])
-        for l, lanes in enumerate(columns):
-            copy = pltpu.make_async_copy(load.at[0, :, at, lanes], u.at[:, l, at, :], sems.at[i + 1, l])
-            copy.start()
-            copies[i].append(copy)
-    first.wait()
+    early = [pltpu.make_async_copy(material.at[0], kinds_buffer, sems.at[2, 0])]
+    for i, at in enumerate((slice(0, TILE), slice(height - TILE, height))):
+        early.append(pltpu.make_async_copy(load.at[0, :, at, :], ends.at[i], sems.at[2, i + 1]))
+    early.append(pltpu.make_async_copy(table, scalars, sems.at[2, 3]))
+    late = []
+    for c in range(2):
+        for s in range(TILE):
+            at = slice(tiles * s, tiles * (s + 1))
+            late.append(pltpu.make_async_copy(load.at[0, c, at, :], v.at[0, c, :, s, :], sems.at[c, s]))
+    for copy in early + late:
+        copy.start()
+    early[0].wait()
     grid = (cols, width)
     expand = iota(grid, 1) // TILE == iota(grid, 0)
     kinds = jnp.dot(
@@ -188,12 +216,13 @@
         expand.astype(F32).astype(jnp.bfloat16),
         preferred_element_type=F32,
     )
+    early[3].wait()
     bulk = jnp.zeros((rows, width), F32)
     shear = bulk
     for k in range(CLASSES):
-        mu = 0.25 * table[1, k]
+        mu = 0.25 * scalars[1, k]
         here = kinds == float(k)
-        bulk = jnp.where(here, 0.25 * table[0, k] + mu, bulk)
+        bulk = jnp.where(here, 0.25 * scalars[0, k] + mu, bulk)
         shear = jnp.where(here, mu, shear)
     for c, values in enumerate((bulk, shear)):
         for l, lanes in enumerate(columns):
@@ -201,13 +230,12 @@
             for g in range(groups):
                 moduli[c, g, :, lanes] = lines[c, l, pl.ds(g, TILE, stride=groups), :]
     place = lax.axis_index("gx")
-    for copy in copies[0] + copies[1]:
+    for copy in early[1:3]:
         copy.wait()
 
     def fill(packet, down):
         for c in range(2):
-            for l, lanes in enumerate(columns):
-                packet[c, :, lanes] = jnp.where(down, u[c, l, ends[1], :], u[c, l, ends[0], :])
+            packet[c] = jnp.where(down, ends[1, c], ends[0, c])
             row = jnp.where(down, moduli[c, groups - 1, TILE - 1 :, :], moduli[c, 0, 0:1, :])
             packet[2, c : c + 1, :] = row
         packet[2, 2:, :] = jnp.zeros((TILE - 2, width), F32)
@@ -217,14 +245,12 @@
     else:
         fill(packets[0], True)
         fill(packets[1], False)
-    for copy in copies[2]:
+    for copy in late:
         copy.wait()
 
 
-def block(u, group_moduli, above, below, v, packet, strips, moduli, partial, *, gx):
-    rows, width = v.shape[2:]
-    tiles = rows // TILE
-    columns = [slice(start, start + LANES) for start in range(0, width, LANES)]
+def block(v_in, group_moduli, above, below, v, packet, strips, beside, push, moduli, partial, *, gx):
+    tiles, _, width = v.shape[2:]
     groups = tiles // TILE
     place = lax.axis_index("gx")
     has_above = place > 0
@@ -237,14 +263,7 @@
         under = jnp.where(has_below, below[c], 0.0)
         over = jnp.where(has_above, above[c], 0.0)
         halo.append(jnp.where(low, under, over))
-        ends = (
-            jnp.concatenate([u[c, l, at, :] for l in range(len(columns))], axis=1)
-            for at in (slice(0, TILE), slice(rows - TILE, rows))
-        )
-        fill_strips(strips, c, halo[c], *ends)
-        for t in range(tiles):
-            for l, lanes in enumerate(columns):
-                v[0, c, TILE * t : TILE * (t + 1), lanes] = u[c, l, pl.ds(t, TILE, stride=tiles), :]
+        fill_strips(strips, c, halo[c], v)
         for g in range(groups):
             moduli[c, g] = group_moduli[c, g]
         under = jnp.where(has_below, below[2, c : c + 1, :], 0.0)
@@ -264,7 +283,7 @@
             slot = 4 * group + part
             for c in range(2):
                 if slot < tiles:
-                    pick = lambda s: v[0, c, TILE * slot : TILE * (slot + 1), s]
+                    pick = lambda s: v[0, c, slot, :, s]
                 elif slot == tiles:
                     pick = lambda s: halo[c][:, s]
                 elif slot <= tiles + groups:
@@ -281,9 +300,7 @@
                 result = jnp.where((lane >= offset + TILE) & (lane < offset + STRIP), final, result)
         packet[TILE * group : TILE * (group + 1), :] = result
 
-    @pl.loop(0, ITERS)
-    def _(k):
-        apply(k, v, strips, moduli, partial, mask, tiles, right, left)
+    basis(v, strips, beside, push, moduli, partial, mask, right, left, lambda x: x)
 
     lane = iota((TILE, width), 1)
     keep = (lane >= HALO) & (lane < width - HALO)
@@ -292,8 +309,8 @@
 
 def interfaces(*refs, gx, gy, sources):
     packets = refs[:gy]
-    v, moments, strips, moduli, partial = refs[gy:]
-    tiles = v.shape[2] // TILE
+    v, moments, strips, beside, push, moduli, partial = refs[gy:]
+    tiles = v.shape[2]
     groups = tiles // TILE
     mine = lax.axis_index("gy")
     has_below = lax.axis_index("gx") < gx - 1
@@ -323,7 +340,7 @@
                     piece = pltpu.roll(pieces[q], shift, 1) if shift else pieces[q]
                     result = jnp.where((lane >= STRIP * q) & (lane < STRIP * (q + 1)), piece, result)
                 if slot < tiles:
-                    v[0, c, TILE * slot : TILE * (slot + 1), :] = result
+                    v[0, c, slot] = result
                 elif slot == tiles:
                     halo[c] = result
                 elif slot <= tiles + groups:
@@ -331,24 +348,17 @@
                 elif slot == tiles + groups + 1:
                     edge[c] = result
     for c in range(2):
-        first = last = halo[c]
-        for r in range(HALO):
-            row = TILE * r
-            first = jnp.where(sub == r, v[0, c, row : row + 1, :], first)
-            row = TILE * (tiles - r) - 1
-            last = jnp.where(sub == TILE - 1 - r, v[0, c, row : row + 1, :], last)
-        fill_strips(strips, c, halo[c], first, last)
+        fill_strips(strips, c, halo[c], v)
         ends = moduli[c, 0, 0:1, :], moduli[c, groups - 1, TILE - 1 :, :]
         fill_moduli(moduli, c, groups, *ends, edge[c])
     mask = jnp.where(sub < HALO, 1.0, jnp.where(has_below, 1.0, 0.0))
     at_end = lane == STRIP * gy - 1
     at_start = lane == 0
-    right = lambda x: jnp.where(at_end, 0.0, pltpu.roll(x, LANES - 1, 1))
+    clear = lambda x: jnp.where(at_end, 0.0, x)
+    right = lambda x: clear(pltpu.roll(x, LANES - 1, 1))
     left = lambda x: jnp.where(at_start, 0.0, pltpu.roll(x, 1, 1))
 
-    @pl.loop(0, ITERS)
-    def _(k):
-        apply(k, v, strips, moduli, partial, mask, tiles, right, left)
+    basis(v, strips, beside, push, moduli, partial, mask, right, left, clear)
 
     column = lane % STRIP
     keep = ((column < HALO) | (column >= STRIP - HALO)) & (lane < STRIP * gy)
@@ -389,16 +399,16 @@
 def combine(*refs, gx):
     gathered = refs[:gx]
     v, strips, *outs, buffer, sems = refs[gx:]
-    rows, width = v.shape[2:]
-    tiles = rows // TILE
+    tiles, _, width = v.shape[2:]
     columns = [slice(start, start + LANES) for start in range(0, width, LANES)]
     total = (gathered[0][0], gathered[0][1])
     for other in gathered[1:]:
         total = ds_add(total, (other[0], other[1]))
-    distance = LANES // 2
-    while distance:
-        total = ds_add(total, tuple(pltpu.roll(x, distance, 1) for x in total))
-        distance //= 2
+    for count, distance in ((8, 16), (16, 1)):
+        terms = [total] + [tuple(pltpu.roll(x, distance * i, 1) for x in total) for i in range(1, count)]
+        while len(terms) > 1:
+            terms = [ds_add(a, b) for a, b in zip(terms[::2], terms[1::2])]
+        total = terms[0]
     weights = coefficients(total)
     mine = lax.axis_index("gy")
     lane = iota((TILE, LANES), 1)
@@ -408,20 +418,20 @@
     for c in range(2):
         for i, w in enumerate(weights):
 
-            @pl.loop(0, tiles, unroll=2)
-            def _(t):
-                at = pl.ds(pl.multiple_of(TILE * t, TILE), TILE)
-                edge = sum(w[k] * strips[k, c, at, :] for k in range(len(w)))
+            weigh = lambda x: sum(a * b for a, b in zip(w, x))
+            edges = [weigh([strips[k, c, t] for k in range(len(w))]) for t in range(tiles)]
+            for t in range(tiles):
                 for l, lanes in enumerate(columns):
-                    value = sum(w[k] * v[k, c, at, lanes] for k in range(len(w)))
+                    value = weigh([v[k, c, t, :, lanes] for k in range(len(w))])
                     if l == 0:
-                        value = jnp.where(lane < HALO, pltpu.roll(edge, to_left, 1), value)
+                        value = jnp.where(lane < HALO, pltpu.roll(edges[t], to_left, 1), value)
                     if l + 1 == len(columns):
-                        value = jnp.where(lane >= LANES - HALO, pltpu.roll(edge, to_right, 1), value)
-                    buffer[i, c, l, pl.ds(t, TILE, stride=tiles), :] = value
-
-            for l, lanes in enumerate(columns):
-                copy = pltpu.make_async_copy(buffer.at[i, c, l], outs[i].at[0, c, :, lanes], sems.at[i, c, l])
+                        value = jnp.where(lane >= LANES - HALO, pltpu.roll(edges[t], to_right, 1), value)
+                    buffer[i, c, t, :, lanes] = value
+
+            for s in range(TILE):
+                at = slice(tiles * s, tiles * (s + 1))
+                copy = pltpu.make_async_copy(buffer.at[i, c, :, s, :], outs[i].at[0, c, at, :], sems.at[i, c, s])
                 copy.start()
                 copies.append(copy)
     for copy in copies:
@@ -446,6 +456,7 @@
     tiles = rows // TILE
     groups = tiles // TILE
     lines = width // LANES
+    dims = (ITERS + 1, 2, tiles, TILE)
     tile_rows, tile_cols = material.shape[1:]
     assert rows == TILE * TILE * groups and width % LANES == 0 and STRIP * gy <= LANES
     vmem = pl.BlockSpec(memory_space=pltpu.VMEM)
@@ -456,20 +467,24 @@
     far = lambda x: pltpu.with_memory_space_constraint(x, pltpu.HBM)
     work = lambda lanes: [
         pltpu.VMEM((2, 2, TILE, lanes), F32),
+        pltpu.VMEM((2, tiles + 2, TILE, lanes), F32),
+        pltpu.VMEM((2, 2, tiles + 2, TILE, lanes), F32),
         pltpu.VMEM((2, groups + 3, TILE, lanes), F32),
         pltpu.VMEM((2 * ITERS, TILE, lanes), F32),
     ]
 
     packets = 1 if gx == 2 else 2
-    u, moduli, *sent = pl.pallas_call(
+    v, moduli, *sent = pl.pallas_call(
         functools.partial(prepare, gx=gx),
-        in_specs=[pl.BlockSpec(memory_space=pltpu.SMEM), hbm, hbm],
+        in_specs=[hbm] * 3,
         out_specs=[vmem] * (2 + packets),
-        out_shape=[shape(2, lines, rows, LANES), shape(2, groups, TILE, width)] + [shape(3, TILE, width)] * packets,
+        out_shape=[shape(*dims, width), shape(2, groups, TILE, width)] + [shape(3, TILE, width)] * packets,
         scratch_shapes=[
             pltpu.VMEM((tile_rows, tile_cols), jnp.int32),
             pltpu.VMEM((2, lines, tile_rows, LANES), F32),
-            pltpu.SemaphoreType.DMA((4, lines)),
+            pltpu.VMEM((2, 2, TILE, width), F32),
+            pltpu.SMEM(lame_table.shape, F32),
+            pltpu.SemaphoreType.DMA((3, TILE)),
         ],
         compiler_params=params,
         name="prepare",
@@ -487,18 +502,19 @@
         functools.partial(block, gx=gx),
         in_specs=[vmem] * 4,
         out_specs=[vmem] * 2,
-        out_shape=[shape(ITERS + 1, 2, rows, width), shape(packet_rows, LANES)],
+        out_shape=[shape(*dims, width), shape(packet_rows, LANES)],
+        input_output_aliases={0: 0},
         scratch_shapes=work(width),
         compiler_params=params,
         name="block",
-    )(pin(u), pin(moduli), pin(above), pin(below))
+    )(pin(v), pin(moduli), pin(above), pin(below))
 
     arrived = [packet] + [lax.ppermute(packet, "gy", route) for route in routes(gy)]
     strips, moments = pl.pallas_call(
         functools.partial(interfaces, gx=gx, gy=gy, sources=source_of(gy)),
         in_specs=[vmem] * gy,
         out_specs=[vmem] * 2,
-        out_shape=[shape(ITERS + 1, 2, rows, LANES), shape(2, 2 * ITERS, LANES)],
+        out_shape=[shape(*dims, LANES), shape(2, 2 * ITERS, LANES)],
         scratch_shapes=work(LANES),
         compiler_params=params,
         name="interfaces",
@@ -510,7 +526,7 @@
         in_specs=[vmem] * (gx + 2),
         out_specs=[hbm] * 2,
         out_shape=[jax.ShapeDtypeStruct(load.shape, F32)] * 2,
-        scratch_shapes=[pltpu.VMEM((2, 2, lines, rows, LANES), F32), pltpu.SemaphoreType.DMA((2, 2, lines))],
+        scratch_shapes=[pltpu.VMEM((2, *dims[1:], width), F32), pltpu.SemaphoreType.DMA((2, 2, TILE))],
         compiler_params=params,
         name="combine",
     )(*map(pin, gathered), pin(v), pin(strips))

time: 25.7 us -> 20.3 us (0.79)
  Pallas kernels: 12.4 us -> 6.98 us
    pallas_call x1, Pallas kernels: 4.94 us -> 2.47 us  [on_device(): pl.pallas_call(functools.partial(block, gx=gx), in_specs=[vmem] * 4, out_...]
    pallas_call x1, Pallas kernels: 4.29 us -> 2.19 us  [on_device(): pl.pallas_call(functools.partial(combine, gx=gx), in_specs=[vmem] * (gx +...]
    pallas_call x1, Pallas kernels: 2.04 us -> 1.27 us  [on_device(): pl.pallas_call(functools.partial(prepare, gx=gx), in_specs=[hbm] * 3, out...]
where the time goes in v4:
time: 20.3 us; the launch traced here: 20 us
  Pallas kernels  6.98 us (34%)
  starting transfers between devices  6.27 us (31%)
  waiting for transfers between devices  6.12 us (30%)
  between operations  0.66 us (3%)
    ppermute x3, starting transfers between devices, on_device(): lax.ppermute(packet, 'gy', route)  5.64 us
    ppermute x3, waiting for transfers between devices, on_device(): lax.ppermute(packet, 'gy', route)  4.08 us
    pallas_call x1, Pallas kernels, on_device(): pl.pallas_call(functools.partial(block, gx=gx), in_specs=[vmem] * 4, out_...  2.47 us
    pallas_call x1, Pallas kernels, on_device(): pl.pallas_call(functools.partial(combine, gx=gx), in_specs=[vmem] * (gx +...  2.19 us
    pallas_call x1, Pallas kernels, on_device(): pl.pallas_call(functools.partial(prepare, gx=gx), in_specs=[hbm] * 3, out...  1.27 us
    ppermute x1, waiting for transfers between devices, on_device(): lax.ppermute(moments, 'gx', route)  1.16 us
    pallas_call x1, Pallas kernels, on_device(): pl.pallas_call(functools.partial(interfaces, gx=gx, gy=gy, sources=source...  1.05 us
    ppermute x1, waiting for transfers between devices, on_device(): above = below = lax.ppermute(sent[0], 'gx', [(0, 1), (1, 0)])  0.88 us
  transfers between devices with their start and end apart: 5, of which 4 were waited for; matrix products, arithmetic and copies ran while one was open for 0% of the time, Pallas kernels for 0%

profile of v4, /device:TPU:0, one launch (start us, length us, event | category | flops | bytes accessed | tf_op | source)
XLA Modules:
  0.0 20.0 jit_solution(15405486734580134984)
XLA Ops:
  0.6 1.3 %prepare.1 = (f32[5,2,16,8,512]{4,3,2,1,0:T(8,128)S(1)}, f32[2,2,8,512]{3,2,1,0:T(8,128)S(1)}, f32[3,8,512]{2,1,0:T(8,128)S(1)}) custom-call(f32[2,8]{1,0:T(2,128)} %table.1, f32[1,2,128,512]{3,2,1,0:T(8,128)} %load.1, s32[1,16,64]{2,1,0:T(8,128)} %material.1), custom_call_target="tpu_custom_call" | custom-call | tf_op jit(solution)/shard_map/prepare/pallas_call | solution.py:477
  1.9 0.6 %collective-permute-start = (f32[3,8,512]{2,1,0:T(8,128)S(1)}, f32[3,8,512]{2,1,0:T(8,128)S(1)}, u32[]{:S(2)}, u32[]{:S(2)}) collective-permute-start(f32[3,8,512]{2,1,0:T(8,128)S(1)} %get-tuple-element.11), channel_id=1, source_target_pairs={{0,4},{4,0},{1,5},{5,1},{2,6},{6,2},{3,7},{7,3},{8,12},{12,8},{9,1... | collective-permute-start | bytes 147464 | tf_op jit(solution)/shard_map/ppermute | solution.py:494
  2.5 0.9 %collective-permute-done.above.below = f32[3,8,512]{2,1,0:T(8,128)S(1)} collective-permute-done((f32[3,8,512]{2,1,0:T(8,128)S(1)}, f32[3,8,512]{2,1,0:T(8,128)S(1)}, u32[]{:S(2)}, u32[]{:S(2)}) %collective-permute-start) | collective-permute-done | bytes 49184 | tf_op jit(solution)/shard_map/ppermute | solution.py:494
  3.3 2.5 %block.1 = (f32[5,2,16,8,512]{4,3,2,1,0:T(8,128)S(1)}, f32[48,128]{1,0:T(8,128)S(1)}) custom-call(f32[5,2,16,8,512]{4,3,2,1,0:T(8,128)S(1)} %get-tuple-element.9.v_in, f32[2,2,8,512]{3,2,1,0:T(8,128)S(1)} %get-tuple-element.10.group_moduli, f32[3,8,512]{2,1,0:T(8,128)S(1)} %collective-permute-done.above.below, ...), custom_call_target="tpu_custom_call", output_to_operand_aliasing={{0}: (0, {})} | custom-call | tf_op jit(solution)/shard_map/block/pallas_call | solution.py:501
  5.8 5.0 %collective-permute-start.3 = (f32[48,128]{1,0:T(8,128)S(1)}, f32[48,128]{1,0:T(8,128)S(1)}, u32[]{:S(2)}, u32[]{:S(2)}) collective-permute-start(f32[48,128]{1,0:T(8,128)S(1)} %get-tuple-element.12.refs_0_), channel_id=1, source_target_pairs={{0,3},{1,2},{2,1},{3,0},{4,7},{5,6},{6,5},{7,4},{8,11},{9,10},{10,... | collective-permute-start | bytes 73736 | tf_op jit(solution)/shard_map/ppermute | solution.py:512
  10.8 0.0 collective-permute-start.2
  10.8 0.6 %collective-permute-start.1 = (f32[48,128]{1,0:T(8,128)S(1)}, f32[48,128]{1,0:T(8,128)S(1)}, u32[]{:S(2)}, u32[]{:S(2)}) collective-permute-start(f32[48,128]{1,0:T(8,128)S(1)} %get-tuple-element.12.refs_0_), channel_id=1, source_target_pairs={{0,1},{1,0},{2,3},{3,2},{4,5},{5,4},{6,7},{7,6},{8,9},{9,8},{10,11... | collective-permute-start | bytes 73736 | tf_op jit(solution)/shard_map/ppermute | solution.py:512
  11.5 1.2 %collective-permute-done.3.refs_3_ = f32[48,128]{1,0:T(8,128)S(1)} collective-permute-done((f32[48,128]{1,0:T(8,128)S(1)}, f32[48,128]{1,0:T(8,128)S(1)}, u32[]{:S(2)}, u32[]{:S(2)}) %collective-permute-start.3) | collective-permute-done | bytes 24608 | tf_op jit(solution)/shard_map/ppermute | solution.py:512
  12.6 2.9 %collective-permute-done.2.refs_2_ = f32[48,128]{1,0:T(8,128)S(1)} collective-permute-done((f32[48,128]{1,0:T(8,128)S(1)}, f32[48,128]{1,0:T(8,128)S(1)}, u32[]{:S(2)}, u32[]{:S(2)}) %collective-permute-start.2) | collective-permute-done | bytes 24608 | tf_op jit(solution)/shard_map/ppermute | solution.py:512
  15.6 0.0 collective-permute-done.1.refs_1_
  15.6 1.1 %interfaces.1 = (f32[5,2,16,8,128]{4,3,2,1,0:T(8,128)S(1)}, f32[2,8,128]{2,1,0:T(8,128)S(1)}) custom-call(f32[48,128]{1,0:T(8,128)S(1)} %get-tuple-element.12.refs_0_, f32[48,128]{1,0:T(8,128)S(1)} %collective-permute-done.1.refs_1_, f32[48,128]{1,0:T(8,128)S(1)} %collective-permute-done.2.refs_2_, f32[48,128]{1,0:T(8,128)S(1)} %collective-permute-done.3.refs_3_), custom_call_target="tpu_custom_call" | custom-call | tf_op jit(solution)/shard_map/interfaces/pallas_call | solution.py:513
  16.6 0.1 collective-permute-start.4
  16.7 1.2 %collective-permute-done.4.refs_1_ = f32[2,8,128]{2,1,0:T(8,128)S(1)} collective-permute-done((f32[2,8,128]{2,1,0:T(8,128)S(1)}, f32[2,8,128]{2,1,0:T(8,128)S(1)}, u32[]{:S(2)}, u32[]{:S(2)}) %collective-permute-start.4) | collective-permute-done | bytes 8224 | tf_op jit(solution)/shard_map/ppermute | solution.py:523
  17.9 2.2 %combine.1 = (f32[1,2,128,512]{3,2,1,0:T(8,128)}, f32[1,2,128,512]{3,2,1,0:T(8,128)}) custom-call(f32[2,8,128]{2,1,0:T(8,128)S(1)} %get-tuple-element.13.refs_0_, f32[2,8,128]{2,1,0:T(8,128)S(1)} %collective-permute-done.4.refs_1_, f32[5,2,16,8,512]{4,3,2,1,0:T(8,128)S(1)} %get-tuple-element.14.refs_2_, f32[5,2,16,8,128]{4,3,2,1,0:T(8,128)S(1)} %get-tuple-element.15.refs_3_), custom_call_target="tpu_custom_call" | custom-call | tf_op jit(solution)/shard_map/combine/pallas_call | solution.py:524
Async XLA Ops:
  1.9 1.4 %collective-permute-start = (f32[3,8,512]{2,1,0:T(8,128)S(1)}, f32[3,8,512]{2,1,0:T(8,128)S(1)}, u32[]{:S(2)}, u32[]{:S(2)}) collective-permute-start(f32[3,8,512]{2,1,0:T(8,128)S(1)} %get-tuple-element.11), channel_id=1, source_target_pairs={{0,4},{4,0},{1,5},{5,1},{2,6},{6,2},{3,7},{7,3},{8,12},{12,8},{9,1... | collective-permute-start | bytes 147464 | tf_op jit(solution)/shard_map/ppermute | solution.py:494
  5.8 6.8 %collective-permute-start.3 = (f32[48,128]{1,0:T(8,128)S(1)}, f32[48,128]{1,0:T(8,128)S(1)}, u32[]{:S(2)}, u32[]{:S(2)}) collective-permute-start(f32[48,128]{1,0:T(8,128)S(1)} %get-tuple-element.12.refs_0_), channel_id=1, source_target_pairs={{0,3},{1,2},{2,1},{3,0},{4,7},{5,6},{6,5},{7,4},{8,11},{9,10},{10,... | collective-permute-start | bytes 73736 | tf_op jit(solution)/shard_map/ppermute | solution.py:512
  10.8 4.7 %collective-permute-start.2 = (f32[48,128]{1,0:T(8,128)S(1)}, f32[48,128]{1,0:T(8,128)S(1)}, u32[]{:S(2)}, u32[]{:S(2)}) collective-permute-start(f32[48,128]{1,0:T(8,128)S(1)} %get-tuple-element.12.refs_0_), channel_id=1, source_target_pairs={{0,2},{1,3},{2,0},{3,1},{4,6},{5,7},{6,4},{7,5},{8,10},{9,11},{10,... | collective-permute-start | bytes 73736 | tf_op jit(solution)/shard_map/ppermute | solution.py:512
  10.8 4.7 %collective-permute-start.1 = (f32[48,128]{1,0:T(8,128)S(1)}, f32[48,128]{1,0:T(8,128)S(1)}, u32[]{:S(2)}, u32[]{:S(2)}) collective-permute-start(f32[48,128]{1,0:T(8,128)S(1)} %get-tuple-element.12.refs_0_), channel_id=1, source_target_pairs={{0,1},{1,0},{2,3},{3,2},{4,5},{5,4},{6,7},{7,6},{8,9},{9,8},{10,11... | collective-permute-start | bytes 73736 | tf_op jit(solution)/shard_map/ppermute | solution.py:512
  16.6 1.2 %collective-permute-start.4 = (f32[2,8,128]{2,1,0:T(8,128)S(1)}, f32[2,8,128]{2,1,0:T(8,128)S(1)}, u32[]{:S(2)}, u32[]{:S(2)}) collective-permute-start(f32[2,8,128]{2,1,0:T(8,128)S(1)} %get-tuple-element.13.refs_0_), channel_id=1, source_target_pairs={{0,4},{4,0},{1,5},{5,1},{2,6},{6,2},{3,7},{7,3},{8,12},{12,8},{9,1... | collective-permute-start | bytes 24584 | tf_op jit(solution)/shard_map/ppermute | solution.py:523

commit v5 on v4

--- a/solution.py
+++ b/solution.py
@@ -81,7 +81,7 @@
     gxy = (gaps[0][1] + gaps[0][0]) + (sums[1][1] - sums[1][0])
     mean = bulk * (exx + eyy)
     apart = mu * (exx - eyy)
-    return mean + apart, mean - apart, mu * gxy
+    return (mean + apart, mean - apart, mu * gxy), (exx, eyy, gxy)
 
 
 def forces(before, s):
@@ -94,52 +94,68 @@
     return (dxx + sxy, dxx - sxy), (dxy + syy, dxy - syy)
 
 
+def total(terms):
+    return functools.reduce(lambda a, b: a + b, terms)
+
+
+def dot(x, y):
+    return total([a * b for a, b in zip(x, y)])
+
+
 def basis(v, strips, beside, push, moduli, partial, mask, right, left, clear):
     tiles = v.shape[2]
     groups = tiles // TILE
-    sub = iota(strips.shape[2:], 0)
     up = lambda x: pltpu.roll(x, TILE - 1, 0)
     down = lambda x: pltpu.roll(x, 1, 0)
-    modulus = lambda g: (moduli[0, g], moduli[1, g])
-
-    for c in range(2):
-        for t in range(tiles):
-            beside[c, t] = right(v[0, c, t])
+
+    for c in range(2):
         for s in range(2):
             beside[c, tiles + s] = right(strips[s, c])
 
-    @pl.loop(0, ITERS)
-    def _(k):
-        last = jnp.maximum(k - 1, 0)
-        tile = lambda c, t: (v[k, c, t], beside[c, t])
-        top, bottom = ([(strips[s, c], beside[c, tiles + s]) for c in range(2)] for s in range(2))
-        for s, here in enumerate((top, bottom)):
-            t = stress(here, [(up(x), up(y)) for x, y in here], *modulus(groups + 1 + s))
+    def cells(k, final, at):
+        modulus = lambda g: (moduli[0, g, :, at], moduli[1, g, :, at])
+        tile = lambda c, t: (v[k, c, t, :, at], beside[c, t, :, at])
+        ends = [[(strips[s, c, :, at], beside[c, tiles + s, :, at]) for c in range(2)] for s in range(2)]
+        sub = iota(ends[0][0][0].shape, 0)
+        for s, here in enumerate([] if final else ends):
+            t, _ = stress(here, [(up(x), up(y)) for x, y in here], *modulus(groups + 1 + s))
             for c, (x, y) in enumerate(forces(tuple(down(x) for x in t), t)):
-                push[0, c, tiles + s], push[1, c, tiles + s] = (x * mask, y * mask) if s else (x, y)
+                push[0, c, tiles + s, :, at] = x * mask[:, at] if s else x
+                push[1, c, tiles + s, :, at] = y * mask[:, at] if s else y
         above, below = [], []
         for c in range(2):
             join = lambda x, y: jnp.where(sub == 0, pltpu.roll(x, 5, 0), down(y))
-            above.append(tuple(map(join, top[c], tile(c, tiles - 1))))
+            above.append(tuple(map(join, ends[0][c], tile(c, tiles - 1))))
             join = lambda x, y: jnp.where(sub == TILE - 1, pltpu.roll(x, 3, 0), up(y))
-            below.append(tuple(map(join, bottom[c], tile(c, 0))))
-
-        own = cross = None
+            below.append(tuple(map(join, ends[1][c], tile(c, 0))))
+
+        own, cross, energy = [], [], []
+        grow = lambda sums, x: sums.append(sums.pop() + x if sums else x)
+        last = max(k - 1, 0) if final else jnp.maximum(k - 1, 0)
         here = [tile(c, 0) for c in range(2)]
-        before = stress(above, here, *modulus(groups))
+        before, _ = stress(above, here, *modulus(groups))
         for t in range(tiles):
             after = [tile(c, t + 1) for c in range(2)] if t + 1 < tiles else below
-            s = stress(here, after, *modulus(t // TILE))
+            s, strain = stress(here, after, *modulus(t // TILE))
             for c, (x, y) in enumerate(forces(before, s)):
-                push[0, c, t], push[1, c, t] = x, y
-            square = here[0][0] * here[0][0] + here[1][0] * here[1][0]
-            mixed = v[last, 0, t] * here[0][0] + v[last, 1, t] * here[1][0]
-            own = square if own is None else own + square
-            cross = mixed if cross is None else cross + mixed
+                push[0, c, t, :, at], push[1, c, t, :, at] = x, y
+            values = [x for x, _ in here]
+            grow(own, dot(values, values))
+            grow(cross, dot([v[last, c, t, :, at] for c in range(2)], values))
+            if final:
+                grow(energy, dot(strain, s))
             before, here = s, after
-        partial[2 * last + 1] = cross
-        partial[2 * k] = own
-
+        partial[2 * last + 1, :, at] = cross[0]
+        partial[2 * k, :, at] = own[0]
+        if final:
+            partial[2 * k + 1, :, at] = energy[0]
+
+    columns = [slice(start, start + LANES) for start in range(0, v.shape[4], LANES)]
+
+    @pl.loop(0, ITERS - 1)
+    def _(k):
+        for at in columns:
+            cells(k, False, at)
         for t in range(tiles + 2):
             for c in range(2):
                 x, y = push[0, c, t], push[1, c, t]
@@ -149,11 +165,17 @@
                 else:
                     strips[t - tiles, c] = left(x) + y
 
-    cross = None
+    for at in columns:
+        cells(ITERS - 1, True, at)
+
+
+def finish(v_in, push, v, *, masked):
+    tiles = v.shape[2]
+    at_start = iota(v.shape[3:], 1) == 0
     for t in range(tiles):
-        mixed = v[ITERS - 1, 0, t] * v[ITERS, 0, t] + v[ITERS - 1, 1, t] * v[ITERS, 1, t]
-        cross = mixed if cross is None else cross + mixed
-    partial[2 * ITERS - 1] = cross
+        for c in range(2):
+            x = pltpu.roll(push[0, c, t], 1, 1)
+            v[ITERS, c, t] = (jnp.where(at_start, 0.0, x) if masked else x) + push[1, c, t]
 
 
 def moment_rows(partial, keep):
@@ -249,7 +271,33 @@
         copy.wait()
 
 
-def block(v_in, group_moduli, above, below, v, packet, strips, beside, push, moduli, partial, *, gx):
+def pack(packet, lines, pick, width):
+    lane = iota((TILE, LANES), 1)
+    for line in lines:
+        result = jnp.zeros((TILE, LANES), F32)
+        for part in range(4):
+            for c in range(2):
+                offset = 32 * part + STRIP * c
+                first = pick(4 * line + part, c, slice(0, LANES))
+                if first is None:
+                    continue
+                first = pltpu.roll(first, offset, 1) if offset else first
+                final = pick(4 * line + part, c, slice(width - LANES, width))
+                final = pltpu.roll(final, (offset + STRIP) % LANES, 1)
+                result = jnp.where((lane >= offset) & (lane < offset + TILE), first, result)
+                result = jnp.where((lane >= offset + TILE) & (lane < offset + STRIP), final, result)
+        packet[TILE * line : TILE * (line + 1), :] = result
+
+
+def early(v, packet, beside):
+    tiles, _, width = v.shape[2:]
+    pack(packet, range(tiles // 4), lambda slot, c, at: v[0, c, slot, :, at], width)
+    for c in range(2):
+        for t in range(tiles):
+            beside[c, t] = pltpu.roll(v[0, c, t], width - 1, 1)
+
+
+def block(v_in, packet_in, beside_in, group_moduli, above, below, v, packet, beside, push, strips, moduli, partial, *, gx):
     tiles, _, width = v.shape[2:]
     groups = tiles // TILE
     place = lax.axis_index("gx")
@@ -275,41 +323,24 @@
     right = lambda x: pltpu.roll(x, width - 1, 1)
     left = lambda x: pltpu.roll(x, 1, 1)
 
-    lane = iota((TILE, LANES), 1)
-    packet_rows = packet.shape[0]
-    for group in range(packet_rows // TILE - 1):
-        result = jnp.zeros((TILE, LANES), F32)
-        for part in range(4):
-            slot = 4 * group + part
-            for c in range(2):
-                if slot < tiles:
-                    pick = lambda s: v[0, c, slot, :, s]
-                elif slot == tiles:
-                    pick = lambda s: halo[c][:, s]
-                elif slot <= tiles + groups:
-                    pick = lambda s: moduli[c, slot - tiles - 1, :, s]
-                elif slot == tiles + groups + 1:
-                    pick = lambda s: edge[c][:, s]
-                else:
-                    continue
-                offset = 32 * part + STRIP * c
-                first = pick(slice(0, LANES))
-                first = pltpu.roll(first, offset, 1) if offset else first
-                final = pltpu.roll(pick(slice(width - LANES, width)), (offset + STRIP) % LANES, 1)
-                result = jnp.where((lane >= offset) & (lane < offset + TILE), first, result)
-                result = jnp.where((lane >= offset + TILE) & (lane < offset + STRIP), final, result)
-        packet[TILE * group : TILE * (group + 1), :] = result
-
+    def pick(slot, c, at):
+        if slot == tiles:
+            return halo[c][:, at]
+        if slot <= tiles + groups:
+            return moduli[c, slot - tiles - 1, :, at]
+        return edge[c][:, at] if slot == tiles + groups + 1 else None
+
+    pack(packet, range(tiles // 4, packet.shape[0] // TILE - 1), pick, width)
     basis(v, strips, beside, push, moduli, partial, mask, right, left, lambda x: x)
 
     lane = iota((TILE, width), 1)
     keep = (lane >= HALO) & (lane < width - HALO)
-    packet[packet_rows - TILE :, :] = moment_rows(partial, keep)
+    packet[packet.shape[0] - TILE :, :] = moment_rows(partial, keep)
 
 
 def interfaces(*refs, gx, gy, sources):
     packets = refs[:gy]
-    v, moments, strips, beside, push, moduli, partial = refs[gy:]
+    v, moments, push, strips, beside, moduli, partial = refs[gy:]
     tiles = v.shape[2]
     groups = tiles // TILE
     mine = lax.axis_index("gy")
@@ -358,6 +389,9 @@
     right = lambda x: clear(pltpu.roll(x, LANES - 1, 1))
     left = lambda x: jnp.where(at_start, 0.0, pltpu.roll(x, 1, 1))
 
+    for c in range(2):
+        for t in range(tiles):
+            beside[c, t] = right(v[0, c, t])
     basis(v, strips, beside, push, moduli, partial, mask, right, left, clear)
 
     column = lane % STRIP
@@ -401,15 +435,15 @@
     v, strips, *outs, buffer, sems = refs[gx:]
     tiles, _, width = v.shape[2:]
     columns = [slice(start, start + LANES) for start in range(0, width, LANES)]
-    total = (gathered[0][0], gathered[0][1])
+    moments = (gathered[0][0], gathered[0][1])
     for other in gathered[1:]:
-        total = ds_add(total, (other[0], other[1]))
+        moments = ds_add(moments, (other[0], other[1]))
     for count, distance in ((8, 16), (16, 1)):
-        terms = [total] + [tuple(pltpu.roll(x, distance * i, 1) for x in total) for i in range(1, count)]
+        terms = [moments] + [tuple(pltpu.roll(x, distance * i, 1) for x in moments) for i in range(1, count)]
         while len(terms) > 1:
             terms = [ds_add(a, b) for a, b in zip(terms[::2], terms[1::2])]
-        total = terms[0]
-    weights = coefficients(total)
+        moments = terms[0]
+    weights = coefficients(moments)
     mine = lax.axis_index("gy")
     lane = iota((TILE, LANES), 1)
     to_left = lax.rem(LANES - STRIP * mine, LANES)
@@ -418,7 +452,7 @@
     for c in range(2):
         for i, w in enumerate(weights):
 
-            weigh = lambda x: sum(a * b for a, b in zip(w, x))
+            weigh = lambda x: dot(w, x)
             edges = [weigh([strips[k, c, t] for k in range(len(w))]) for t in range(tiles)]
             for t in range(tiles):
                 for l, lanes in enumerate(columns):
@@ -465,13 +499,24 @@
     params = pltpu.CompilerParams(vmem_limit_bytes=VMEM_LIMIT)
     pin = lambda x: pltpu.with_memory_space_constraint(x, pltpu.VMEM)
     far = lambda x: pltpu.with_memory_space_constraint(x, pltpu.HBM)
+    strips_of = lambda lanes: pltpu.VMEM((2, 2, TILE, lanes), F32)
+    beside_of = lambda lanes: pltpu.VMEM((2, tiles + 2, TILE, lanes), F32)
+    push_of = lambda lanes: pltpu.VMEM((2, 2, tiles + 2, TILE, lanes), F32)
     work = lambda lanes: [
-        pltpu.VMEM((2, 2, TILE, lanes), F32),
-        pltpu.VMEM((2, tiles + 2, TILE, lanes), F32),
-        pltpu.VMEM((2, 2, tiles + 2, TILE, lanes), F32),
         pltpu.VMEM((2, groups + 3, TILE, lanes), F32),
         pltpu.VMEM((2 * ITERS, TILE, lanes), F32),
     ]
+
+    def finished(v, push, masked):
+        return pl.pallas_call(
+            functools.partial(finish, masked=masked),
+            in_specs=[vmem] * 2,
+            out_specs=vmem,
+            out_shape=pltpu.VMEM(v.shape, F32),
+            input_output_aliases={0: 0},
+            compiler_params=params,
+            name="finish",
+        )(pin(v), pin(push))
 
     packets = 1 if gx == 2 else 2
     v, moduli, *sent = pl.pallas_call(
@@ -498,29 +543,39 @@
 
     slots = tiles + groups + 2
     packet_rows = TILE * (-(-slots // 4) + 1)
-    v, packet = pl.pallas_call(
+    packet, beside = pl.pallas_call(
+        early,
+        in_specs=[vmem],
+        out_specs=[vmem] * 2,
+        out_shape=[shape(packet_rows, LANES), beside_of(width)],
+        compiler_params=params,
+        name="early",
+    )(pin(v))
+    v, packet, _, push = pl.pallas_call(
         functools.partial(block, gx=gx),
-        in_specs=[vmem] * 4,
-        out_specs=[vmem] * 2,
-        out_shape=[shape(*dims, width), shape(packet_rows, LANES)],
-        input_output_aliases={0: 0},
-        scratch_shapes=work(width),
+        in_specs=[vmem] * 6,
+        out_specs=[vmem] * 4,
+        out_shape=[shape(*dims, width), shape(packet_rows, LANES), beside_of(width), push_of(width)],
+        scratch_shapes=[strips_of(width)] + work(width),
+        input_output_aliases={0: 0, 1: 1, 2: 2},
         compiler_params=params,
         name="block",
-    )(pin(v), pin(moduli), pin(above), pin(below))
+    )(*map(pin, (v, packet, beside, moduli, above, below)))
 
     arrived = [packet] + [lax.ppermute(packet, "gy", route) for route in routes(gy)]
-    strips, moments = pl.pallas_call(
+    v = finished(v, push, False)
+    strips, moments, push = pl.pallas_call(
         functools.partial(interfaces, gx=gx, gy=gy, sources=source_of(gy)),
         in_specs=[vmem] * gy,
-        out_specs=[vmem] * 2,
-        out_shape=[shape(*dims, LANES), shape(2, 2 * ITERS, LANES)],
-        scratch_shapes=work(LANES),
+        out_specs=[vmem] * 3,
+        out_shape=[shape(*dims, LANES), shape(2, 2 * ITERS, LANES), push_of(LANES)],
+        scratch_shapes=[strips_of(LANES), beside_of(LANES)] + work(LANES),
         compiler_params=params,
         name="interfaces",
     )(*map(pin, arrived))
 
     gathered = [moments] + [lax.ppermute(moments, "gx", route) for route in routes(gx)]
+    strips = finished(strips, push, True)
     return pl.pallas_call(
         functools.partial(combine, gx=gx),
         in_specs=[vmem] * (gx + 2),

time: 20.3 us -> 19.8 us (0.975)
  waiting for transfers between devices: 6.12 us -> 5.55 us
    ppermute x1, waiting for transfers between devices: 1.16 us -> 0.85 us  [on_device(): lax.ppermute(moments, 'gx', route)]
    ppermute x1, waiting for transfers between devices: 0.88 us -> 0.62 us  [on_device(): above = below = lax.ppermute(sent[0], 'gx', [(0, 1), (1, 0)])]
    pallas_call x1 -> x4, Pallas kernels: 2.47 us -> 2.71 us  [the longest x1 2.15 us: on_device(): pl.pallas_call(functools.partial(block, gx=gx), in_specs=[vmem] * 6, out_...]
  transfers between devices with their start and end apart: 5 -> 5, of which waited for: 4 -> 4; matrix products, arithmetic and copies ran while one was open for 0% -> 0% of each run, Pallas kernels for 0% -> 3%
where the time goes in v5:
time: 19.8 us; the launch traced here: 19.6 us
  Pallas kernels  7.12 us (36%)
  starting transfers between devices  6.27 us (32%)
  waiting for transfers between devices  5.55 us (28%)
  between operations  0.69 us (3%)
    ppermute x3, starting transfers between devices, on_device(): lax.ppermute(packet, 'gy', route)  5.64 us
    ppermute x3, waiting for transfers between devices, on_device(): lax.ppermute(packet, 'gy', route)  4.08 us
    pallas_call x1, Pallas kernels, on_device(): pl.pallas_call(functools.partial(combine, gx=gx), in_specs=[vmem] * (gx +...  2.2 us
    pallas_call x1, Pallas kernels, on_device(): pl.pallas_call(functools.partial(block, gx=gx), in_specs=[vmem] * 6, out_...  2.15 us
    pallas_call x1, Pallas kernels, on_device(): pl.pallas_call(functools.partial(prepare, gx=gx), in_specs=[hbm] * 3, out...  1.27 us
    pallas_call x1, Pallas kernels, on_device(): pl.pallas_call(functools.partial(interfaces, gx=gx, gy=gy, sources=source...  0.94 us
    ppermute x1, waiting for transfers between devices, on_device(): lax.ppermute(moments, 'gx', route)  0.85 us
    ppermute x1, waiting for transfers between devices, on_device(): above = below = lax.ppermute(sent[0], 'gx', [(0, 1), (1, 0)])  0.62 us
  transfers between devices with their start and end apart: 5, of which 4 were waited for; matrix products, arithmetic and copies ran while one was open for 0% of the time, Pallas kernels for 3%

profile of v5, /device:TPU:0, one launch (start us, length us, event | category | flops | bytes accessed | tf_op | source)
XLA Modules:
  0.0 19.6 jit_solution(16939655454355064666)
XLA Ops:
  0.6 1.3 %prepare.1 = (f32[5,2,16,8,512]{4,3,2,1,0:T(8,128)S(1)}, f32[2,2,8,512]{3,2,1,0:T(8,128)S(1)}, f32[3,8,512]{2,1,0:T(8,128)S(1)}) custom-call(f32[2,8]{1,0:T(2,128)} %table.1, f32[1,2,128,512]{3,2,1,0:T(8,128)} %load.1, s32[1,16,64]{2,1,0:T(8,128)} %material.1), custom_call_target="tpu_custom_call" | custom-call | tf_op jit(solution)/shard_map/prepare/pallas_call | solution.py:522
  1.9 0.6 %collective-permute-start = (f32[3,8,512]{2,1,0:T(8,128)S(1)}, f32[3,8,512]{2,1,0:T(8,128)S(1)}, u32[]{:S(2)}, u32[]{:S(2)}) collective-permute-start(f32[3,8,512]{2,1,0:T(8,128)S(1)} %get-tuple-element.17), channel_id=1, source_target_pairs={{0,4},{4,0},{1,5},{5,1},{2,6},{6,2},{3,7},{7,3},{8,12},{12,8},{9,1... | collective-permute-start | bytes 147464 | tf_op jit(solution)/shard_map/ppermute | solution.py:539
  2.5 0.3 %early.1 = (f32[48,128]{1,0:T(8,128)S(1)}, f32[2,18,8,512]{3,2,1,0:T(8,128)S(1)}) custom-call(f32[5,2,16,8,512]{4,3,2,1,0:T(8,128)S(1)} %get-tuple-element.13.v.v_in), custom_call_target="tpu_custom_call" | custom-call | tf_op jit(solution)/shard_map/early/pallas_call | solution.py:546
  2.7 0.6 %collective-permute-done.above.below = f32[3,8,512]{2,1,0:T(8,128)S(1)} collective-permute-done((f32[3,8,512]{2,1,0:T(8,128)S(1)}, f32[3,8,512]{2,1,0:T(8,128)S(1)}, u32[]{:S(2)}, u32[]{:S(2)}) %collective-permute-start) | collective-permute-done | bytes 49184 | tf_op jit(solution)/shard_map/ppermute | solution.py:539
  3.3 2.2 %block.1 = (f32[5,2,16,8,512]{4,3,2,1,0:T(8,128)S(1)}, f32[48,128]{1,0:T(8,128)S(1)}, f32[2,18,8,512]{3,2,1,0:T(8,128)S(1)}, f32[2,2,18,8,512]{4,3,2,1,0:T(8,128)S(1)}) custom-call(f32[5,2,16,8,512]{4,3,2,1,0:T(8,128)S(1)} %get-tuple-element.13.v.v_in, ...), custom_call_target="tpu_custom_call", output_to_operand_aliasing={{0}: (0, {}), {1}: (1, {}), {2}: (2, {})} | custom-call | tf_op jit(solution)/shard_map/block/pallas_call | solution.py:554
  5.5 5.0 %collective-permute-start.3 = (f32[48,128]{1,0:T(8,128)S(1)}, f32[48,128]{1,0:T(8,128)S(1)}, u32[]{:S(2)}, u32[]{:S(2)}) collective-permute-start(f32[48,128]{1,0:T(8,128)S(1)} %get-tuple-element.18.refs_0_), channel_id=1, source_target_pairs={{0,3},{1,2},{2,1},{3,0},{4,7},{5,6},{6,5},{7,4},{8,11},{9,10},{10,... | collective-permute-start | bytes 73736 | tf_op jit(solution)/shard_map/ppermute | solution.py:565
  10.5 0.0 collective-permute-start.2
  10.5 0.6 %collective-permute-start.1 = (f32[48,128]{1,0:T(8,128)S(1)}, f32[48,128]{1,0:T(8,128)S(1)}, u32[]{:S(2)}, u32[]{:S(2)}) collective-permute-start(f32[48,128]{1,0:T(8,128)S(1)} %get-tuple-element.18.refs_0_), channel_id=1, source_target_pairs={{0,1},{1,0},{2,3},{3,2},{4,5},{5,4},{6,7},{7,6},{8,9},{9,8},{10,11... | collective-permute-start | bytes 73736 | tf_op jit(solution)/shard_map/ppermute | solution.py:565
  11.1 1.2 %collective-permute-done.3.refs_3_ = f32[48,128]{1,0:T(8,128)S(1)} collective-permute-done((f32[48,128]{1,0:T(8,128)S(1)}, f32[48,128]{1,0:T(8,128)S(1)}, u32[]{:S(2)}, u32[]{:S(2)}) %collective-permute-start.3) | collective-permute-done | bytes 24608 | tf_op jit(solution)/shard_map/ppermute | solution.py:565
  12.3 2.9 %collective-permute-done.2.refs_2_ = f32[48,128]{1,0:T(8,128)S(1)} collective-permute-done((f32[48,128]{1,0:T(8,128)S(1)}, f32[48,128]{1,0:T(8,128)S(1)}, u32[]{:S(2)}, u32[]{:S(2)}) %collective-permute-start.2) | collective-permute-done | bytes 24608 | tf_op jit(solution)/shard_map/ppermute | solution.py:565
  15.2 0.0 collective-permute-done.1.refs_1_
  15.2 0.9 %interfaces.1 = (f32[5,2,16,8,128]{4,3,2,1,0:T(8,128)S(1)}, f32[2,8,128]{2,1,0:T(8,128)S(1)}, f32[2,2,18,8,128]{4,3,2,1,0:T(8,128)S(1)}) custom-call(f32[48,128]{1,0:T(8,128)S(1)} %get-tuple-element.18.refs_0_, f32[48,128]{1,0:T(8,128)S(1)} %collective-permute-done.1.refs_1_, f32[48,128]{1,0:T(8,128)S(1)} %collective-permute-done.2.refs_2_, ...), custom_call_target="tpu_custom_call" | custom-call | tf_op jit(solution)/shard_map/interfaces/pallas_call | solution.py:567
  16.2 0.1 collective-permute-start.4
  16.3 0.2 %finish.2.refs_2_ = f32[5,2,16,8,512]{4,3,2,1,0:T(8,128)S(1)} custom-call(f32[5,2,16,8,512]{4,3,2,1,0:T(8,128)S(1)} %get-tuple-element.20.v_in, f32[2,2,18,8,512]{4,3,2,1,0:T(8,128)S(1)} %get-tuple-element.21.push), custom_call_target="tpu_custom_call", output_to_operand_aliasing={{}: (0, {})} | custom-call | tf_op jit(solution)/shard_map/finish/pallas_call | solution.py:511
  16.5 0.1 finish.3.refs_3_
  16.6 0.8 %collective-permute-done.4.refs_1_ = f32[2,8,128]{2,1,0:T(8,128)S(1)} collective-permute-done((f32[2,8,128]{2,1,0:T(8,128)S(1)}, f32[2,8,128]{2,1,0:T(8,128)S(1)}, u32[]{:S(2)}, u32[]{:S(2)}) %collective-permute-start.4) | collective-permute-done | bytes 8224 | tf_op jit(solution)/shard_map/ppermute | solution.py:577
  17.4 2.2 %combine.1 = (f32[1,2,128,512]{3,2,1,0:T(8,128)}, f32[1,2,128,512]{3,2,1,0:T(8,128)}) custom-call(f32[2,8,128]{2,1,0:T(8,128)S(1)} %get-tuple-element.19.refs_0_, f32[2,8,128]{2,1,0:T(8,128)S(1)} %collective-permute-done.4.refs_1_, f32[5,2,16,8,512]{4,3,2,1,0:T(8,128)S(1)} %finish.2.refs_2_, f32[5,2,16,8,128]{4,3,2,1,0:T(8,128)S(1)} %finish.3.refs_3_), custom_call_target="tpu_custom_call" | custom-call | tf_op jit(solution)/shard_map/combine/pallas_call | solution.py:579
Async XLA Ops:
  1.9 1.4 %collective-permute-start = (f32[3,8,512]{2,1,0:T(8,128)S(1)}, f32[3,8,512]{2,1,0:T(8,128)S(1)}, u32[]{:S(2)}, u32[]{:S(2)}) collective-permute-start(f32[3,8,512]{2,1,0:T(8,128)S(1)} %get-tuple-element.17), channel_id=1, source_target_pairs={{0,4},{4,0},{1,5},{5,1},{2,6},{6,2},{3,7},{7,3},{8,12},{12,8},{9,1... | collective-permute-start | bytes 147464 | tf_op jit(solution)/shard_map/ppermute | solution.py:539
  5.5 6.8 %collective-permute-start.3 = (f32[48,128]{1,0:T(8,128)S(1)}, f32[48,128]{1,0:T(8,128)S(1)}, u32[]{:S(2)}, u32[]{:S(2)}) collective-permute-start(f32[48,128]{1,0:T(8,128)S(1)} %get-tuple-element.18.refs_0_), channel_id=1, source_target_pairs={{0,3},{1,2},{2,1},{3,0},{4,7},{5,6},{6,5},{7,4},{8,11},{9,10},{10,... | collective-permute-start | bytes 73736 | tf_op jit(solution)/shard_map/ppermute | solution.py:565
  10.5 4.7 %collective-permute-start.2 = (f32[48,128]{1,0:T(8,128)S(1)}, f32[48,128]{1,0:T(8,128)S(1)}, u32[]{:S(2)}, u32[]{:S(2)}) collective-permute-start(f32[48,128]{1,0:T(8,128)S(1)} %get-tuple-element.18.refs_0_), channel_id=1, source_target_pairs={{0,2},{1,3},{2,0},{3,1},{4,6},{5,7},{6,4},{7,5},{8,10},{9,11},{10,... | collective-permute-start | bytes 73736 | tf_op jit(solution)/shard_map/ppermute | solution.py:565
  10.5 4.7 %collective-permute-start.1 = (f32[48,128]{1,0:T(8,128)S(1)}, f32[48,128]{1,0:T(8,128)S(1)}, u32[]{:S(2)}, u32[]{:S(2)}) collective-permute-start(f32[48,128]{1,0:T(8,128)S(1)} %get-tuple-element.18.refs_0_), channel_id=1, source_target_pairs={{0,1},{1,0},{2,3},{3,2},{4,5},{5,4},{6,7},{7,6},{8,9},{9,8},{10,11... | collective-permute-start | bytes 73736 | tf_op jit(solution)/shard_map/ppermute | solution.py:565
  16.2 1.2 %collective-permute-start.4 = (f32[2,8,128]{2,1,0:T(8,128)S(1)}, f32[2,8,128]{2,1,0:T(8,128)S(1)}, u32[]{:S(2)}, u32[]{:S(2)}) collective-permute-start(f32[2,8,128]{2,1,0:T(8,128)S(1)} %get-tuple-element.19.refs_0_), channel_id=1, source_target_pairs={{0,4},{4,0},{1,5},{5,1},{2,6},{6,2},{3,7},{7,3},{8,12},{12,8},{9,1... | collective-permute-start | bytes 24584 | tf_op jit(solution)/shard_map/ppermute | solution.py:577

commit v6 on v5

--- a/solution.py
+++ b/solution.py
@@ -169,13 +169,37 @@
         cells(ITERS - 1, True, at)
 
 
-def finish(v_in, push, v, *, masked):
-    tiles = v.shape[2]
-    at_start = iota(v.shape[3:], 1) == 0
-    for t in range(tiles):
+def finish(v_in, push, v):
+    for t in range(v.shape[2]):
         for c in range(2):
-            x = pltpu.roll(push[0, c, t], 1, 1)
-            v[ITERS, c, t] = (jnp.where(at_start, 0.0, x) if masked else x) + push[1, c, t]
+            v[ITERS, c, t] = pltpu.roll(push[0, c, t], 1, 1) + push[1, c, t]
+
+
+def merge(v_in, strips, strips_push, v, ends):
+    tiles, _, width = v.shape[2:]
+    mine = lax.axis_index("gy")
+    to_left = lax.rem(LANES - STRIP * mine, LANES)
+    to_right = lax.rem(2 * LANES - STRIP - STRIP * mine, LANES)
+    lane = iota((TILE, LANES), 1)
+
+    @pl.loop(0, tiles, unroll=4)
+    def _(t):
+        for c in range(2):
+            x = pltpu.roll(strips_push[0, c, t], 1, 1)
+            last = jnp.where(lane == 0, 0.0, x) + strips_push[1, c, t]
+            for k in range(ITERS):
+                edge = strips[k + 1, c, t] if k + 1 < ITERS else last
+                ends[0, k, c, t] = pltpu.roll(edge, to_left, 1)
+                ends[1, k, c, t] = pltpu.roll(edge, to_right, 1)
+
+    @pl.loop(0, tiles, unroll=4)
+    def _(t):
+        for k in range(ITERS):
+            for c in range(2):
+                for side, start in enumerate((0, width - LANES)):
+                    at = slice(start, start + LANES)
+                    inside = lane < LANES - HALO if side else lane >= HALO
+                    v[k + 1, c, t, :, at] = jnp.where(inside, v[k + 1, c, t, :, at], ends[side, k, c, t])
 
 
 def moment_rows(partial, keep):
@@ -340,7 +364,7 @@
 
 def interfaces(*refs, gx, gy, sources):
     packets = refs[:gy]
-    v, moments, push, strips, beside, moduli, partial = refs[gy:]
+    _, v, moments, push, _, strips, beside, moduli, partial = refs[gy:]
     tiles = v.shape[2]
     groups = tiles // TILE
     mine = lax.axis_index("gy")
@@ -432,7 +456,7 @@
 
 def combine(*refs, gx):
     gathered = refs[:gx]
-    v, strips, *outs, buffer, sems = refs[gx:]
+    v, *outs, buffer, sems = refs[gx:]
     tiles, _, width = v.shape[2:]
     columns = [slice(start, start + LANES) for start in range(0, width, LANES)]
     moments = (gathered[0][0], gathered[0][1])
@@ -444,30 +468,17 @@
             terms = [ds_add(a, b) for a, b in zip(terms[::2], terms[1::2])]
         moments = terms[0]
     weights = coefficients(moments)
-    mine = lax.axis_index("gy")
-    lane = iota((TILE, LANES), 1)
-    to_left = lax.rem(LANES - STRIP * mine, LANES)
-    to_right = lax.rem(2 * LANES - STRIP - STRIP * mine, LANES)
     copies = []
-    for c in range(2):
-        for i, w in enumerate(weights):
-
-            weigh = lambda x: dot(w, x)
-            edges = [weigh([strips[k, c, t] for k in range(len(w))]) for t in range(tiles)]
+    for i, w in enumerate(weights):
+        for c in range(2):
             for t in range(tiles):
-                for l, lanes in enumerate(columns):
-                    value = weigh([v[k, c, t, :, lanes] for k in range(len(w))])
-                    if l == 0:
-                        value = jnp.where(lane < HALO, pltpu.roll(edges[t], to_left, 1), value)
-                    if l + 1 == len(columns):
-                        value = jnp.where(lane >= LANES - HALO, pltpu.roll(edges[t], to_right, 1), value)
-                    buffer[i, c, t, :, lanes] = value
-
-            for s in range(TILE):
-                at = slice(tiles * s, tiles * (s + 1))
-                copy = pltpu.make_async_copy(buffer.at[i, c, :, s, :], outs[i].at[0, c, at, :], sems.at[i, c, s])
-                copy.start()
-                copies.append(copy)
+                for lanes in columns:
+                    buffer[i, c, t, :, lanes] = dot(w, [v[k, c, t, :, lanes] for k in range(len(w))])
+        for s in range(TILE):
+            at = slice(tiles * s, tiles * (s + 1))
+            copy = pltpu.make_async_copy(buffer.at[i, :, :, s, :], outs[i].at[0, :, at, :], sems.at[i, 0, s])
+            copy.start()
+            copies.append(copy)
     for copy in copies:
         copy.wait()
 
@@ -507,17 +518,6 @@
         pltpu.VMEM((2 * ITERS, TILE, lanes), F32),
     ]
 
-    def finished(v, push, masked):
-        return pl.pallas_call(
-            functools.partial(finish, masked=masked),
-            in_specs=[vmem] * 2,
-            out_specs=vmem,
-            out_shape=pltpu.VMEM(v.shape, F32),
-            input_output_aliases={0: 0},
-            compiler_params=params,
-            name="finish",
-        )(pin(v), pin(push))
-
     packets = 1 if gx == 2 else 2
     v, moduli, *sent = pl.pallas_call(
         functools.partial(prepare, gx=gx),
@@ -563,28 +563,46 @@
     )(*map(pin, (v, packet, beside, moduli, above, below)))
 
     arrived = [packet] + [lax.ppermute(packet, "gy", route) for route in routes(gy)]
-    v = finished(v, push, False)
-    strips, moments, push = pl.pallas_call(
+    v = pl.pallas_call(
+        finish,
+        in_specs=[vmem] * 2,
+        out_specs=vmem,
+        out_shape=pltpu.VMEM(v.shape, F32),
+        input_output_aliases={0: 0},
+        compiler_params=params,
+        name="finish",
+    )(pin(v), pin(push))
+    strips, moments, strips_push, v = pl.pallas_call(
         functools.partial(interfaces, gx=gx, gy=gy, sources=source_of(gy)),
-        in_specs=[vmem] * gy,
-        out_specs=[vmem] * 3,
-        out_shape=[shape(*dims, LANES), shape(2, 2 * ITERS, LANES), push_of(LANES)],
+        in_specs=[vmem] * (gy + 1),
+        out_specs=[vmem] * 4,
+        out_shape=[shape(*dims, LANES), shape(2, 2 * ITERS, LANES), push_of(LANES), shape(*dims, width)],
+        input_output_aliases={gy: 3},
         scratch_shapes=[strips_of(LANES), beside_of(LANES)] + work(LANES),
         compiler_params=params,
         name="interfaces",
-    )(*map(pin, arrived))
+    )(*map(pin, arrived), pin(v))
 
     gathered = [moments] + [lax.ppermute(moments, "gx", route) for route in routes(gx)]
-    strips = finished(strips, push, True)
+    v = pl.pallas_call(
+        merge,
+        in_specs=[vmem] * 3,
+        out_specs=vmem,
+        out_shape=pltpu.VMEM(v.shape, F32),
+        scratch_shapes=[pltpu.VMEM((2, ITERS, 2, tiles, TILE, LANES), F32)],
+        input_output_aliases={0: 0},
+        compiler_params=params,
+        name="merge",
+    )(*map(pin, (v, strips, strips_push)))
     return pl.pallas_call(
         functools.partial(combine, gx=gx),
-        in_specs=[vmem] * (gx + 2),
+        in_specs=[vmem] * (gx + 1),
         out_specs=[hbm] * 2,
         out_shape=[jax.ShapeDtypeStruct(load.shape, F32)] * 2,
         scratch_shapes=[pltpu.VMEM((2, *dims[1:], width), F32), pltpu.SemaphoreType.DMA((2, 2, TILE))],
         compiler_params=params,
         name="combine",
-    )(*map(pin, gathered), pin(v), pin(strips))
+    )(*map(pin, gathered), pin(v))
 
 
 def solution(mesh):

time: 19.8 us -> 19.6 us (0.990)
  waiting for transfers between devices: 5.55 us -> 4.83 us
  Pallas kernels: 7.12 us -> 7.6 us
    pallas_call x2, Pallas kernels: 0.3 us -> 1.02 us  [the longest x1 0.82 us: on_device(): pl.pallas_call(merge, in_specs=[vmem] * 3, out_specs=vmem, out_shape=pltp...]
    ppermute x1, waiting for transfers between devices: 0.85 us -> 0.33 us  [on_device(): lax.ppermute(moments, 'gx', route)]
    pallas_call x1, Pallas kernels: 2.2 us -> 1.95 us  [on_device(): pl.pallas_call(functools.partial(combine, gx=gx), in_specs=[vmem] * (gx +...]
    ppermute x3, waiting for transfers between devices: 4.08 us -> 3.88 us  [on_device(): lax.ppermute(packet, 'gy', route)]
  transfers between devices with their start and end apart: 5 -> 5, of which waited for: 4 -> 4; matrix products, arithmetic and copies ran while one was open for 0% -> 0% of each run, Pallas kernels for 3% -> 7%
where the time goes in v6:
time: 19.6 us; the launch traced here: 19.4 us
  Pallas kernels  7.6 us (39%)
  starting transfers between devices  6.27 us (32%)
  waiting for transfers between devices  4.83 us (25%)
  between operations  0.69 us (4%)
    ppermute x3, starting transfers between devices, on_device(): lax.ppermute(packet, 'gy', route)  5.64 us
    ppermute x3, waiting for transfers between devices, on_device(): lax.ppermute(packet, 'gy', route)  3.88 us
    pallas_call x1, Pallas kernels, on_device(): pl.pallas_call(functools.partial(block, gx=gx), in_specs=[vmem] * 6, out_...  2.15 us
    pallas_call x1, Pallas kernels, on_device(): pl.pallas_call(functools.partial(combine, gx=gx), in_specs=[vmem] * (gx +...  1.95 us
    pallas_call x1, Pallas kernels, on_device(): pl.pallas_call(functools.partial(prepare, gx=gx), in_specs=[hbm] * 3, out...  1.27 us
    pallas_call x1, Pallas kernels, on_device(): pl.pallas_call(functools.partial(interfaces, gx=gx, gy=gy, sources=source...  0.96 us
    pallas_call x1, Pallas kernels, on_device(): pl.pallas_call(merge, in_specs=[vmem] * 3, out_specs=vmem, out_shape=pltp...  0.82 us
    ppermute x1, waiting for transfers between devices, on_device(): above = below = lax.ppermute(sent[0], 'gx', [(0, 1), (1, 0)])  0.62 us
  transfers between devices with their start and end apart: 5, of which 4 were waited for; matrix products, arithmetic and copies ran while one was open for 0% of the time, Pallas kernels for 7%

profile of v6, /device:TPU:0, one launch (start us, length us, event | category | flops | bytes accessed | tf_op | source)
XLA Modules:
  0.0 19.4 jit_solution(16100226594864359052)
XLA Ops:
  0.6 1.3 %prepare.1 = (f32[5,2,16,8,512]{4,3,2,1,0:T(8,128)S(1)}, f32[2,2,8,512]{3,2,1,0:T(8,128)S(1)}, f32[3,8,512]{2,1,0:T(8,128)S(1)}) custom-call(f32[2,8]{1,0:T(2,128)} %table.1, f32[1,2,128,512]{3,2,1,0:T(8,128)} %load.1, s32[1,16,64]{2,1,0:T(8,128)} %material.1), custom_call_target="tpu_custom_call" | custom-call | tf_op jit(solution)/shard_map/prepare/pallas_call | solution.py:522
  1.9 0.6 %collective-permute-start = (f32[3,8,512]{2,1,0:T(8,128)S(1)}, f32[3,8,512]{2,1,0:T(8,128)S(1)}, u32[]{:S(2)}, u32[]{:S(2)}) collective-permute-start(f32[3,8,512]{2,1,0:T(8,128)S(1)} %get-tuple-element.18), channel_id=1, source_target_pairs={{0,4},{4,0},{1,5},{5,1},{2,6},{6,2},{3,7},{7,3},{8,12},{12,8},{9,1... | collective-permute-start | bytes 147464 | tf_op jit(solution)/shard_map/ppermute | solution.py:539
  2.5 0.3 %early.1 = (f32[48,128]{1,0:T(8,128)S(1)}, f32[2,18,8,512]{3,2,1,0:T(8,128)S(1)}) custom-call(f32[5,2,16,8,512]{4,3,2,1,0:T(8,128)S(1)} %get-tuple-element.14.v.v_in), custom_call_target="tpu_custom_call" | custom-call | tf_op jit(solution)/shard_map/early/pallas_call | solution.py:546
  2.7 0.6 %collective-permute-done.above.below = f32[3,8,512]{2,1,0:T(8,128)S(1)} collective-permute-done((f32[3,8,512]{2,1,0:T(8,128)S(1)}, f32[3,8,512]{2,1,0:T(8,128)S(1)}, u32[]{:S(2)}, u32[]{:S(2)}) %collective-permute-start) | collective-permute-done | bytes 49184 | tf_op jit(solution)/shard_map/ppermute | solution.py:539
  3.3 2.2 %block.1 = (f32[5,2,16,8,512]{4,3,2,1,0:T(8,128)S(1)}, f32[48,128]{1,0:T(8,128)S(1)}, f32[2,18,8,512]{3,2,1,0:T(8,128)S(1)}, f32[2,2,18,8,512]{4,3,2,1,0:T(8,128)S(1)}) custom-call(f32[5,2,16,8,512]{4,3,2,1,0:T(8,128)S(1)} %get-tuple-element.14.v.v_in, ...), custom_call_target="tpu_custom_call", output_to_operand_aliasing={{0}: (0, {}), {1}: (1, {}), {2}: (2, {})} | custom-call | tf_op jit(solution)/shard_map/block/pallas_call | solution.py:554
  5.5 5.0 %collective-permute-start.3 = (f32[48,128]{1,0:T(8,128)S(1)}, f32[48,128]{1,0:T(8,128)S(1)}, u32[]{:S(2)}, u32[]{:S(2)}) collective-permute-start(f32[48,128]{1,0:T(8,128)S(1)} %get-tuple-element.19.refs_0_), channel_id=1, source_target_pairs={{0,3},{1,2},{2,1},{3,0},{4,7},{5,6},{6,5},{7,4},{8,11},{9,10},{10,... | collective-permute-start | bytes 73736 | tf_op jit(solution)/shard_map/ppermute | solution.py:565
  10.5 0.0 collective-permute-start.2
  10.5 0.6 %collective-permute-start.1 = (f32[48,128]{1,0:T(8,128)S(1)}, f32[48,128]{1,0:T(8,128)S(1)}, u32[]{:S(2)}, u32[]{:S(2)}) collective-permute-start(f32[48,128]{1,0:T(8,128)S(1)} %get-tuple-element.19.refs_0_), channel_id=1, source_target_pairs={{0,1},{1,0},{2,3},{3,2},{4,5},{5,4},{6,7},{7,6},{8,9},{9,8},{10,11... | collective-permute-start | bytes 73736 | tf_op jit(solution)/shard_map/ppermute | solution.py:565
  11.1 0.2 %finish.1.refs_4_ = f32[5,2,16,8,512]{4,3,2,1,0:T(8,128)S(1)} custom-call(f32[5,2,16,8,512]{4,3,2,1,0:T(8,128)S(1)} %get-tuple-element.20.v_in, f32[2,2,18,8,512]{4,3,2,1,0:T(8,128)S(1)} %get-tuple-element.21.push), custom_call_target="tpu_custom_call", output_to_operand_aliasing={{}: (0, {})} | custom-call | tf_op jit(solution)/shard_map/finish/pallas_call | solution.py:566
  11.4 1.0 %collective-permute-done.3.refs_3_ = f32[48,128]{1,0:T(8,128)S(1)} collective-permute-done((f32[48,128]{1,0:T(8,128)S(1)}, f32[48,128]{1,0:T(8,128)S(1)}, u32[]{:S(2)}, u32[]{:S(2)}) %collective-permute-start.3) | collective-permute-done | bytes 24608 | tf_op jit(solution)/shard_map/ppermute | solution.py:565
  12.3 2.9 %collective-permute-done.2.refs_2_ = f32[48,128]{1,0:T(8,128)S(1)} collective-permute-done((f32[48,128]{1,0:T(8,128)S(1)}, f32[48,128]{1,0:T(8,128)S(1)}, u32[]{:S(2)}, u32[]{:S(2)}) %collective-permute-start.2) | collective-permute-done | bytes 24608 | tf_op jit(solution)/shard_map/ppermute | solution.py:565
  15.2 0.0 collective-permute-done.1.refs_1_
  15.2 1.0 %interfaces.1 = (f32[5,2,16,8,128]{4,3,2,1,0:T(8,128)S(1)}, f32[2,8,128]{2,1,0:T(8,128)S(1)}, f32[2,2,18,8,128]{4,3,2,1,0:T(8,128)S(1)}, f32[5,2,16,8,512]{4,3,2,1,0:T(8,128)S(1)}) custom-call(f32[48,128]{1,0:T(8,128)S(1)} %get-tuple-element.19.refs_0_, f32[48,128]{1,0:T(8,128)S(1)} %collective-permute-done.1.refs_1_, ...), custom_call_target="tpu_custom_call", output_to_operand_aliasing={{3}: (4, {})} | custom-call | tf_op jit(solution)/shard_map/interfaces/pallas_call | solution.py:575
  16.2 0.1 collective-permute-start.4
  16.3 0.8 %merge.1.refs_2_ = f32[5,2,16,8,512]{4,3,2,1,0:T(8,128)S(1)} custom-call(f32[5,2,16,8,512]{4,3,2,1,0:T(8,128)S(1)} %get-tuple-element.23.v_in, f32[5,2,16,8,128]{4,3,2,1,0:T(8,128)S(1)} %get-tuple-element.24.strips, f32[2,2,18,8,128]{4,3,2,1,0:T(8,128)S(1)} %get-tuple-element.25.strips_push), custom_call_target="tpu_custom_call", output_to_operand_aliasing={{}: (0, {})} | custom-call | tf_op jit(solution)/shard_map/merge/pallas_call | solution.py:587
  17.1 0.3 %collective-permute-done.4.refs_1_ = f32[2,8,128]{2,1,0:T(8,128)S(1)} collective-permute-done((f32[2,8,128]{2,1,0:T(8,128)S(1)}, f32[2,8,128]{2,1,0:T(8,128)S(1)}, u32[]{:S(2)}, u32[]{:S(2)}) %collective-permute-start.4) | collective-permute-done | bytes 8224 | tf_op jit(solution)/shard_map/ppermute | solution.py:586
  17.4 2.0 %combine.1 = (f32[1,2,128,512]{3,2,1,0:T(8,128)}, f32[1,2,128,512]{3,2,1,0:T(8,128)}) custom-call(f32[2,8,128]{2,1,0:T(8,128)S(1)} %get-tuple-element.22.refs_0_, f32[2,8,128]{2,1,0:T(8,128)S(1)} %collective-permute-done.4.refs_1_, f32[5,2,16,8,512]{4,3,2,1,0:T(8,128)S(1)} %merge.1.refs_2_), custom_call_target="tpu_custom_call" | custom-call | tf_op jit(solution)/shard_map/combine/pallas_call | solution.py:597
Async XLA Ops:
  1.9 1.4 %collective-permute-start = (f32[3,8,512]{2,1,0:T(8,128)S(1)}, f32[3,8,512]{2,1,0:T(8,128)S(1)}, u32[]{:S(2)}, u32[]{:S(2)}) collective-permute-start(f32[3,8,512]{2,1,0:T(8,128)S(1)} %get-tuple-element.18), channel_id=1, source_target_pairs={{0,4},{4,0},{1,5},{5,1},{2,6},{6,2},{3,7},{7,3},{8,12},{12,8},{9,1... | collective-permute-start | bytes 147464 | tf_op jit(solution)/shard_map/ppermute | solution.py:539
  5.5 6.8 %collective-permute-start.3 = (f32[48,128]{1,0:T(8,128)S(1)}, f32[48,128]{1,0:T(8,128)S(1)}, u32[]{:S(2)}, u32[]{:S(2)}) collective-permute-start(f32[48,128]{1,0:T(8,128)S(1)} %get-tuple-element.19.refs_0_), channel_id=1, source_target_pairs={{0,3},{1,2},{2,1},{3,0},{4,7},{5,6},{6,5},{7,4},{8,11},{9,10},{10,... | collective-permute-start | bytes 73736 | tf_op jit(solution)/shard_map/ppermute | solution.py:565
  10.5 4.7 %collective-permute-start.2 = (f32[48,128]{1,0:T(8,128)S(1)}, f32[48,128]{1,0:T(8,128)S(1)}, u32[]{:S(2)}, u32[]{:S(2)}) collective-permute-start(f32[48,128]{1,0:T(8,128)S(1)} %get-tuple-element.19.refs_0_), channel_id=1, source_target_pairs={{0,2},{1,3},{2,0},{3,1},{4,6},{5,7},{6,4},{7,5},{8,10},{9,11},{10,... | collective-permute-start | bytes 73736 | tf_op jit(solution)/shard_map/ppermute | solution.py:565
  10.5 4.7 %collective-permute-start.1 = (f32[48,128]{1,0:T(8,128)S(1)}, f32[48,128]{1,0:T(8,128)S(1)}, u32[]{:S(2)}, u32[]{:S(2)}) collective-permute-start(f32[48,128]{1,0:T(8,128)S(1)} %get-tuple-element.19.refs_0_), channel_id=1, source_target_pairs={{0,1},{1,0},{2,3},{3,2},{4,5},{5,4},{6,7},{7,6},{8,9},{9,8},{10,11... | collective-permute-start | bytes 73736 | tf_op jit(solution)/shard_map/ppermute | solution.py:565
  16.2 1.2 %collective-permute-start.4 = (f32[2,8,128]{2,1,0:T(8,128)S(1)}, f32[2,8,128]{2,1,0:T(8,128)S(1)}, u32[]{:S(2)}, u32[]{:S(2)}) collective-permute-start(f32[2,8,128]{2,1,0:T(8,128)S(1)} %get-tuple-element.22.refs_0_), channel_id=1, source_target_pairs={{0,4},{4,0},{1,5},{5,1},{2,6},{6,2},{3,7},{7,3},{8,12},{12,8},{9,1... | collective-permute-start | bytes 24584 | tf_op jit(solution)/shard_map/ppermute | solution.py:586

commit v7 on v6

--- a/solution.py
+++ b/solution.py
@@ -102,71 +102,93 @@
     return total([a * b for a, b in zip(x, y)])
 
 
-def basis(v, strips, beside, push, moduli, partial, mask, right, left, clear):
+def up(x):
+    return pltpu.roll(x, TILE - 1, 0)
+
+
+def down(x):
+    return pltpu.roll(x, 1, 0)
+
+
+def lane_tiles(width):
+    return [slice(start, start + LANES) for start in range(0, width, LANES)]
+
+
+def inner_cells(k, v, beside, push, moduli, partial, at, above=None, below=None):
     tiles = v.shape[2]
     groups = tiles // TILE
-    up = lambda x: pltpu.roll(x, TILE - 1, 0)
-    down = lambda x: pltpu.roll(x, 1, 0)
-
+    tile = lambda c, t: (v[k, c, t, :, at], beside[c, t, :, at])
+    modulus = lambda g: (moduli[0, g, :, at], moduli[1, g, :, at])
+    here = [tile(c, 0) for c in range(2)]
+    before = stress(above, here, *modulus(groups))[0] if above else None
+    own = energy = None
+    for t in range(tiles):
+        values = [x for x, _ in here]
+        square = dot(values, values)
+        own = square if own is None else own + square
+        after = [tile(c, t + 1) for c in range(2)] if t + 1 < tiles else below
+        if after:
+            s, strain = stress(here, after, *modulus(t // TILE))
+            work = dot(strain, s)
+            energy = work if energy is None else energy + work
+            if before:
+                for c, (x, y) in enumerate(forces(before, s)):
+                    push[0, c, t, :, at], push[1, c, t, :, at] = x, y
+            before, here = s, after
+    partial[2 * k, :, at] = own
+    partial[2 * k + 1, :, at] = energy
+
+
+def outer_tiles(k, v, strips, beside, at):
+    tiles = v.shape[2]
+    sub = iota((TILE, LANES), 0)
+    above, below = [], []
+    for c in range(2):
+        first = v[k, c, 0, :, at], beside[c, 0, :, at]
+        last = v[k, c, tiles - 1, :, at], beside[c, tiles - 1, :, at]
+        top, bottom = ((strips[s, c, :, at], beside[c, tiles + s, :, at]) for s in range(2))
+        above.append(tuple(jnp.where(sub == 0, pltpu.roll(x, 5, 0), down(y)) for x, y in zip(top, last)))
+        below.append(tuple(jnp.where(sub == TILE - 1, pltpu.roll(x, 3, 0), up(y)) for x, y in zip(bottom, first)))
+    return above, below
+
+
+def strip_cells(strips, beside, push, moduli, mask, at):
+    tiles = push.shape[2] - 2
+    groups = tiles // TILE
+    for s in range(2):
+        here = [(strips[s, c, :, at], beside[c, tiles + s, :, at]) for c in range(2)]
+        modulus = [moduli[c, groups + 1 + s, :, at] for c in range(2)]
+        t, _ = stress(here, [(up(x), up(y)) for x, y in here], *modulus)
+        for c, (x, y) in enumerate(forces(tuple(down(x) for x in t), t)):
+            push[0, c, tiles + s, :, at] = x * mask[:, at] if s else x
+            push[1, c, tiles + s, :, at] = y * mask[:, at] if s else y
+
+
+def strip_neighbours(strips, beside, right):
+    tiles = beside.shape[1] - 2
     for c in range(2):
         for s in range(2):
             beside[c, tiles + s] = right(strips[s, c])
 
-    def cells(k, final, at):
-        modulus = lambda g: (moduli[0, g, :, at], moduli[1, g, :, at])
-        tile = lambda c, t: (v[k, c, t, :, at], beside[c, t, :, at])
-        ends = [[(strips[s, c, :, at], beside[c, tiles + s, :, at]) for c in range(2)] for s in range(2)]
-        sub = iota(ends[0][0][0].shape, 0)
-        for s, here in enumerate([] if final else ends):
-            t, _ = stress(here, [(up(x), up(y)) for x, y in here], *modulus(groups + 1 + s))
-            for c, (x, y) in enumerate(forces(tuple(down(x) for x in t), t)):
-                push[0, c, tiles + s, :, at] = x * mask[:, at] if s else x
-                push[1, c, tiles + s, :, at] = y * mask[:, at] if s else y
-        above, below = [], []
+
+def advance(k, v, strips, beside, push, right, left, clear):
+    tiles = v.shape[2]
+    for t in range(tiles + 2):
         for c in range(2):
-            join = lambda x, y: jnp.where(sub == 0, pltpu.roll(x, 5, 0), down(y))
-            above.append(tuple(map(join, ends[0][c], tile(c, tiles - 1))))
-            join = lambda x, y: jnp.where(sub == TILE - 1, pltpu.roll(x, 3, 0), up(y))
-            below.append(tuple(map(join, ends[1][c], tile(c, 0))))
-
-        own, cross, energy = [], [], []
-        grow = lambda sums, x: sums.append(sums.pop() + x if sums else x)
-        last = max(k - 1, 0) if final else jnp.maximum(k - 1, 0)
-        here = [tile(c, 0) for c in range(2)]
-        before, _ = stress(above, here, *modulus(groups))
-        for t in range(tiles):
-            after = [tile(c, t + 1) for c in range(2)] if t + 1 < tiles else below
-            s, strain = stress(here, after, *modulus(t // TILE))
-            for c, (x, y) in enumerate(forces(before, s)):
-                push[0, c, t, :, at], push[1, c, t, :, at] = x, y
-            values = [x for x, _ in here]
-            grow(own, dot(values, values))
-            grow(cross, dot([v[last, c, t, :, at] for c in range(2)], values))
-            if final:
-                grow(energy, dot(strain, s))
-            before, here = s, after
-        partial[2 * last + 1, :, at] = cross[0]
-        partial[2 * k, :, at] = own[0]
-        if final:
-            partial[2 * k + 1, :, at] = energy[0]
-
-    columns = [slice(start, start + LANES) for start in range(0, v.shape[4], LANES)]
-
-    @pl.loop(0, ITERS - 1)
-    def _(k):
-        for at in columns:
-            cells(k, False, at)
-        for t in range(tiles + 2):
-            for c in range(2):
-                x, y = push[0, c, t], push[1, c, t]
-                beside[c, t] = clear(x + right(y))
-                if t < tiles:
-                    v[k + 1, c, t] = left(x) + y
-                else:
-                    strips[t - tiles, c] = left(x) + y
-
-    for at in columns:
-        cells(ITERS - 1, True, at)
+            x, y = push[0, c, t], push[1, c, t]
+            beside[c, t] = clear(x + right(y))
+            if t < tiles:
+                v[k + 1, c, t] = left(x) + y
+            else:
+                strips[t - tiles, c] = left(x) + y
+
+
+def basis_pass(k, v, strips, beside, push, moduli, partial, mask):
+    for at in lane_tiles(v.shape[4]):
+        above, below = outer_tiles(k, v, strips, beside, at)
+        inner_cells(k, v, beside, push, moduli, partial, at, above, below)
+    for at in lane_tiles(v.shape[4]) if k + 1 < ITERS else []:
+        strip_cells(strips, beside, push, moduli, mask, at)
 
 
 def finish(v_in, push, v):
@@ -313,15 +335,18 @@
         packet[TILE * line : TILE * (line + 1), :] = result
 
 
-def early(v, packet, beside):
+def early(v, moduli, packet, beside, push, partial):
     tiles, _, width = v.shape[2:]
-    pack(packet, range(tiles // 4), lambda slot, c, at: v[0, c, slot, :, at], width)
     for c in range(2):
         for t in range(tiles):
             beside[c, t] = pltpu.roll(v[0, c, t], width - 1, 1)
-
-
-def block(v_in, packet_in, beside_in, group_moduli, above, below, v, packet, beside, push, strips, moduli, partial, *, gx):
+    pack(packet, range(tiles // 4), lambda slot, c, at: v[0, c, slot, :, at], width)
+    for at in lane_tiles(width):
+        inner_cells(0, v, beside, push, moduli, partial, at)
+
+
+def block(*refs, gx):
+    group_moduli, above, below, v, packet, beside, push, partial, strips, moduli = refs[5:]
     tiles, _, width = v.shape[2:]
     groups = tiles // TILE
     place = lax.axis_index("gx")
@@ -355,7 +380,25 @@
         return edge[c][:, at] if slot == tiles + groups + 1 else None
 
     pack(packet, range(tiles // 4, packet.shape[0] // TILE - 1), pick, width)
-    basis(v, strips, beside, push, moduli, partial, mask, right, left, lambda x: x)
+    strip_neighbours(strips, beside, right)
+    for at in lane_tiles(width):
+        strip_cells(strips, beside, push, moduli, mask, at)
+        over, under = outer_tiles(0, v, strips, beside, at)
+        tile = lambda t: [(v[0, c, t, :, at], beside[c, t, :, at]) for c in range(2)]
+        modulus = lambda g: (moduli[0, g, :, at], moduli[1, g, :, at])
+        last = groups - 1
+        first_cells = stress(over, tile(0), *modulus(groups))[0], stress(tile(0), tile(1), *modulus(0))[0]
+        final, strain = stress(tile(tiles - 1), under, *modulus(last))
+        final_cells = stress(tile(tiles - 2), tile(tiles - 1), *modulus(last))[0], final
+        for t, pair in ((0, first_cells), (tiles - 1, final_cells)):
+            for c, (x, y) in enumerate(forces(*pair)):
+                push[0, c, t, :, at], push[1, c, t, :, at] = x, y
+        partial[1, :, at] = partial[1, :, at] + dot(strain, final)
+
+    for k in range(ITERS - 1):
+        advance(k, v, strips, beside, push, right, left, lambda x: x)
+        basis_pass(k + 1, v, strips, beside, push, moduli, partial, mask)
+
 
     lane = iota((TILE, width), 1)
     keep = (lane >= HALO) & (lane < width - HALO)
@@ -416,7 +459,12 @@
     for c in range(2):
         for t in range(tiles):
             beside[c, t] = right(v[0, c, t])
-    basis(v, strips, beside, push, moduli, partial, mask, right, left, clear)
+    strip_neighbours(strips, beside, right)
+
+    for k in range(ITERS - 1):
+        basis_pass(k, v, strips, beside, push, moduli, partial, mask)
+        advance(k, v, strips, beside, push, right, left, clear)
+    basis_pass(ITERS - 1, v, strips, beside, push, moduli, partial, mask)
 
     column = lane % STRIP
     keep = ((column < HALO) | (column >= STRIP - HALO)) & (lane < STRIP * gy)
@@ -513,10 +561,7 @@
     strips_of = lambda lanes: pltpu.VMEM((2, 2, TILE, lanes), F32)
     beside_of = lambda lanes: pltpu.VMEM((2, tiles + 2, TILE, lanes), F32)
     push_of = lambda lanes: pltpu.VMEM((2, 2, tiles + 2, TILE, lanes), F32)
-    work = lambda lanes: [
-        pltpu.VMEM((2, groups + 3, TILE, lanes), F32),
-        pltpu.VMEM((2 * ITERS, TILE, lanes), F32),
-    ]
+    moduli_of = lambda lanes: pltpu.VMEM((2, groups + 3, TILE, lanes), F32)
 
     packets = 1 if gx == 2 else 2
     v, moduli, *sent = pl.pallas_call(
@@ -543,24 +588,26 @@
 
     slots = tiles + groups + 2
     packet_rows = TILE * (-(-slots // 4) + 1)
-    packet, beside = pl.pallas_call(
+    partial_of = lambda lanes: pltpu.VMEM((2 * ITERS, TILE, lanes), F32)
+    packet, beside, push, partial = pl.pallas_call(
         early,
-        in_specs=[vmem],
-        out_specs=[vmem] * 2,
-        out_shape=[shape(packet_rows, LANES), beside_of(width)],
+        in_specs=[vmem] * 2,
+        out_specs=[vmem] * 4,
+        out_shape=[shape(packet_rows, LANES), beside_of(width), push_of(width), partial_of(width)],
         compiler_params=params,
         name="early",
-    )(pin(v))
-    v, packet, _, push = pl.pallas_call(
+    )(pin(v), pin(moduli))
+    carried = v, packet, beside, push, partial
+    v, packet, _, push, _ = pl.pallas_call(
         functools.partial(block, gx=gx),
-        in_specs=[vmem] * 6,
-        out_specs=[vmem] * 4,
-        out_shape=[shape(*dims, width), shape(packet_rows, LANES), beside_of(width), push_of(width)],
-        scratch_shapes=[strips_of(width)] + work(width),
-        input_output_aliases={0: 0, 1: 1, 2: 2},
+        in_specs=[vmem] * 8,
+        out_specs=[vmem] * 5,
+        out_shape=[pltpu.VMEM(x.shape, F32) for x in carried],
+        scratch_shapes=[strips_of(width), moduli_of(width)],
+        input_output_aliases={i: i for i in range(5)},
         compiler_params=params,
         name="block",
-    )(*map(pin, (v, packet, beside, moduli, above, below)))
+    )(*map(pin, (*carried, moduli, above, below)))
 
     arrived = [packet] + [lax.ppermute(packet, "gy", route) for route in routes(gy)]
     v = pl.pallas_call(
@@ -578,7 +625,7 @@
         out_specs=[vmem] * 4,
         out_shape=[shape(*dims, LANES), shape(2, 2 * ITERS, LANES), push_of(LANES), shape(*dims, width)],
         input_output_aliases={gy: 3},
-        scratch_shapes=[strips_of(LANES), beside_of(LANES)] + work(LANES),
+        scratch_shapes=[strips_of(LANES), beside_of(LANES), moduli_of(LANES), partial_of(LANES)],
         compiler_params=params,
         name="interfaces",
     )(*map(pin, arrived), pin(v))

time: 19.6 us -> 19.1 us (0.974)
  Pallas kernels: 7.6 us -> 7.3 us
  transfers between devices with their start and end apart: 5 -> 5, of which waited for: 4 -> 4; matrix products, arithmetic and copies ran while one was open for 0% -> 0% of each run, Pallas kernels for 7% -> 8%
where the time goes in v7:
time: 19.1 us; the launch traced here: 18.9 us
  Pallas kernels  7.3 us (38%)
  starting transfers between devices  6.27 us (33%)
  waiting for transfers between devices  4.67 us (24%)
  between operations  0.68 us (4%)
    ppermute x3, starting transfers between devices, on_device(): lax.ppermute(packet, 'gy', route)  5.64 us
    ppermute x3, waiting for transfers between devices, on_device(): lax.ppermute(packet, 'gy', route)  3.88 us
    pallas_call x1, Pallas kernels, on_device(): pl.pallas_call(functools.partial(combine, gx=gx), in_specs=[vmem] * (gx +...  1.95 us
    pallas_call x1, Pallas kernels, on_device(): pl.pallas_call(functools.partial(block, gx=gx), in_specs=[vmem] * 8, out_...  1.84 us
    pallas_call x1, Pallas kernels, on_device(): pl.pallas_call(functools.partial(prepare, gx=gx), in_specs=[hbm] * 3, out...  1.27 us
    pallas_call x1, Pallas kernels, on_device(): pl.pallas_call(merge, in_specs=[vmem] * 3, out_specs=vmem, out_shape=pltp...  0.82 us
    pallas_call x1, Pallas kernels, on_device(): pl.pallas_call(functools.partial(interfaces, gx=gx, gy=gy, sources=source...  0.81 us
    ppermute x1, starting transfers between devices, on_device(): above = below = lax.ppermute(sent[0], 'gx', [(0, 1), (1, 0)])  0.56 us
  transfers between devices with their start and end apart: 5, of which 4 were waited for; matrix products, arithmetic and copies ran while one was open for 0% of the time, Pallas kernels for 8%

profile of v7, /device:TPU:0, one launch (start us, length us, event | category | flops | bytes accessed | tf_op | source)
XLA Modules:
  0.0 18.9 jit_solution(10453658481659131167)
XLA Ops:
  0.6 1.3 %prepare.1 = (f32[5,2,16,8,512]{4,3,2,1,0:T(8,128)S(1)}, f32[2,2,8,512]{3,2,1,0:T(8,128)S(1)}, f32[3,8,512]{2,1,0:T(8,128)S(1)}) custom-call(f32[2,8]{1,0:T(2,128)} %table.1, f32[1,2,128,512]{3,2,1,0:T(8,128)} %load.1, s32[1,16,64]{2,1,0:T(8,128)} %material.1), custom_call_target="tpu_custom_call" | custom-call | tf_op jit(solution)/shard_map/prepare/pallas_call | solution.py:567
  1.9 0.6 %collective-permute-start = (f32[3,8,512]{2,1,0:T(8,128)S(1)}, f32[3,8,512]{2,1,0:T(8,128)S(1)}, u32[]{:S(2)}, u32[]{:S(2)}) collective-permute-start(f32[3,8,512]{2,1,0:T(8,128)S(1)} %get-tuple-element.22), channel_id=1, source_target_pairs={{0,4},{4,0},{1,5},{5,1},{2,6},{6,2},{3,7},{7,3},{8,12},{12,8},{9,1... | collective-permute-start | bytes 147464 | tf_op jit(solution)/shard_map/ppermute | solution.py:584
  2.5 0.4 %early.1 = (f32[48,128]{1,0:T(8,128)S(1)}, f32[2,18,8,512]{3,2,1,0:T(8,128)S(1)}, f32[2,2,18,8,512]{4,3,2,1,0:T(8,128)S(1)}, f32[8,8,512]{2,1,0:T(8,128)S(1)}) custom-call(f32[5,2,16,8,512]{4,3,2,1,0:T(8,128)S(1)} %get-tuple-element.16.v.refs_0_, f32[2,2,8,512]{3,2,1,0:T(8,128)S(1)} %get-tuple-element.17.moduli.refs_5_), custom_call_target="tpu_custom_call" | custom-call | tf_op jit(solution)/shard_map/early/pallas_call | solution.py:592
  2.9 0.5 %collective-permute-done.refs_6_.refs_7_ = f32[3,8,512]{2,1,0:T(8,128)S(1)} collective-permute-done((f32[3,8,512]{2,1,0:T(8,128)S(1)}, f32[3,8,512]{2,1,0:T(8,128)S(1)}, u32[]{:S(2)}, u32[]{:S(2)}) %collective-permute-start) | collective-permute-done | bytes 49184 | tf_op jit(solution)/shard_map/ppermute | solution.py:584
  3.3 1.8 %block.1 = (f32[5,2,16,8,512]{4,3,2,1,0:T(8,128)S(1)}, f32[48,128]{1,0:T(8,128)S(1)}, f32[2,18,8,512]{3,2,1,0:T(8,128)S(1)}, f32[2,2,18,8,512]{4,3,2,1,0:T(8,128)S(1)}, f32[8,8,512]{2,1,0:T(8,128)S(1)}) custom-call(f32[5,2,16,8,512]{4,3,2,1,0:T(8,128)S(1)} %get-tuple-element.16.v.refs_, ...), custom_call_target="tpu_custom_call", output_to_operand_aliasing={{0}: (0, {}), {1}: (1, {}), {2}: (2, {}), {3}: (3, {}), {4}... | custom-call | tf_op jit(solution)/shard_map/block/pallas_call | solution.py:601
  5.2 5.0 %collective-permute-start.3 = (f32[48,128]{1,0:T(8,128)S(1)}, f32[48,128]{1,0:T(8,128)S(1)}, u32[]{:S(2)}, u32[]{:S(2)}) collective-permute-start(f32[48,128]{1,0:T(8,128)S(1)} %get-tuple-element.23.refs_0_), channel_id=1, source_target_pairs={{0,3},{1,2},{2,1},{3,0},{4,7},{5,6},{6,5},{7,4},{8,11},{9,10},{10,... | collective-permute-start | bytes 73736 | tf_op jit(solution)/shard_map/ppermute | solution.py:612
  10.2 0.0 collective-permute-start.2
  10.2 0.6 %collective-permute-start.1 = (f32[48,128]{1,0:T(8,128)S(1)}, f32[48,128]{1,0:T(8,128)S(1)}, u32[]{:S(2)}, u32[]{:S(2)}) collective-permute-start(f32[48,128]{1,0:T(8,128)S(1)} %get-tuple-element.23.refs_0_), channel_id=1, source_target_pairs={{0,1},{1,0},{2,3},{3,2},{4,5},{5,4},{6,7},{7,6},{8,9},{9,8},{10,11... | collective-permute-start | bytes 73736 | tf_op jit(solution)/shard_map/ppermute | solution.py:612
  10.8 0.2 %finish.1.refs_4_ = f32[5,2,16,8,512]{4,3,2,1,0:T(8,128)S(1)} custom-call(f32[5,2,16,8,512]{4,3,2,1,0:T(8,128)S(1)} %get-tuple-element.24.v_in, f32[2,2,18,8,512]{4,3,2,1,0:T(8,128)S(1)} %get-tuple-element.25.push), custom_call_target="tpu_custom_call", output_to_operand_aliasing={{}: (0, {})} | custom-call | tf_op jit(solution)/shard_map/finish/pallas_call | solution.py:613
  11.0 1.0 %collective-permute-done.3.refs_3_ = f32[48,128]{1,0:T(8,128)S(1)} collective-permute-done((f32[48,128]{1,0:T(8,128)S(1)}, f32[48,128]{1,0:T(8,128)S(1)}, u32[]{:S(2)}, u32[]{:S(2)}) %collective-permute-start.3) | collective-permute-done | bytes 24608 | tf_op jit(solution)/shard_map/ppermute | solution.py:612
  12.0 2.9 %collective-permute-done.2.refs_2_ = f32[48,128]{1,0:T(8,128)S(1)} collective-permute-done((f32[48,128]{1,0:T(8,128)S(1)}, f32[48,128]{1,0:T(8,128)S(1)}, u32[]{:S(2)}, u32[]{:S(2)}) %collective-permute-start.2) | collective-permute-done | bytes 24608 | tf_op jit(solution)/shard_map/ppermute | solution.py:612
  14.9 0.0 collective-permute-done.1.refs_1_
  14.9 0.8 %interfaces.1 = (f32[5,2,16,8,128]{4,3,2,1,0:T(8,128)S(1)}, f32[2,8,128]{2,1,0:T(8,128)S(1)}, f32[2,2,18,8,128]{4,3,2,1,0:T(8,128)S(1)}, f32[5,2,16,8,512]{4,3,2,1,0:T(8,128)S(1)}) custom-call(f32[48,128]{1,0:T(8,128)S(1)} %get-tuple-element.23.refs_0_, f32[48,128]{1,0:T(8,128)S(1)} %collective-permute-done.1.refs_1_, ...), custom_call_target="tpu_custom_call", output_to_operand_aliasing={{3}: (4, {})} | custom-call | tf_op jit(solution)/shard_map/interfaces/pallas_call | solution.py:622
  15.7 0.1 collective-permute-start.4
  15.8 0.8 %merge.1.refs_2_ = f32[5,2,16,8,512]{4,3,2,1,0:T(8,128)S(1)} custom-call(f32[5,2,16,8,512]{4,3,2,1,0:T(8,128)S(1)} %get-tuple-element.27.v_in, f32[5,2,16,8,128]{4,3,2,1,0:T(8,128)S(1)} %get-tuple-element.28.strips, f32[2,2,18,8,128]{4,3,2,1,0:T(8,128)S(1)} %get-tuple-element.29.strips_push), custom_call_target="tpu_custom_call", output_to_operand_aliasing={{}: (0, {})} | custom-call | tf_op jit(solution)/shard_map/merge/pallas_call | solution.py:634
  16.6 0.3 %collective-permute-done.4.refs_1_ = f32[2,8,128]{2,1,0:T(8,128)S(1)} collective-permute-done((f32[2,8,128]{2,1,0:T(8,128)S(1)}, f32[2,8,128]{2,1,0:T(8,128)S(1)}, u32[]{:S(2)}, u32[]{:S(2)}) %collective-permute-start.4) | collective-permute-done | bytes 8224 | tf_op jit(solution)/shard_map/ppermute | solution.py:633
  17.0 2.0 %combine.1 = (f32[1,2,128,512]{3,2,1,0:T(8,128)}, f32[1,2,128,512]{3,2,1,0:T(8,128)}) custom-call(f32[2,8,128]{2,1,0:T(8,128)S(1)} %get-tuple-element.26.refs_0_, f32[2,8,128]{2,1,0:T(8,128)S(1)} %collective-permute-done.4.refs_1_, f32[5,2,16,8,512]{4,3,2,1,0:T(8,128)S(1)} %merge.1.refs_2_), custom_call_target="tpu_custom_call" | custom-call | tf_op jit(solution)/shard_map/combine/pallas_call | solution.py:644
Async XLA Ops:
  1.9 1.4 %collective-permute-start = (f32[3,8,512]{2,1,0:T(8,128)S(1)}, f32[3,8,512]{2,1,0:T(8,128)S(1)}, u32[]{:S(2)}, u32[]{:S(2)}) collective-permute-start(f32[3,8,512]{2,1,0:T(8,128)S(1)} %get-tuple-element.22), channel_id=1, source_target_pairs={{0,4},{4,0},{1,5},{5,1},{2,6},{6,2},{3,7},{7,3},{8,12},{12,8},{9,1... | collective-permute-start | bytes 147464 | tf_op jit(solution)/shard_map/ppermute | solution.py:584
  5.2 6.8 %collective-permute-start.3 = (f32[48,128]{1,0:T(8,128)S(1)}, f32[48,128]{1,0:T(8,128)S(1)}, u32[]{:S(2)}, u32[]{:S(2)}) collective-permute-start(f32[48,128]{1,0:T(8,128)S(1)} %get-tuple-element.23.refs_0_), channel_id=1, source_target_pairs={{0,3},{1,2},{2,1},{3,0},{4,7},{5,6},{6,5},{7,4},{8,11},{9,10},{10,... | collective-permute-start | bytes 73736 | tf_op jit(solution)/shard_map/ppermute | solution.py:612
  10.2 4.7 %collective-permute-start.2 = (f32[48,128]{1,0:T(8,128)S(1)}, f32[48,128]{1,0:T(8,128)S(1)}, u32[]{:S(2)}, u32[]{:S(2)}) collective-permute-start(f32[48,128]{1,0:T(8,128)S(1)} %get-tuple-element.23.refs_0_), channel_id=1, source_target_pairs={{0,2},{1,3},{2,0},{3,1},{4,6},{5,7},{6,4},{7,5},{8,10},{9,11},{10,... | collective-permute-start | bytes 73736 | tf_op jit(solution)/shard_map/ppermute | solution.py:612
  10.2 4.7 %collective-permute-start.1 = (f32[48,128]{1,0:T(8,128)S(1)}, f32[48,128]{1,0:T(8,128)S(1)}, u32[]{:S(2)}, u32[]{:S(2)}) collective-permute-start(f32[48,128]{1,0:T(8,128)S(1)} %get-tuple-element.23.refs_0_), channel_id=1, source_target_pairs={{0,1},{1,0},{2,3},{3,2},{4,5},{5,4},{6,7},{7,6},{8,9},{9,8},{10,11... | collective-permute-start | bytes 73736 | tf_op jit(solution)/shard_map/ppermute | solution.py:612
  15.7 1.2 %collective-permute-start.4 = (f32[2,8,128]{2,1,0:T(8,128)S(1)}, f32[2,8,128]{2,1,0:T(8,128)S(1)}, u32[]{:S(2)}, u32[]{:S(2)}) collective-permute-start(f32[2,8,128]{2,1,0:T(8,128)S(1)} %get-tuple-element.26.refs_0_), channel_id=1, source_target_pairs={{0,4},{4,0},{1,5},{5,1},{2,6},{6,2},{3,7},{7,3},{8,12},{12,8},{9,1... | collective-permute-start | bytes 24584 | tf_op jit(solution)/shard_map/ppermute | solution.py:633

commit v8 on v7

--- a/solution.py
+++ b/solution.py
@@ -114,29 +114,38 @@
     return [slice(start, start + LANES) for start in range(0, width, LANES)]
 
 
-def inner_cells(k, v, beside, push, moduli, partial, at, above=None, below=None):
+def cells(k, v, beside, push, moduli, partial, at, span, squares, works, outer=(None, None), more=False):
     tiles = v.shape[2]
     groups = tiles // TILE
-    tile = lambda c, t: (v[k, c, t, :, at], beside[c, t, :, at])
-    modulus = lambda g: (moduli[0, g, :, at], moduli[1, g, :, at])
-    here = [tile(c, 0) for c in range(2)]
-    before = stress(above, here, *modulus(groups))[0] if above else None
-    own = energy = None
-    for t in range(tiles):
-        values = [x for x, _ in here]
-        square = dot(values, values)
-        own = square if own is None else own + square
-        after = [tile(c, t + 1) for c in range(2)] if t + 1 < tiles else below
-        if after:
-            s, strain = stress(here, after, *modulus(t // TILE))
-            work = dot(strain, s)
-            energy = work if energy is None else energy + work
-            if before:
-                for c, (x, y) in enumerate(forces(before, s)):
-                    push[0, c, t, :, at], push[1, c, t, :, at] = x, y
-            before, here = s, after
-    partial[2 * k, :, at] = own
-    partial[2 * k + 1, :, at] = energy
+
+    def nodes(t):
+        if 0 <= t < tiles:
+            return [(v[k, c, t, :, at], beside[c, t, :, at]) for c in range(2)]
+        return outer[t > 0]
+
+    first, last = span
+    here = nodes(first)
+    before = None
+    own = [partial[2 * k, :, at]] if more else []
+    energy = [partial[2 * k + 1, :, at]] if more else []
+    for t in range(first, last):
+        after = nodes(t + 1)
+        g = groups if t < 0 else t // TILE
+        s, strain = stress(here, after, moduli[0, g, :, at], moduli[1, g, :, at])
+        if t in works:
+            energy = [total(energy + [dot(strain, s)])]
+        for node, tile in ((t, here), (t + 1, after)):
+            if node in squares and (node == t or node == last):
+                values = [x for x, _ in tile]
+                own = [total(own + [dot(values, values)])]
+        if before:
+            for c, (x, y) in enumerate(forces(before, s)):
+                push[0, c, t, :, at], push[1, c, t, :, at] = x, y
+        before, here = s, after
+    if squares:
+        partial[2 * k, :, at] = own[0]
+    if works:
+        partial[2 * k + 1, :, at] = energy[0]
 
 
 def outer_tiles(k, v, strips, beside, at):
@@ -171,9 +180,9 @@
             beside[c, tiles + s] = right(strips[s, c])
 
 
-def advance(k, v, strips, beside, push, right, left, clear):
+def advance(k, v, strips, beside, push, right, left, clear, which=None):
     tiles = v.shape[2]
-    for t in range(tiles + 2):
+    for t in which or range(tiles + 2):
         for c in range(2):
             x, y = push[0, c, t], push[1, c, t]
             beside[c, t] = clear(x + right(y))
@@ -185,8 +194,9 @@
 
 def basis_pass(k, v, strips, beside, push, moduli, partial, mask):
     for at in lane_tiles(v.shape[4]):
-        above, below = outer_tiles(k, v, strips, beside, at)
-        inner_cells(k, v, beside, push, moduli, partial, at, above, below)
+        outer = outer_tiles(k, v, strips, beside, at)
+        every = range(v.shape[2])
+        cells(k, v, beside, push, moduli, partial, at, (-1, len(every)), every, every, outer)
     for at in lane_tiles(v.shape[4]) if k + 1 < ITERS else []:
         strip_cells(strips, beside, push, moduli, mask, at)
 
@@ -335,14 +345,20 @@
         packet[TILE * line : TILE * (line + 1), :] = result
 
 
-def early(v, moduli, packet, beside, push, partial):
+def early(v_in, moduli, v, packet, beside, push, partial):
     tiles, _, width = v.shape[2:]
     for c in range(2):
         for t in range(tiles):
             beside[c, t] = pltpu.roll(v[0, c, t], width - 1, 1)
     pack(packet, range(tiles // 4), lambda slot, c, at: v[0, c, slot, :, at], width)
+    right = lambda x: pltpu.roll(x, width - 1, 1)
+    left = lambda x: pltpu.roll(x, 1, 1)
     for at in lane_tiles(width):
-        inner_cells(0, v, beside, push, moduli, partial, at)
+        cells(0, v, beside, push, moduli, partial, at, (0, tiles - 1), range(tiles), range(tiles - 1))
+    inner = range(2, tiles - 2)
+    advance(0, v, None, beside, push, right, left, lambda x: x, inner)
+    for at in lane_tiles(width):
+        cells(1, v, beside, push, moduli, partial, at, (2, tiles - 3), inner, range(2, tiles - 3))
 
 
 def block(*refs, gx):
@@ -381,24 +397,21 @@
 
     pack(packet, range(tiles // 4, packet.shape[0] // TILE - 1), pick, width)
     strip_neighbours(strips, beside, right)
-    for at in lane_tiles(width):
-        strip_cells(strips, beside, push, moduli, mask, at)
-        over, under = outer_tiles(0, v, strips, beside, at)
-        tile = lambda t: [(v[0, c, t, :, at], beside[c, t, :, at]) for c in range(2)]
-        modulus = lambda g: (moduli[0, g, :, at], moduli[1, g, :, at])
-        last = groups - 1
-        first_cells = stress(over, tile(0), *modulus(groups))[0], stress(tile(0), tile(1), *modulus(0))[0]
-        final, strain = stress(tile(tiles - 1), under, *modulus(last))
-        final_cells = stress(tile(tiles - 2), tile(tiles - 1), *modulus(last))[0], final
-        for t, pair in ((0, first_cells), (tiles - 1, final_cells)):
-            for c, (x, y) in enumerate(forces(*pair)):
-                push[0, c, t, :, at], push[1, c, t, :, at] = x, y
-        partial[1, :, at] = partial[1, :, at] + dot(strain, final)
-
-    for k in range(ITERS - 1):
-        advance(k, v, strips, beside, push, right, left, lambda x: x)
-        basis_pass(k + 1, v, strips, beside, push, moduli, partial, mask)
-
+    edges = [0, 1, tiles - 2, tiles - 1]
+    same = lambda x: x
+    for k in range(ITERS):
+        if k < 2:
+            for at in lane_tiles(width):
+                strip_cells(strips, beside, push, moduli, mask, at)
+                outer = outer_tiles(k, v, strips, beside, at)
+                part = functools.partial(cells, k, v, beside, push, moduli, partial, at, outer=outer, more=True)
+                part((-1, 1 + 2 * k), edges[: 2 * k], edges[: 2 * k])
+                part((tiles - 2 - 2 * k, tiles), edges[2:] * k, range(tiles - 1 - 2 * k, tiles))
+        else:
+            basis_pass(k, v, strips, beside, push, moduli, partial, mask)
+        if k + 1 < ITERS:
+            which = None if k else edges + [tiles, tiles + 1]
+            advance(k, v, strips, beside, push, right, left, same, which)
 
     lane = iota((TILE, width), 1)
     keep = (lane >= HALO) & (lane < width - HALO)
@@ -589,15 +602,15 @@
     slots = tiles + groups + 2
     packet_rows = TILE * (-(-slots // 4) + 1)
     partial_of = lambda lanes: pltpu.VMEM((2 * ITERS, TILE, lanes), F32)
-    packet, beside, push, partial = pl.pallas_call(
+    carried = pl.pallas_call(
         early,
         in_specs=[vmem] * 2,
-        out_specs=[vmem] * 4,
-        out_shape=[shape(packet_rows, LANES), beside_of(width), push_of(width), partial_of(width)],
+        out_specs=[vmem] * 5,
+        input_output_aliases={0: 0},
+        out_shape=[shape(*dims, width), shape(packet_rows, LANES), beside_of(width), push_of(width), partial_of(width)],
         compiler_params=params,
         name="early",
     )(pin(v), pin(moduli))
-    carried = v, packet, beside, push, partial
     v, packet, _, push, _ = pl.pallas_call(
         functools.partial(block, gx=gx),
         in_specs=[vmem] * 8,

time: 19.1 us -> 18.8 us (0.984)
  waiting for transfers between devices: 4.67 us -> 4.35 us
    pallas_call x1, Pallas kernels: 1.84 us -> 1.52 us  [on_device(): pl.pallas_call(functools.partial(block, gx=gx), in_specs=[vmem] * 8, out_...]
    pallas_call x1, Pallas kernels: 0.41 us -> 0.73 us  [on_device(): pl.pallas_call(early, in_specs=[vmem] * 2, out_specs=[vmem] * 5, input_ou...]
    ppermute x1, waiting for transfers between devices: 0.46 us -> 0.15 us  [on_device(): above = below = lax.ppermute(sent[0], 'gx', [(0, 1), (1, 0)])]
  transfers between devices with their start and end apart: 5 -> 5, of which waited for: 4 -> 4; matrix products, arithmetic and copies ran while one was open for 0% -> 0% of each run, Pallas kernels for 8% -> 9%
where the time goes in v8:
time: 18.8 us; the launch traced here: 18.6 us
  Pallas kernels  7.31 us (39%)
  starting transfers between devices  6.27 us (33%)
  waiting for transfers between devices  4.35 us (23%)
  between operations  0.68 us (4%)
    ppermute x3, starting transfers between devices, on_device(): lax.ppermute(packet, 'gy', route)  5.64 us
    ppermute x3, waiting for transfers between devices, on_device(): lax.ppermute(packet, 'gy', route)  3.88 us
    pallas_call x1, Pallas kernels, on_device(): pl.pallas_call(functools.partial(combine, gx=gx), in_specs=[vmem] * (gx +...  1.95 us
    pallas_call x1, Pallas kernels, on_device(): pl.pallas_call(functools.partial(block, gx=gx), in_specs=[vmem] * 8, out_...  1.52 us
    pallas_call x1, Pallas kernels, on_device(): pl.pallas_call(functools.partial(prepare, gx=gx), in_specs=[hbm] * 3, out...  1.27 us
    pallas_call x1, Pallas kernels, on_device(): pl.pallas_call(merge, in_specs=[vmem] * 3, out_specs=vmem, out_shape=pltp...  0.82 us
    pallas_call x1, Pallas kernels, on_device(): pl.pallas_call(functools.partial(interfaces, gx=gx, gy=gy, sources=source...  0.81 us
    pallas_call x1, Pallas kernels, on_device(): pl.pallas_call(early, in_specs=[vmem] * 2, out_specs=[vmem] * 5, input_ou...  0.73 us
  transfers between devices with their start and end apart: 5, of which 4 were waited for; matrix products, arithmetic and copies ran while one was open for 0% of the time, Pallas kernels for 9%

profile of v8, /device:TPU:0, one launch (start us, length us, event | category | flops | bytes accessed | tf_op | source)
XLA Modules:
  0.0 18.6 jit_solution(18111852879953863476)
XLA Ops:
  0.6 1.3 %prepare.1 = (f32[5,2,16,8,512]{4,3,2,1,0:T(8,128)S(1)}, f32[2,2,8,512]{3,2,1,0:T(8,128)S(1)}, f32[3,8,512]{2,1,0:T(8,128)S(1)}) custom-call(f32[2,8]{1,0:T(2,128)} %table.1, f32[1,2,128,512]{3,2,1,0:T(8,128)} %load.1, s32[1,16,64]{2,1,0:T(8,128)} %material.1), custom_call_target="tpu_custom_call" | custom-call | tf_op jit(solution)/shard_map/prepare/pallas_call | solution.py:580
  1.9 0.6 %collective-permute-start = (f32[3,8,512]{2,1,0:T(8,128)S(1)}, f32[3,8,512]{2,1,0:T(8,128)S(1)}, u32[]{:S(2)}, u32[]{:S(2)}) collective-permute-start(f32[3,8,512]{2,1,0:T(8,128)S(1)} %get-tuple-element.24), channel_id=1, source_target_pairs={{0,4},{4,0},{1,5},{5,1},{2,6},{6,2},{3,7},{7,3},{8,12},{12,8},{9,1... | collective-permute-start | bytes 147464 | tf_op jit(solution)/shard_map/ppermute | solution.py:597
  2.5 0.7 %early.1 = (f32[5,2,16,8,512]{4,3,2,1,0:T(8,128)S(1)}, f32[48,128]{1,0:T(8,128)S(1)}, f32[2,18,8,512]{3,2,1,0:T(8,128)S(1)}, f32[2,2,18,8,512]{4,3,2,1,0:T(8,128)S(1)}, f32[8,8,512]{2,1,0:T(8,128)S(1)}) custom-call(f32[5,2,16,8,512]{4,3,2,1,0:T(8,128)S(1)} %get-tuple-element.17.v_in, ...), custom_call_target="tpu_custom_call", output_to_operand_aliasing={{0}: (0, {})} | custom-call | tf_op jit(solution)/shard_map/early/pallas_call | solution.py:605
  3.2 0.1 collective-permute-done.refs_6_.refs_7_
  3.3 1.5 %block.1 = (f32[5,2,16,8,512]{4,3,2,1,0:T(8,128)S(1)}, f32[48,128]{1,0:T(8,128)S(1)}, f32[2,18,8,512]{3,2,1,0:T(8,128)S(1)}, f32[2,2,18,8,512]{4,3,2,1,0:T(8,128)S(1)}, f32[8,8,512]{2,1,0:T(8,128)S(1)}) custom-call(f32[5,2,16,8,512]{4,3,2,1,0:T(8,128)S(1)} %get-tuple-element.19.refs_0_, ...), custom_call_target="tpu_custom_call", output_to_operand_aliasing={{0}: (0, {}), {1}: (1, {}), {2}: (2, {}), {3}: (3, {}), {4}... | custom-call | tf_op jit(solution)/shard_map/block/pallas_call | solution.py:614
  4.9 5.0 %collective-permute-start.3 = (f32[48,128]{1,0:T(8,128)S(1)}, f32[48,128]{1,0:T(8,128)S(1)}, u32[]{:S(2)}, u32[]{:S(2)}) collective-permute-start(f32[48,128]{1,0:T(8,128)S(1)} %get-tuple-element.25.refs_0_), channel_id=1, source_target_pairs={{0,3},{1,2},{2,1},{3,0},{4,7},{5,6},{6,5},{7,4},{8,11},{9,10},{10,... | collective-permute-start | bytes 73736 | tf_op jit(solution)/shard_map/ppermute | solution.py:625
  9.9 0.0 collective-permute-start.2
  9.9 0.6 %collective-permute-start.1 = (f32[48,128]{1,0:T(8,128)S(1)}, f32[48,128]{1,0:T(8,128)S(1)}, u32[]{:S(2)}, u32[]{:S(2)}) collective-permute-start(f32[48,128]{1,0:T(8,128)S(1)} %get-tuple-element.25.refs_0_), channel_id=1, source_target_pairs={{0,1},{1,0},{2,3},{3,2},{4,5},{5,4},{6,7},{7,6},{8,9},{9,8},{10,11... | collective-permute-start | bytes 73736 | tf_op jit(solution)/shard_map/ppermute | solution.py:625
  10.5 0.2 %finish.1.refs_4_ = f32[5,2,16,8,512]{4,3,2,1,0:T(8,128)S(1)} custom-call(f32[5,2,16,8,512]{4,3,2,1,0:T(8,128)S(1)} %get-tuple-element.26.v_in, f32[2,2,18,8,512]{4,3,2,1,0:T(8,128)S(1)} %get-tuple-element.27.push), custom_call_target="tpu_custom_call", output_to_operand_aliasing={{}: (0, {})} | custom-call | tf_op jit(solution)/shard_map/finish/pallas_call | solution.py:626
  10.7 1.0 %collective-permute-done.3.refs_3_ = f32[48,128]{1,0:T(8,128)S(1)} collective-permute-done((f32[48,128]{1,0:T(8,128)S(1)}, f32[48,128]{1,0:T(8,128)S(1)}, u32[]{:S(2)}, u32[]{:S(2)}) %collective-permute-start.3) | collective-permute-done | bytes 24608 | tf_op jit(solution)/shard_map/ppermute | solution.py:625
  11.7 2.9 %collective-permute-done.2.refs_2_ = f32[48,128]{1,0:T(8,128)S(1)} collective-permute-done((f32[48,128]{1,0:T(8,128)S(1)}, f32[48,128]{1,0:T(8,128)S(1)}, u32[]{:S(2)}, u32[]{:S(2)}) %collective-permute-start.2) | collective-permute-done | bytes 24608 | tf_op jit(solution)/shard_map/ppermute | solution.py:625
  14.6 0.0 collective-permute-done.1.refs_1_
  14.6 0.8 %interfaces.1 = (f32[5,2,16,8,128]{4,3,2,1,0:T(8,128)S(1)}, f32[2,8,128]{2,1,0:T(8,128)S(1)}, f32[2,2,18,8,128]{4,3,2,1,0:T(8,128)S(1)}, f32[5,2,16,8,512]{4,3,2,1,0:T(8,128)S(1)}) custom-call(f32[48,128]{1,0:T(8,128)S(1)} %get-tuple-element.25.refs_0_, f32[48,128]{1,0:T(8,128)S(1)} %collective-permute-done.1.refs_1_, ...), custom_call_target="tpu_custom_call", output_to_operand_aliasing={{3}: (4, {})} | custom-call | tf_op jit(solution)/shard_map/interfaces/pallas_call | solution.py:635
  15.4 0.1 collective-permute-start.4
  15.5 0.8 %merge.1.refs_2_ = f32[5,2,16,8,512]{4,3,2,1,0:T(8,128)S(1)} custom-call(f32[5,2,16,8,512]{4,3,2,1,0:T(8,128)S(1)} %get-tuple-element.29.v_in, f32[5,2,16,8,128]{4,3,2,1,0:T(8,128)S(1)} %get-tuple-element.30.strips, f32[2,2,18,8,128]{4,3,2,1,0:T(8,128)S(1)} %get-tuple-element.31.strips_push), custom_call_target="tpu_custom_call", output_to_operand_aliasing={{}: (0, {})} | custom-call | tf_op jit(solution)/shard_map/merge/pallas_call | solution.py:647
  16.3 0.3 %collective-permute-done.4.refs_1_ = f32[2,8,128]{2,1,0:T(8,128)S(1)} collective-permute-done((f32[2,8,128]{2,1,0:T(8,128)S(1)}, f32[2,8,128]{2,1,0:T(8,128)S(1)}, u32[]{:S(2)}, u32[]{:S(2)}) %collective-permute-start.4) | collective-permute-done | bytes 8224 | tf_op jit(solution)/shard_map/ppermute | solution.py:646
  16.7 2.0 %combine.1 = (f32[1,2,128,512]{3,2,1,0:T(8,128)}, f32[1,2,128,512]{3,2,1,0:T(8,128)}) custom-call(f32[2,8,128]{2,1,0:T(8,128)S(1)} %get-tuple-element.28.refs_0_, f32[2,8,128]{2,1,0:T(8,128)S(1)} %collective-permute-done.4.refs_1_, f32[5,2,16,8,512]{4,3,2,1,0:T(8,128)S(1)} %merge.1.refs_2_), custom_call_target="tpu_custom_call" | custom-call | tf_op jit(solution)/shard_map/combine/pallas_call | solution.py:657
Async XLA Ops:
  1.9 1.4 %collective-permute-start = (f32[3,8,512]{2,1,0:T(8,128)S(1)}, f32[3,8,512]{2,1,0:T(8,128)S(1)}, u32[]{:S(2)}, u32[]{:S(2)}) collective-permute-start(f32[3,8,512]{2,1,0:T(8,128)S(1)} %get-tuple-element.24), channel_id=1, source_target_pairs={{0,4},{4,0},{1,5},{5,1},{2,6},{6,2},{3,7},{7,3},{8,12},{12,8},{9,1... | collective-permute-start | bytes 147464 | tf_op jit(solution)/shard_map/ppermute | solution.py:597
  4.9 6.8 %collective-permute-start.3 = (f32[48,128]{1,0:T(8,128)S(1)}, f32[48,128]{1,0:T(8,128)S(1)}, u32[]{:S(2)}, u32[]{:S(2)}) collective-permute-start(f32[48,128]{1,0:T(8,128)S(1)} %get-tuple-element.25.refs_0_), channel_id=1, source_target_pairs={{0,3},{1,2},{2,1},{3,0},{4,7},{5,6},{6,5},{7,4},{8,11},{9,10},{10,... | collective-permute-start | bytes 73736 | tf_op jit(solution)/shard_map/ppermute | solution.py:625
  9.9 4.7 %collective-permute-start.2 = (f32[48,128]{1,0:T(8,128)S(1)}, f32[48,128]{1,0:T(8,128)S(1)}, u32[]{:S(2)}, u32[]{:S(2)}) collective-permute-start(f32[48,128]{1,0:T(8,128)S(1)} %get-tuple-element.25.refs_0_), channel_id=1, source_target_pairs={{0,2},{1,3},{2,0},{3,1},{4,6},{5,7},{6,4},{7,5},{8,10},{9,11},{10,... | collective-permute-start | bytes 73736 | tf_op jit(solution)/shard_map/ppermute | solution.py:625
  9.9 4.7 %collective-permute-start.1 = (f32[48,128]{1,0:T(8,128)S(1)}, f32[48,128]{1,0:T(8,128)S(1)}, u32[]{:S(2)}, u32[]{:S(2)}) collective-permute-start(f32[48,128]{1,0:T(8,128)S(1)} %get-tuple-element.25.refs_0_), channel_id=1, source_target_pairs={{0,1},{1,0},{2,3},{3,2},{4,5},{5,4},{6,7},{7,6},{8,9},{9,8},{10,11... | collective-permute-start | bytes 73736 | tf_op jit(solution)/shard_map/ppermute | solution.py:625
  15.4 1.2 %collective-permute-start.4 = (f32[2,8,128]{2,1,0:T(8,128)S(1)}, f32[2,8,128]{2,1,0:T(8,128)S(1)}, u32[]{:S(2)}, u32[]{:S(2)}) collective-permute-start(f32[2,8,128]{2,1,0:T(8,128)S(1)} %get-tuple-element.28.refs_0_), channel_id=1, source_target_pairs={{0,4},{4,0},{1,5},{5,1},{2,6},{6,2},{3,7},{7,3},{8,12},{12,8},{9,1... | collective-permute-start | bytes 24584 | tf_op jit(solution)/shard_map/ppermute | solution.py:646

commit v9 on v8

--- a/solution.py
+++ b/solution.py
@@ -50,9 +50,14 @@
     return fast_two_sum(s, e + (x[1] + y[1]))
 
 
+def loose_add(x, y):
+    s, e = two_sum(x[0], y[0])
+    return s, e + (x[1] + y[1])
+
+
 def ds_mul(x, y):
     p, e = two_prod(x[0], y[0])
-    return fast_two_sum(p, e + (x[0] * y[1] + x[1] * y[0]))
+    return p, e + (x[0] * y[1] + x[1] * y[0])
 
 
 def ds_neg(x):
@@ -61,14 +66,14 @@
 
 def ds_scale(c, x):
     p, e = two_prod(jnp.full(x[0].shape, c, F32), x[0])
-    return fast_two_sum(p, e + c * x[1])
+    return p, e + c * x[1]
 
 
 def ds_inverse(x):
     first = 1.0 / x[0]
     p, e = two_prod(first, x[0])
     rest = ((1.0 - p) - e) - first * x[1]
-    return fast_two_sum(first, first * rest)
+    return first, first * rest
 
 
 def stress(here, below, bulk, mu):
@@ -526,8 +531,9 @@
     for count, distance in ((8, 16), (16, 1)):
         terms = [moments] + [tuple(pltpu.roll(x, distance * i, 1) for x in moments) for i in range(1, count)]
         while len(terms) > 1:
-            terms = [ds_add(a, b) for a, b in zip(terms[::2], terms[1::2])]
+            terms = [loose_add(a, b) for a, b in zip(terms[::2], terms[1::2])]
         moments = terms[0]
+    moments = fast_two_sum(*moments)
     weights = coefficients(moments)
     copies = []
     for i, w in enumerate(weights):

time: 18.8 us -> 18.7 us (level)
  no operation moved by 1% of the time
where the time goes in v9:
time: 18.7 us; the launch traced here: 18.5 us
  Pallas kernels  7.15 us (38%)
  starting transfers between devices  6.27 us (34%)
  waiting for transfers between devices  4.35 us (23%)
  between operations  0.68 us (4%)
    ppermute x3, starting transfers between devices, on_device(): lax.ppermute(packet, 'gy', route)  5.64 us
    ppermute x3, waiting for transfers between devices, on_device(): lax.ppermute(packet, 'gy', route)  3.88 us
    pallas_call x1, Pallas kernels, on_device(): pl.pallas_call(functools.partial(combine, gx=gx), in_specs=[vmem] * (gx +...  1.79 us
    pallas_call x1, Pallas kernels, on_device(): pl.pallas_call(functools.partial(block, gx=gx), in_specs=[vmem] * 8, out_...  1.52 us
    pallas_call x1, Pallas kernels, on_device(): pl.pallas_call(functools.partial(prepare, gx=gx), in_specs=[hbm] * 3, out...  1.27 us
    pallas_call x1, Pallas kernels, on_device(): pl.pallas_call(merge, in_specs=[vmem] * 3, out_specs=vmem, out_shape=pltp...  0.82 us
    pallas_call x1, Pallas kernels, on_device(): pl.pallas_call(functools.partial(interfaces, gx=gx, gy=gy, sources=source...  0.81 us
    pallas_call x1, Pallas kernels, on_device(): pl.pallas_call(early, in_specs=[vmem] * 2, out_specs=[vmem] * 5, input_ou...  0.73 us
  transfers between devices with their start and end apart: 5, of which 4 were waited for; matrix products, arithmetic and copies ran while one was open for 0% of the time, Pallas kernels for 9%

profile of v9, /device:TPU:0, one launch (start us, length us, event | category | flops | bytes accessed | tf_op | source)
XLA Modules:
  0.0 18.5 jit_solution(16875481628515221264)
XLA Ops:
  0.6 1.3 %prepare.1 = (f32[5,2,16,8,512]{4,3,2,1,0:T(8,128)S(1)}, f32[2,2,8,512]{3,2,1,0:T(8,128)S(1)}, f32[3,8,512]{2,1,0:T(8,128)S(1)}) custom-call(f32[2,8]{1,0:T(2,128)} %table.1, f32[1,2,128,512]{3,2,1,0:T(8,128)} %load.1, s32[1,16,64]{2,1,0:T(8,128)} %material.1), custom_call_target="tpu_custom_call" | custom-call | tf_op jit(solution)/shard_map/prepare/pallas_call | solution.py:586
  1.9 0.6 %collective-permute-start = (f32[3,8,512]{2,1,0:T(8,128)S(1)}, f32[3,8,512]{2,1,0:T(8,128)S(1)}, u32[]{:S(2)}, u32[]{:S(2)}) collective-permute-start(f32[3,8,512]{2,1,0:T(8,128)S(1)} %get-tuple-element.24), channel_id=1, source_target_pairs={{0,4},{4,0},{1,5},{5,1},{2,6},{6,2},{3,7},{7,3},{8,12},{12,8},{9,1... | collective-permute-start | bytes 147464 | tf_op jit(solution)/shard_map/ppermute | solution.py:603
  2.5 0.7 %early.1 = (f32[5,2,16,8,512]{4,3,2,1,0:T(8,128)S(1)}, f32[48,128]{1,0:T(8,128)S(1)}, f32[2,18,8,512]{3,2,1,0:T(8,128)S(1)}, f32[2,2,18,8,512]{4,3,2,1,0:T(8,128)S(1)}, f32[8,8,512]{2,1,0:T(8,128)S(1)}) custom-call(f32[5,2,16,8,512]{4,3,2,1,0:T(8,128)S(1)} %get-tuple-element.17.v_in, ...), custom_call_target="tpu_custom_call", output_to_operand_aliasing={{0}: (0, {})} | custom-call | tf_op jit(solution)/shard_map/early/pallas_call | solution.py:611
  3.2 0.1 collective-permute-done.refs_6_.refs_7_
  3.3 1.5 %block.1 = (f32[5,2,16,8,512]{4,3,2,1,0:T(8,128)S(1)}, f32[48,128]{1,0:T(8,128)S(1)}, f32[2,18,8,512]{3,2,1,0:T(8,128)S(1)}, f32[2,2,18,8,512]{4,3,2,1,0:T(8,128)S(1)}, f32[8,8,512]{2,1,0:T(8,128)S(1)}) custom-call(f32[5,2,16,8,512]{4,3,2,1,0:T(8,128)S(1)} %get-tuple-element.19.refs_0_, ...), custom_call_target="tpu_custom_call", output_to_operand_aliasing={{0}: (0, {}), {1}: (1, {}), {2}: (2, {}), {3}: (3, {}), {4}... | custom-call | tf_op jit(solution)/shard_map/block/pallas_call | solution.py:620
  4.9 5.0 %collective-permute-start.3 = (f32[48,128]{1,0:T(8,128)S(1)}, f32[48,128]{1,0:T(8,128)S(1)}, u32[]{:S(2)}, u32[]{:S(2)}) collective-permute-start(f32[48,128]{1,0:T(8,128)S(1)} %get-tuple-element.25.refs_0_), channel_id=1, source_target_pairs={{0,3},{1,2},{2,1},{3,0},{4,7},{5,6},{6,5},{7,4},{8,11},{9,10},{10,... | collective-permute-start | bytes 73736 | tf_op jit(solution)/shard_map/ppermute | solution.py:631
  9.9 0.0 collective-permute-start.2
  9.9 0.6 %collective-permute-start.1 = (f32[48,128]{1,0:T(8,128)S(1)}, f32[48,128]{1,0:T(8,128)S(1)}, u32[]{:S(2)}, u32[]{:S(2)}) collective-permute-start(f32[48,128]{1,0:T(8,128)S(1)} %get-tuple-element.25.refs_0_), channel_id=1, source_target_pairs={{0,1},{1,0},{2,3},{3,2},{4,5},{5,4},{6,7},{7,6},{8,9},{9,8},{10,11... | collective-permute-start | bytes 73736 | tf_op jit(solution)/shard_map/ppermute | solution.py:631
  10.5 0.2 %finish.1.refs_4_ = f32[5,2,16,8,512]{4,3,2,1,0:T(8,128)S(1)} custom-call(f32[5,2,16,8,512]{4,3,2,1,0:T(8,128)S(1)} %get-tuple-element.26.v_in, f32[2,2,18,8,512]{4,3,2,1,0:T(8,128)S(1)} %get-tuple-element.27.push), custom_call_target="tpu_custom_call", output_to_operand_aliasing={{}: (0, {})} | custom-call | tf_op jit(solution)/shard_map/finish/pallas_call | solution.py:632
  10.7 1.0 %collective-permute-done.3.refs_3_ = f32[48,128]{1,0:T(8,128)S(1)} collective-permute-done((f32[48,128]{1,0:T(8,128)S(1)}, f32[48,128]{1,0:T(8,128)S(1)}, u32[]{:S(2)}, u32[]{:S(2)}) %collective-permute-start.3) | collective-permute-done | bytes 24608 | tf_op jit(solution)/shard_map/ppermute | solution.py:631
  11.7 2.9 %collective-permute-done.2.refs_2_ = f32[48,128]{1,0:T(8,128)S(1)} collective-permute-done((f32[48,128]{1,0:T(8,128)S(1)}, f32[48,128]{1,0:T(8,128)S(1)}, u32[]{:S(2)}, u32[]{:S(2)}) %collective-permute-start.2) | collective-permute-done | bytes 24608 | tf_op jit(solution)/shard_map/ppermute | solution.py:631
  14.6 0.0 collective-permute-done.1.refs_1_
  14.6 0.8 %interfaces.1 = (f32[5,2,16,8,128]{4,3,2,1,0:T(8,128)S(1)}, f32[2,8,128]{2,1,0:T(8,128)S(1)}, f32[2,2,18,8,128]{4,3,2,1,0:T(8,128)S(1)}, f32[5,2,16,8,512]{4,3,2,1,0:T(8,128)S(1)}) custom-call(f32[48,128]{1,0:T(8,128)S(1)} %get-tuple-element.25.refs_0_, f32[48,128]{1,0:T(8,128)S(1)} %collective-permute-done.1.refs_1_, ...), custom_call_target="tpu_custom_call", output_to_operand_aliasing={{3}: (4, {})} | custom-call | tf_op jit(solution)/shard_map/interfaces/pallas_call | solution.py:641
  15.4 0.1 collective-permute-start.4
  15.5 0.8 %merge.1.refs_2_ = f32[5,2,16,8,512]{4,3,2,1,0:T(8,128)S(1)} custom-call(f32[5,2,16,8,512]{4,3,2,1,0:T(8,128)S(1)} %get-tuple-element.29.v_in, f32[5,2,16,8,128]{4,3,2,1,0:T(8,128)S(1)} %get-tuple-element.30.strips, f32[2,2,18,8,128]{4,3,2,1,0:T(8,128)S(1)} %get-tuple-element.31.strips_push), custom_call_target="tpu_custom_call", output_to_operand_aliasing={{}: (0, {})} | custom-call | tf_op jit(solution)/shard_map/merge/pallas_call | solution.py:653
  16.3 0.3 %collective-permute-done.4.refs_1_ = f32[2,8,128]{2,1,0:T(8,128)S(1)} collective-permute-done((f32[2,8,128]{2,1,0:T(8,128)S(1)}, f32[2,8,128]{2,1,0:T(8,128)S(1)}, u32[]{:S(2)}, u32[]{:S(2)}) %collective-permute-start.4) | collective-permute-done | bytes 8224 | tf_op jit(solution)/shard_map/ppermute | solution.py:652
  16.7 1.8 %combine.1 = (f32[1,2,128,512]{3,2,1,0:T(8,128)}, f32[1,2,128,512]{3,2,1,0:T(8,128)}) custom-call(f32[2,8,128]{2,1,0:T(8,128)S(1)} %get-tuple-element.28.refs_0_, f32[2,8,128]{2,1,0:T(8,128)S(1)} %collective-permute-done.4.refs_1_, f32[5,2,16,8,512]{4,3,2,1,0:T(8,128)S(1)} %merge.1.refs_2_), custom_call_target="tpu_custom_call" | custom-call | tf_op jit(solution)/shard_map/combine/pallas_call | solution.py:663
Async XLA Ops:
  1.9 1.4 %collective-permute-start = (f32[3,8,512]{2,1,0:T(8,128)S(1)}, f32[3,8,512]{2,1,0:T(8,128)S(1)}, u32[]{:S(2)}, u32[]{:S(2)}) collective-permute-start(f32[3,8,512]{2,1,0:T(8,128)S(1)} %get-tuple-element.24), channel_id=1, source_target_pairs={{0,4},{4,0},{1,5},{5,1},{2,6},{6,2},{3,7},{7,3},{8,12},{12,8},{9,1... | collective-permute-start | bytes 147464 | tf_op jit(solution)/shard_map/ppermute | solution.py:603
  4.9 6.8 %collective-permute-start.3 = (f32[48,128]{1,0:T(8,128)S(1)}, f32[48,128]{1,0:T(8,128)S(1)}, u32[]{:S(2)}, u32[]{:S(2)}) collective-permute-start(f32[48,128]{1,0:T(8,128)S(1)} %get-tuple-element.25.refs_0_), channel_id=1, source_target_pairs={{0,3},{1,2},{2,1},{3,0},{4,7},{5,6},{6,5},{7,4},{8,11},{9,10},{10,... | collective-permute-start | bytes 73736 | tf_op jit(solution)/shard_map/ppermute | solution.py:631
  9.9 4.7 %collective-permute-start.2 = (f32[48,128]{1,0:T(8,128)S(1)}, f32[48,128]{1,0:T(8,128)S(1)}, u32[]{:S(2)}, u32[]{:S(2)}) collective-permute-start(f32[48,128]{1,0:T(8,128)S(1)} %get-tuple-element.25.refs_0_), channel_id=1, source_target_pairs={{0,2},{1,3},{2,0},{3,1},{4,6},{5,7},{6,4},{7,5},{8,10},{9,11},{10,... | collective-permute-start | bytes 73736 | tf_op jit(solution)/shard_map/ppermute | solution.py:631
  9.9 4.7 %collective-permute-start.1 = (f32[48,128]{1,0:T(8,128)S(1)}, f32[48,128]{1,0:T(8,128)S(1)}, u32[]{:S(2)}, u32[]{:S(2)}) collective-permute-start(f32[48,128]{1,0:T(8,128)S(1)} %get-tuple-element.25.refs_0_), channel_id=1, source_target_pairs={{0,1},{1,0},{2,3},{3,2},{4,5},{5,4},{6,7},{7,6},{8,9},{9,8},{10,11... | collective-permute-start | bytes 73736 | tf_op jit(solution)/shard_map/ppermute | solution.py:631
  15.4 1.2 %collective-permute-start.4 = (f32[2,8,128]{2,1,0:T(8,128)S(1)}, f32[2,8,128]{2,1,0:T(8,128)S(1)}, u32[]{:S(2)}, u32[]{:S(2)}) collective-permute-start(f32[2,8,128]{2,1,0:T(8,128)S(1)} %get-tuple-element.28.refs_0_), channel_id=1, source_target_pairs={{0,4},{4,0},{1,5},{5,1},{2,6},{6,2},{3,7},{7,3},{8,12},{12,8},{9,1... | collective-permute-start | bytes 24584 | tf_op jit(solution)/shard_map/ppermute | solution.py:652
